TPU v7x, 1024 devices: a whole 8x8x8 slice. The times are simulated.
1024 devices in a mesh: lat: 16 (over x, core), lon: 64 (over z, y).
Axes of the slice: x: 8, y: 8, z: 8, core: 2. Of those that a mesh axis runs over, the one named last changes fastest.
Arguments:
- eastward_velocity: float32 [384, 1024, 128], P('lat', 'lon'), may hold values from -6 to 6
- northward_velocity: float32 [384, 1024, 128], P('lat', 'lon'), may hold values from -6 to 6
- thermal_anomaly: float32 [384, 1024, 128], P('lat', 'lon'), may hold values from -6 to 6
- water_content: float32 [384, 1024, 128], P('lat', 'lon'), may hold values from 0 to 1
- gridbox_factor: float32 [384, 1024], replicated, may hold values from 0.5 to 2
- filter_threshold: float32 [384], replicated, may hold values from 0.03 to 1
- layers_to_eigen: float32 [128, 128], replicated, may hold values from -0.5 to 0.5
- eigen_to_layers: float32 [128, 128], replicated, may hold values from -0.5 to 0.5
- eigen_screening_factor: float32 [128], replicated, may hold values from 0.3 to 30
- chebyshev_sweeps: int32 [128], replicated, may hold values from 3 to 6, as said below
- eigen_region_holder: int32 [128], replicated, may hold values from 0 to 63, as said below
Outputs:
- wind_u_new: float32 [384, 1024, 128], P('lat', 'lon')
- wind_v_new: float32 [384, 1024, 128], P('lat', 'lon')
- mode_solution: float32 [384, 384, 1024], P('lon', 'lat')
Inputs may be any that keep to these rules, and one draw needn't show every extreme that they name: `chebyshev_sweeps`: some mode takes exactly 6 iterations and some exactly 3. `eigen_region_holder`: no longitude patch owns more than 6 modes, and some patch owns exactly 6.
All inputs are finite; a program needn't handle non-finite values.
Results may differ from a plain program's by a relative error of at most 0.0003.
Values sent between devices are 32-bit elements; how exact they have to be, the bound alone decides.
No kernel may reach another device: no remote copies, remote signals or barrier semaphores. Data moves between devices by JAX's collectives and lax.ppermute only.
A program may use at most 64 MiB of HBM per device.

v0:
```python
import math

import jax
import jax.numpy as jnp
from jax import lax
from jax.sharding import PartitionSpec as P

MAXIT = 6


highest = lax.Precision.HIGHEST
viscous_factor = 0.125
elastic_factor = 0.5
step_coef = 0.5
moisture_factor = 0.61


def padded_2(shard, sides, width, wrap):
    for axis, dim in sides:
        size, length = (lax.axis_size(axis), shard.shape[dim])
        up = [(i, (i + 1) % size) for i in range(size if wrap else size - 1)]
        down = [(j, i) for i, j in up]
        last = lax.slice_in_dim(shard, length - width, length, axis=dim)
        leading = lax.slice_in_dim(shard, 0, width, axis=dim)
        before = lax.ppermute(last, axis, up)
        after = lax.ppermute(leading, axis, down)
        shard = jnp.concatenate([before, shard, after], axis=dim)
    return shard


def pole_keep(lat_rows, lat_pos, lat_count):
    row_index = lax.iota(jnp.int32, lat_rows + 2)
    south = jnp.logical_and(row_index == 0, lat_pos == 0)
    north = jnp.logical_and(row_index == lat_rows + 1, lat_pos == lat_count - 1)
    return jnp.where(jnp.logical_or(south, north), 0.0, 1.0).astype(jnp.float32)


def band_rim(values):
    return padded_2(values, (("lat", 1),), 1, False)


def apply_helm(values, metric_rows, item_depth, rim):
    padded = rim(values)
    adjacent_regions = (
        padded[:, 2:] + padded[:, :-2] + jnp.roll(values, -1, axis=2) + jnp.roll(values, 1, axis=2)
    )
    return values - item_depth * metric_rows * (adjacent_regions - 4.0 * values)


def chebyshev(source, metric_rows, item_depth, item_iters, rim):
    safe_depth = jnp.where(item_depth > 0.0, item_depth, 1.0)
    centre = 1.0 + 8.0 * safe_depth
    radius = 8.0 * safe_depth
    relative = centre / radius
    ratio_now = 1.0 / relative
    direction = source / centre
    residual = source
    solution = jnp.zeros_like(source)
    for sweep in range(MAXIT):
        active = jnp.where(item_iters > sweep, 1.0, 0.0)
        solution = solution + active * direction
        if sweep + 1 < MAXIT:
            residual = residual - apply_helm(direction, metric_rows, item_depth, rim)
            ratio_next = 1.0 / (2.0 * relative - ratio_now)
            direction = ratio_next * ratio_now * direction + 2.0 * ratio_next / radius * residual
            ratio_now = ratio_next
    return solution


def damp_factor(cutoff_rows, lon_total, folded):
    scale = cutoff_rows[:, None] * (0.5 * lon_total)
    ratio = folded[None, :] / scale
    ratio = ratio * ratio
    return 1.0 / (1.0 + ratio * ratio)


def fourier_table(lon_total):
    half_lon = lon_total // 2
    position = lax.iota(jnp.int32, lon_total)
    wavenumber = lax.iota(jnp.int32, half_lon)
    angles = (position[:, None] * wavenumber[None, :] % lon_total).astype(jnp.float32) * (
        2.0 * math.pi / lon_total
    )
    return jnp.concatenate([jnp.cos(angles), jnp.sin(angles)], axis=1)


def polar_filter(grid_field, cutoff_rows, fourier):
    lon_total = grid_field.shape[2]
    half_lon = lon_total // 2
    folded = lax.iota(jnp.float32, half_lon)
    damping = damp_factor(cutoff_rows, lon_total, folded) * jnp.where(folded > 0.0, 2.0, 1.0)
    weights = jnp.concatenate([damping, damping], axis=1)
    nyquist_damp = damp_factor(cutoff_rows, lon_total, jnp.zeros((1,), jnp.float32) + half_lon)
    parity = 1.0 - 2.0 * (lax.iota(jnp.int32, lon_total) % 2).astype(jnp.float32)
    spectrum = jnp.einsum("irn,nk->irk", grid_field, fourier, precision=highest)
    nyquist = jnp.einsum("irn,n->ir", grid_field, parity, precision=highest)
    rebuilt = jnp.einsum("irk,nk->irn", spectrum * weights[None], fourier, precision=highest)
    return (rebuilt + nyquist_damp[None, :, :] * nyquist[:, :, None] * parity) / lon_total


def to_patches(band_values, lon_count):
    item_count, lat_rows, lon_total = band_values.shape
    lon_cols = lon_total // lon_count
    split_band = band_values.reshape(item_count, lat_rows, lon_count, lon_cols).transpose(
        2, 0, 1, 3
    )
    return split_band.reshape(lon_count, item_count, lat_rows * lon_cols)


def local(
    eastward_velocity,
    northward_velocity,
    thermal_anomaly,
    water_content,
    gridbox_factor,
    filter_threshold,
    layers_to_eigen,
    eigen_to_layers,
    eigen_screening_factor,
    chebyshev_sweeps,
    eigen_region_holder,
):
    lat_rows, lon_cols, level_count = eastward_velocity.shape
    cell_count = lat_rows * lon_cols
    lat_count = lax.axis_size("lat")
    lon_count = lax.axis_size("lon")
    lat_pos = lax.axis_index("lat")
    lon_pos = lax.axis_index("lon")
    full_lon = gridbox_factor.shape[1]
    slot_room = 3 * level_count // lon_count
    band_start = lat_pos * lat_rows
    band_metric = lax.dynamic_slice_in_dim(gridbox_factor, band_start, lat_rows, 0)
    band_cutoff = lax.dynamic_slice_in_dim(filter_threshold, band_start, lat_rows, 0)
    region_scaling = lax.dynamic_slice_in_dim(band_metric, lon_pos * lon_cols, lon_cols, 1)[
        :, :, None
    ]
    keep_rows = pole_keep(lat_rows, lat_pos, lat_count)[:, None, None]
    moist_thermal_field = thermal_anomaly * (1.0 + moisture_factor * water_content)
    piled_fields = jnp.stack([eastward_velocity, northward_velocity, moist_thermal_field])
    padded = padded_2(piled_fields, (("lat", 1), ("lon", 2)), 1, True) * keep_rows[None]
    zonal_pad = padded[0]
    merid_pad = padded[1]
    virtual_pad = padded[2]
    outflow_field = (
        region_scaling
        * (
            zonal_pad[1:-1, 2:]
            - zonal_pad[1:-1, :-2]
            + (merid_pad[2:, 1:-1] - merid_pad[:-2, 1:-1])
        )
        * 0.5
    )
    adjacent_regions = (
        virtual_pad[2:, 1:-1]
        + virtual_pad[:-2, 1:-1]
        + virtual_pad[1:-1, 2:]
        + virtual_pad[1:-1, :-2]
    )
    source_term = (
        moist_thermal_field
        + viscous_factor * region_scaling * (adjacent_regions - 4.0 * moist_thermal_field)
        - elastic_factor * outflow_field
    )
    mode_rhs = lax.dot_general(
        source_term.reshape(cell_count, level_count),
        layers_to_eigen,
        (((1,), (1,)), ((), ())),
        precision=highest,
    )
    mode_index = lax.iota(jnp.int32, level_count)
    earlier = jnp.logical_and(
        eigen_region_holder[:, None] == eigen_region_holder[None, :],
        mode_index[:, None] > mode_index[None, :],
    )
    slot_rank = jnp.sum(earlier.astype(jnp.int32), axis=1)
    patch_index = lax.iota(jnp.int32, lon_count)
    slot_index = lax.iota(jnp.int32, slot_room)
    select = jnp.logical_and(
        eigen_region_holder[None, None, :] == patch_index[:, None, None],
        slot_rank[None, None, :] == slot_index[None, :, None],
    ).astype(jnp.float32)
    packed = jnp.einsum("psm,cm->psc", select, mode_rhs, precision=highest)
    slot_depth = jnp.einsum("psm,m->ps", select, eigen_screening_factor, precision=highest)
    slot_iters = jnp.einsum(
        "psm,m->ps", select, chebyshev_sweeps.astype(jnp.float32), precision=highest
    )
    slot_params = jnp.stack([slot_depth, slot_iters], axis=2)
    fourier = fourier_table(full_lon)
    mode_data = lax.all_to_all(packed, "lon", split_axis=0, concat_axis=0, tiled=True)
    item_params = lax.all_to_all(slot_params, "lon", split_axis=0, concat_axis=0, tiled=True)
    item_count = mode_data.shape[1]
    band_rhs = (
        mode_data.reshape(lon_count, item_count, lat_rows, lon_cols)
        .transpose(1, 2, 0, 3)
        .reshape(item_count, lat_rows, full_lon)
    )
    item_depth = item_params[0, :, 0][:, None, None]
    item_iters = item_params[0, :, 1][:, None, None]
    solved = chebyshev(band_rhs, band_metric, item_depth, item_iters, band_rim)
    filtered = polar_filter(solved, band_cutoff, fourier)
    back_solved = lax.all_to_all(
        to_patches(filtered, lon_count), "lon", split_axis=0, concat_axis=0, tiled=True
    )
    results = (back_solved, filtered[None])
    mode_solution = results[-1][0]
    solved_modes = jnp.einsum("psm,psc->cm", select, results[0], precision=highest)
    pressure = lax.dot_general(
        solved_modes, eigen_to_layers, (((1,), (1,)), ((), ())), precision=highest
    ).reshape(lat_rows, lon_cols, level_count)
    framed_pressure = padded_2(pressure, (("lat", 0), ("lon", 1)), 1, True) * keep_rows
    step_lon = region_scaling * (framed_pressure[1:-1, 2:] - framed_pressure[1:-1, :-2]) * 0.5
    step_lat = region_scaling * (framed_pressure[2:, 1:-1] - framed_pressure[:-2, 1:-1]) * 0.5
    return (
        eastward_velocity - step_coef * step_lon,
        northward_velocity - step_coef * step_lat,
        mode_solution,
    )


def solution(mesh):
    return jax.shard_map(
        local,
        mesh=mesh,
        in_specs=(
            P("lat", "lon", None),
            P("lat", "lon", None),
            P("lat", "lon", None),
            P("lat", "lon", None),
            P(),
            P(),
            P(),
            P(),
            P(),
            P(),
            P(),
        ),
        out_specs=(P("lat", "lon", None), P("lat", "lon", None), P("lon", "lat", None)),
        check_vma=False,
    )
```

profile of v0, /device:TPU:6, one launch (start us, length us, event | category | flops | bytes accessed | tf_op | source)
XLA Modules:
  0.0 198.4 jit_solution(15477913555957250873)
XLA Ops:
  0.7 1.1 fusion.75
  2.5 1.7 collective-permute-start.1
  5.0 0.9 convert_reduce_fusion
  5.9 1.0 convolution_bitcast_fusion.2
  6.9 1.0 convolution_bitcast_fusion.3
  8.7 23.4 %all-to-all-start = ((f32[64,6,2]{1,2,0:T(2,128)}), f32[64,6,2]{1,2,0:T(2,128)S(1)}, u32[]{:S(2)}, u32[]{:S(2)}) async-start(f32[64,6,2]{1,2,0:T(2,128)} %copy.43), calls=%async_computation | async-start | bytes 131072 | tf_op jit(solution)/shard_map/all_to_all | solution.py:190
  32.2 0.9 constant_dynamic-slice_fusion
  33.1 1.3 fusion.85
  34.4 0.8 broadcast_multiply_fusion
  35.4 3.6 %collective-permute-start.2 = (f32[3,26,1,128]{3,2,1,0:T(1,128)S(1)}, f32[3,26,1,128]{3,2,1,0:T(1,128)S(1)}, u32[]{:S(2)}, u32[]{:S(2)}) collective-permute-start(f32[3,26,1,128]{3,2,1,0:T(1,128)S(1)} %get-tuple-element.25), channel_id=1, source_target_pairs={{0,1},{1,2},{2,3},{3,4},{4,5},{5,6},{6,7},{7,8},{8,9},{9,10},{10,1... | collective-permute-start | bytes 119816 | tf_op jit(solution)/shard_map/ppermute | solution.py:25
  39.0 5.7 %collective-permute-start.3 = (f32[3,26,1,128]{3,2,1,0:T(1,128)S(1)}, f32[3,26,1,128]{3,2,1,0:T(1,128)S(1)}, u32[]{:S(2)}, u32[]{:S(2)}) collective-permute-start(f32[3,26,1,128]{3,2,1,0:T(1,128)S(1)} %get-tuple-element.26), channel_id=1, source_target_pairs={{1,0},{2,1},{3,2},{4,3},{5,4},{6,5},{7,6},{8,7},{9,8},{10,9},{11,1... | collective-permute-start | bytes 119816 | tf_op jit(solution)/shard_map/ppermute | solution.py:26
  45.0 1.3 collective-permute-done.3
  47.7 1.2 copy.44
  48.9 11.7 %all-to-all-start.1 = ((f32[64,6,384]{2,1,0:T(8,128)}), f32[64,6,384]{2,1,0:T(8,128)}, u32[]{:S(2)}, u32[]{:S(2)}) async-start(f32[64,6,384]{2,1,0:T(8,128)} %copy.44), calls=%async_computation.1 | async-start | bytes 1572864 | tf_op jit(solution)/shard_map/all_to_all | solution.py:189
  60.6 9.0 %fusion.11 = (f32[1024,512]{1,0:T(8,128)S(1)}, f32[1024,512]{1,0:T(8,128)}) fusion(), kind=kLoop, calls=%fused_computation.24 | loop fusion | flops 7340032 | bytes 4194304 | tf_op jit(solution)/shard_map/sin | solution.py:84
  71.4 12.8 %all-to-all-done.1 = f32[64,6,384]{2,1,0:T(8,128)} async-done(((f32[64,6,384]{2,1,0:T(8,128)}), f32[64,6,384]{2,1,0:T(8,128)}, u32[]{:S(2)}, u32[]{:S(2)}) %all-to-all-start.1) | async-done | bytes 589856 | tf_op jit(solution)/shard_map/all_to_all | solution.py:189
  84.3 1.5 copy.45
  85.8 3.0 %copy.46 = f32[6,24,64,16]{3,2,1,0:T(8,128)} copy(f32[6,24,64,16]{2,3,1,0:T(8,128)S(1)} %bitcast.79) | data formatting | bytes 1179648 | tf_op jit(solution)/shard_map/transpose | solution.py:194
  88.8 5.0 %reshape.351 = f32[6,24,1024]{2,1,0:T(8,128)S(1)} reshape(f32[6,24,64,16]{3,2,1,0:T(8,128)} %copy.46) | data formatting | bytes 1179648 | tf_op jit(solution)/shard_map/reshape | solution.py:195
  94.2 1.9 collective-permute-start.4
  96.1 2.4 %collective-permute-start.5 = (f32[6,1,1024]{2,1,0:T(1,128)S(1)}, f32[6,1,1024]{2,1,0:T(1,128)S(1)}, u32[]{:S(2)}, u32[]{:S(2)}) collective-permute-start(f32[6,1,1024]{2,1,0:T(1,128)S(1)} %get-tuple-element.52), channel_id=1, source_target_pairs={{0,64},{64,128},{128,192},{192,256},{256,320},{320,384},{384,448},... | collective-permute-start | bytes 73736 | tf_op jit(solution)/shard_map/ppermute | solution.py:25
  98.6 2.6 %collective-permute-done.5 = f32[6,1,1024]{2,1,0:T(1,128)S(1)} collective-permute-done((f32[6,1,1024]{2,1,0:T(1,128)S(1)}, f32[6,1,1024]{2,1,0:T(1,128)S(1)}, u32[]{:S(2)}, u32[]{:S(2)}) %collective-permute-start.5) | collective-permute-done | bytes 24608 | tf_op jit(solution)/shard_map/ppermute | solution.py:25
  102.1 1.9 collective-permute-start.6
  104.0 2.4 %collective-permute-start.7 = (f32[6,1,1024]{2,1,0:T(1,128)S(1)}, f32[6,1,1024]{2,1,0:T(1,128)S(1)}, u32[]{:S(2)}, u32[]{:S(2)}) collective-permute-start(f32[6,1,1024]{2,1,0:T(1,128)S(1)} %get-tuple-element.46), channel_id=1, source_target_pairs={{0,64},{64,128},{128,192},{192,256},{256,320},{320,384},{384,448},... | collective-permute-start | bytes 73736 | tf_op jit(solution)/shard_map/ppermute | solution.py:25
  106.5 2.6 %collective-permute-done.7 = f32[6,1,1024]{2,1,0:T(1,128)S(1)} collective-permute-done((f32[6,1,1024]{2,1,0:T(1,128)S(1)}, f32[6,1,1024]{2,1,0:T(1,128)S(1)}, u32[]{:S(2)}, u32[]{:S(2)}) %collective-permute-start.7) | collective-permute-done | bytes 24608 | tf_op jit(solution)/shard_map/ppermute | solution.py:25
  109.9 1.9 collective-permute-start.8
  111.8 2.4 %collective-permute-start.9 = (f32[6,1,1024]{2,1,0:T(1,128)S(1)}, f32[6,1,1024]{2,1,0:T(1,128)S(1)}, u32[]{:S(2)}, u32[]{:S(2)}) collective-permute-start(f32[6,1,1024]{2,1,0:T(1,128)S(1)} %get-tuple-element.40), channel_id=1, source_target_pairs={{0,64},{64,128},{128,192},{192,256},{256,320},{320,384},{384,448},... | collective-permute-start | bytes 73736 | tf_op jit(solution)/shard_map/ppermute | solution.py:25
  114.3 2.6 %collective-permute-done.9 = f32[6,1,1024]{2,1,0:T(1,128)S(1)} collective-permute-done((f32[6,1,1024]{2,1,0:T(1,128)S(1)}, f32[6,1,1024]{2,1,0:T(1,128)S(1)}, u32[]{:S(2)}, u32[]{:S(2)}) %collective-permute-start.9) | collective-permute-done | bytes 24608 | tf_op jit(solution)/shard_map/ppermute | solution.py:25
  117.8 1.9 collective-permute-start.10
  119.7 3.1 %collective-permute-start.11 = (f32[6,1,1024]{2,1,0:T(1,128)S(1)}, f32[6,1,1024]{2,1,0:T(1,128)S(1)}, u32[]{:S(2)}, u32[]{:S(2)}) collective-permute-start(f32[6,1,1024]{2,1,0:T(1,128)S(1)} %get-tuple-element.34), channel_id=1, source_target_pairs={{0,64},{64,128},{128,192},{192,256},{256,320},{320,384},{384,448},... | collective-permute-start | bytes 73736 | tf_op jit(solution)/shard_map/ppermute | solution.py:25
  122.9 1.9 collective-permute-done.11
  125.7 1.9 collective-permute-start.12
  127.6 4.2 %collective-permute-start.13 = (f32[6,1,1024]{2,1,0:T(1,128)S(1)}, f32[6,1,1024]{2,1,0:T(1,128)S(1)}, u32[]{:S(2)}, u32[]{:S(2)}) collective-permute-start(f32[6,1,1024]{2,1,0:T(1,128)S(1)} %get-tuple-element.32), channel_id=1, source_target_pairs={{0,64},{64,128},{128,192},{192,256},{256,320},{320,384},{384,448},... | collective-permute-start | bytes 73736 | tf_op jit(solution)/shard_map/ppermute | solution.py:25
  131.9 0.9 collective-permute-done.13
  132.8 1.2 fusion.26
  134.1 1.5 fusion.118
  135.7 2.6 %fusion.8 = f32[6,24,1024]{2,1,0:T(8,128)S(1)} fusion(f32[6,24,1024]{2,1,0:T(8,128)S(1)} %fusion.26, f32[1024,512]{1,0:T(8,128)S(1)} %get-tuple-element.82, f32[1024,512]{1,0:T(8,128)S(1)} %copy-done.1, f32[24,1024]{1,0:T(8,128)S(1)} %pad_maximum_fusion.10), kind=kOutput, calls=%fused_computation.17 | convolution fusion | flops 1813135360 | bytes 5472256 | tf_op jit(solution)/shard_map/irn,nk->irk/dot_general | solution.py:95
  138.2 4.6 %fusion.10 = f32[6,24,1024]{2,1,0:T(8,128)S(1)} fusion(f32[6,24,1024]{2,1,0:T(8,128)S(1)} %fusion.8, f32[1024,512]{1,0:T(8,128)S(1)} %get-tuple-element.82, f32[1024,512]{1,0:T(8,128)S(1)} %copy-done.1, f32[1024]{0:T(1024)S(1)} %fusion.78, f32[6,24]{1,0:T(8,128)S(1)} %bitcast_multiply_fusion), kind=kOutput, calls=%fused_computation.19 | convolution fusion | flops 1813430272 | bytes 5378624 | tf_op jit(solution)/shard_map/irk,nk->irn/dot_general | solution.py:97
  142.8 3.1 %reshape.352 = f32[6,24,64,16]{3,2,1,0:T(8,128)} reshape(f32[6,24,1024]{2,1,0:T(8,128)S(1)} %fusion.10) | data formatting | bytes 1179648 | tf_op jit(solution)/shard_map/reshape | solution.py:104
  145.9 3.0 %copy.47 = f32[64,6,24,16]{0,3,2,1:T(8,128)S(1)} copy(f32[64,6,24,16]{3,0,2,1:T(8,128)} %bitcast.78) | data formatting | bytes 1179648 | tf_op jit(solution)/shard_map/transpose | solution.py:104
  149.5 28.4 %all_to_all.15 = f32[64,6,384]{2,1,0:T(8,128)S(1)} all-to-all(f32[64,6,384]{2,1,0:T(8,128)S(1)} %copy.48), channel_id=1, replica_groups=mesh['lat'=16,'lon'=64] {'lon'}, dimensions={0} | all-to-all | bytes 1179648 | tf_op jit(solution)/shard_map/all_to_all | solution.py:201
  178.9 3.8 %collective-permute-start.14 = (f32[1,16,128]{2,1,0:T(8,128)S(1)}, f32[1,16,128]{2,1,0:T(8,128)S(1)}, u32[]{:S(2)}, u32[]{:S(2)}) collective-permute-start(f32[1,16,128]{2,1,0:T(8,128)S(1)} %get-tuple-element.63), channel_id=1, source_target_pairs={{0,64},{64,128},{128,192},{192,256},{256,320},{320,384},{384,448},... | collective-permute-start | bytes 24584 | tf_op jit(solution)/shard_map/ppermute | solution.py:25
  182.7 0.8 collective-permute-done.14
  183.6 3.3 %collective-permute-done.15 = f32[1,16,128]{2,1,0:T(8,128)S(1)} collective-permute-done((f32[1,16,128]{2,1,0:T(8,128)S(1)}, f32[1,16,128]{2,1,0:T(8,128)S(1)}, u32[]{:S(2)}, u32[]{:S(2)}) %collective-permute-start.15) | collective-permute-done | bytes 8224 | tf_op jit(solution)/shard_map/ppermute | solution.py:26
  186.9 3.4 %collective-permute-start.16 = (f32[26,1,128]{2,1,0:T(1,128)S(1)}, f32[26,1,128]{2,1,0:T(1,128)S(1)}, u32[]{:S(2)}, u32[]{:S(2)}) collective-permute-start(f32[26,1,128]{2,1,0:T(1,128)S(1)} %get-tuple-element.61), channel_id=1, source_target_pairs={{0,1},{1,2},{2,3},{3,4},{4,5},{5,6},{6,7},{7,8},{8,9},{9,10},{10,1... | collective-permute-start | bytes 39944 | tf_op jit(solution)/shard_map/ppermute | solution.py:25
  190.3 5.7 %collective-permute-start.17 = (f32[26,1,128]{2,1,0:T(1,128)S(1)}, f32[26,1,128]{2,1,0:T(1,128)S(1)}, u32[]{:S(2)}, u32[]{:S(2)}) collective-permute-start(f32[26,1,128]{2,1,0:T(1,128)S(1)} %get-tuple-element.62), channel_id=1, source_target_pairs={{1,0},{2,1},{3,2},{4,3},{5,4},{6,5},{7,6},{8,7},{9,8},{10,9},{11,1... | collective-permute-start | bytes 39944 | tf_op jit(solution)/shard_map/ppermute | solution.py:26
  196.1 1.4 collective-permute-done.17
  197.6 0.9 fusion.55
  (129 shorter events, 11.3 us)
Async XLA Ops:
  0.6 46.2 %copy-start = (f32[128,128]{1,0:T(8,128)S(1)}, f32[128,128]{1,0:T(8,128)}, u32[]{:S(2)}) copy-start(f32[128,128]{1,0:T(8,128)} %param.17) | copy-start | bytes 196612
  0.6 34.7 %copy-start.4 = (f32[24,16,128]{2,1,0:T(8,128)S(1)}, f32[24,16,128]{2,1,0:T(8,128)}, u32[]{:S(2)}) copy-start(f32[24,16,128]{2,1,0:T(8,128)} %param.11) | copy-start | bytes 589828
  0.7 34.7 %copy-start.2 = (f32[24,16,128]{2,1,0:T(8,128)S(1)}, f32[24,16,128]{2,1,0:T(8,128)}, u32[]{:S(2)}) copy-start(f32[24,16,128]{2,1,0:T(8,128)} %param.12) | copy-start | bytes 589828
  2.5 32.8 %collective-permute-start = (f32[3,1,16,128]{3,2,1,0:T(8,128)S(1)}, f32[3,1,16,128]{3,2,1,0:T(8,128)S(1)}, u32[]{:S(2)}, u32[]{:S(2)}) collective-permute-start(f32[3,1,16,128]{3,2,1,0:T(8,128)S(1)} %get-tuple-element.57), channel_id=1, source_target_pairs={{0,64},{64,128},{128,192},{192,256},{256,320},{320,384},{384,448},... | collective-permute-start | bytes 73736 | tf_op jit(solution)/shard_map/ppermute | solution.py:25
  2.5 32.8 %collective-permute-start.1 = (f32[3,1,16,128]{3,2,1,0:T(8,128)S(1)}, f32[3,1,16,128]{3,2,1,0:T(8,128)S(1)}, u32[]{:S(2)}, u32[]{:S(2)}) collective-permute-start(f32[3,1,16,128]{3,2,1,0:T(8,128)S(1)} %get-tuple-element.58), channel_id=1, source_target_pairs={{64,0},{128,64},{192,128},{256,192},{320,256},{384,320},{448,384},... | collective-permute-start | bytes 73736 | tf_op jit(solution)/shard_map/ppermute | solution.py:26
  5.0 42.3 %copy-start.9 = (pred[64,128]{1,0:T(8,128)(4,1)}, pred[64,128]{1,0:T(8,128)(4,1)S(1)}, u32[]{:S(2)}) copy-start(pred[64,128]{1,0:T(8,128)(4,1)S(1)} %iota_compare_fusion.1) | copy-start | bytes 24580
  5.9 41.4 %copy-start.14 = (pred[6,128]{1,0:T(8,128)(4,1)}, pred[6,128]{1,0:T(8,128)(4,1)S(1)}, u32[]{:S(2)}) copy-start(pred[6,128]{1,0:T(8,128)(4,1)S(1)} %iota_compare_fusion.2) | copy-start | bytes 2308
  8.7 40.2 %all-to-all-start = ((f32[64,6,2]{1,2,0:T(2,128)}), f32[64,6,2]{1,2,0:T(2,128)S(1)}, u32[]{:S(2)}, u32[]{:S(2)}) async-start(f32[64,6,2]{1,2,0:T(2,128)} %copy.43), calls=%async_computation | async-start | bytes 131072 | tf_op jit(solution)/shard_map/all_to_all | solution.py:190
  35.3 11.3 %copy-start.7 = (f32[24,16,128]{2,1,0:T(8,128)S(1)}, f32[24,16,128]{2,1,0:T(8,128)}, u32[]{:S(2)}) copy-start(f32[24,16,128]{2,1,0:T(8,128)} %param.13) | copy-start | bytes 589828
  35.3 11.3 %copy-start.8 = (f32[24,16,128]{2,1,0:T(8,128)S(1)}, f32[24,16,128]{2,1,0:T(8,128)}, u32[]{:S(2)}) copy-start(f32[24,16,128]{2,1,0:T(8,128)} %param.14) | copy-start | bytes 589828
  35.4 9.6 %collective-permute-start.2 = (f32[3,26,1,128]{3,2,1,0:T(1,128)S(1)}, f32[3,26,1,128]{3,2,1,0:T(1,128)S(1)}, u32[]{:S(2)}, u32[]{:S(2)}) collective-permute-start(f32[3,26,1,128]{3,2,1,0:T(1,128)S(1)} %get-tuple-element.25), channel_id=1, source_target_pairs={{0,1},{1,2},{2,3},{3,4},{4,5},{5,6},{6,7},{7,8},{8,9},{9,10},{10,1... | collective-permute-start | bytes 119816 | tf_op jit(solution)/shard_map/ppermute | solution.py:25
  39.0 7.3 %collective-permute-start.3 = (f32[3,26,1,128]{3,2,1,0:T(1,128)S(1)}, f32[3,26,1,128]{3,2,1,0:T(1,128)S(1)}, u32[]{:S(2)}, u32[]{:S(2)}) collective-permute-start(f32[3,26,1,128]{3,2,1,0:T(1,128)S(1)} %get-tuple-element.26), channel_id=1, source_target_pairs={{1,0},{2,1},{3,2},{4,3},{5,4},{6,5},{7,6},{8,7},{9,8},{10,9},{11,1... | collective-permute-start | bytes 119816 | tf_op jit(solution)/shard_map/ppermute | solution.py:26
  48.9 35.4 %all-to-all-start.1 = ((f32[64,6,384]{2,1,0:T(8,128)}), f32[64,6,384]{2,1,0:T(8,128)}, u32[]{:S(2)}, u32[]{:S(2)}) async-start(f32[64,6,384]{2,1,0:T(8,128)} %copy.44), calls=%async_computation.1 | async-start | bytes 1572864 | tf_op jit(solution)/shard_map/all_to_all | solution.py:189
  93.7 7.5 %copy-start.12 = (f32[6]{0:T(128)S(1)}, f32[6]{0:T(128)}, u32[]{:S(2)}) copy-start(f32[6]{0:T(128)} %get-tuple-element.71) | copy-start | bytes 76
  93.8 7.5 %copy-start.32 = (f32[6]{0:T(128)S(1)}, f32[6]{0:T(128)}, u32[]{:S(2)}) copy-start(f32[6]{0:T(128)} %get-tuple-element.79) | copy-start | bytes 76
  93.8 7.5 %copy-start.33 = (f32[6]{0:T(128)S(1)}, f32[6]{0:T(128)}, u32[]{:S(2)}) copy-start(f32[6]{0:T(128)} %get-tuple-element.80) | copy-start | bytes 76
  94.2 4.4 %collective-permute-start.4 = (f32[6,1,1024]{2,1,0:T(1,128)S(1)}, f32[6,1,1024]{2,1,0:T(1,128)S(1)}, u32[]{:S(2)}, u32[]{:S(2)}) collective-permute-start(f32[6,1,1024]{2,1,0:T(1,128)S(1)} %get-tuple-element.51), channel_id=1, source_target_pairs={{64,0},{128,64},{192,128},{256,192},{320,256},{384,320},{448,384},... | collective-permute-start | bytes 73736 | tf_op jit(solution)/shard_map/ppermute | solution.py:26
  96.1 5.1 %collective-permute-start.5 = (f32[6,1,1024]{2,1,0:T(1,128)S(1)}, f32[6,1,1024]{2,1,0:T(1,128)S(1)}, u32[]{:S(2)}, u32[]{:S(2)}) collective-permute-start(f32[6,1,1024]{2,1,0:T(1,128)S(1)} %get-tuple-element.52), channel_id=1, source_target_pairs={{0,64},{64,128},{128,192},{192,256},{256,320},{320,384},{384,448},... | collective-permute-start | bytes 73736 | tf_op jit(solution)/shard_map/ppermute | solution.py:25
  101.8 7.4 %copy-start.30 = (f32[6]{0:T(128)S(1)}, f32[6]{0:T(128)}, u32[]{:S(2)}) copy-start(f32[6]{0:T(128)} %get-tuple-element.77) | copy-start | bytes 76
  102.1 4.4 %collective-permute-start.6 = (f32[6,1,1024]{2,1,0:T(1,128)S(1)}, f32[6,1,1024]{2,1,0:T(1,128)S(1)}, u32[]{:S(2)}, u32[]{:S(2)}) collective-permute-start(f32[6,1,1024]{2,1,0:T(1,128)S(1)} %get-tuple-element.45), channel_id=1, source_target_pairs={{64,0},{128,64},{192,128},{256,192},{320,256},{384,320},{448,384},... | collective-permute-start | bytes 73736 | tf_op jit(solution)/shard_map/ppermute | solution.py:26
  104.0 5.1 %collective-permute-start.7 = (f32[6,1,1024]{2,1,0:T(1,128)S(1)}, f32[6,1,1024]{2,1,0:T(1,128)S(1)}, u32[]{:S(2)}, u32[]{:S(2)}) collective-permute-start(f32[6,1,1024]{2,1,0:T(1,128)S(1)} %get-tuple-element.46), channel_id=1, source_target_pairs={{0,64},{64,128},{128,192},{192,256},{256,320},{320,384},{384,448},... | collective-permute-start | bytes 73736 | tf_op jit(solution)/shard_map/ppermute | solution.py:25
  109.6 7.4 %copy-start.28 = (f32[6]{0:T(128)S(1)}, f32[6]{0:T(128)}, u32[]{:S(2)}) copy-start(f32[6]{0:T(128)} %get-tuple-element.75) | copy-start | bytes 76
  109.9 4.4 %collective-permute-start.8 = (f32[6,1,1024]{2,1,0:T(1,128)S(1)}, f32[6,1,1024]{2,1,0:T(1,128)S(1)}, u32[]{:S(2)}, u32[]{:S(2)}) collective-permute-start(f32[6,1,1024]{2,1,0:T(1,128)S(1)} %get-tuple-element.39), channel_id=1, source_target_pairs={{64,0},{128,64},{192,128},{256,192},{320,256},{384,320},{448,384},... | collective-permute-start | bytes 73736 | tf_op jit(solution)/shard_map/ppermute | solution.py:26
  111.8 5.1 %collective-permute-start.9 = (f32[6,1,1024]{2,1,0:T(1,128)S(1)}, f32[6,1,1024]{2,1,0:T(1,128)S(1)}, u32[]{:S(2)}, u32[]{:S(2)}) collective-permute-start(f32[6,1,1024]{2,1,0:T(1,128)S(1)} %get-tuple-element.40), channel_id=1, source_target_pairs={{0,64},{64,128},{128,192},{192,256},{256,320},{320,384},{384,448},... | collective-permute-start | bytes 73736 | tf_op jit(solution)/shard_map/ppermute | solution.py:25
  117.5 7.4 %copy-start.26 = (f32[6]{0:T(128)S(1)}, f32[6]{0:T(128)}, u32[]{:S(2)}) copy-start(f32[6]{0:T(128)} %get-tuple-element.73) | copy-start | bytes 76
  117.5 7.4 %copy-start.27 = (f32[6]{0:T(128)S(1)}, f32[6]{0:T(128)}, u32[]{:S(2)}) copy-start(f32[6]{0:T(128)} %get-tuple-element.74) | copy-start | bytes 76
  117.8 5.2 %collective-permute-start.10 = (f32[6,1,1024]{2,1,0:T(1,128)S(1)}, f32[6,1,1024]{2,1,0:T(1,128)S(1)}, u32[]{:S(2)}, u32[]{:S(2)}) collective-permute-start(f32[6,1,1024]{2,1,0:T(1,128)S(1)} %get-tuple-element.33), channel_id=1, source_target_pairs={{64,0},{128,64},{192,128},{256,192},{320,256},{384,320},{448,384},... | collective-permute-start | bytes 73736 | tf_op jit(solution)/shard_map/ppermute | solution.py:26
  119.7 5.1 %collective-permute-start.11 = (f32[6,1,1024]{2,1,0:T(1,128)S(1)}, f32[6,1,1024]{2,1,0:T(1,128)S(1)}, u32[]{:S(2)}, u32[]{:S(2)}) collective-permute-start(f32[6,1,1024]{2,1,0:T(1,128)S(1)} %get-tuple-element.34), channel_id=1, source_target_pairs={{0,64},{64,128},{128,192},{192,256},{256,320},{320,384},{384,448},... | collective-permute-start | bytes 73736 | tf_op jit(solution)/shard_map/ppermute | solution.py:25
  125.3 7.4 %copy-start.18 = (f32[6]{0:T(128)S(1)}, f32[6]{0:T(128)}, u32[]{:S(2)}) copy-start(f32[6]{0:T(128)} %get-tuple-element.5) | copy-start | bytes 76
  125.3 7.4 %copy-start.19 = (f32[6]{0:T(128)S(1)}, f32[6]{0:T(128)}, u32[]{:S(2)}) copy-start(f32[6]{0:T(128)} %get-tuple-element.65) | copy-start | bytes 76
  125.3 7.4 %copy-start.20 = (f32[6]{0:T(128)S(1)}, f32[6]{0:T(128)}, u32[]{:S(2)}) copy-start(f32[6]{0:T(128)} %get-tuple-element.66) | copy-start | bytes 76
  125.3 7.4 %copy-start.21 = (f32[6]{0:T(128)S(1)}, f32[6]{0:T(128)}, u32[]{:S(2)}) copy-start(f32[6]{0:T(128)} %get-tuple-element.67) | copy-start | bytes 76
  125.4 7.4 %copy-start.22 = (f32[6]{0:T(128)S(1)}, f32[6]{0:T(128)}, u32[]{:S(2)}) copy-start(f32[6]{0:T(128)} %get-tuple-element.68) | copy-start | bytes 76
  125.4 7.4 %copy-start.23 = (f32[6]{0:T(128)S(1)}, f32[6]{0:T(128)}, u32[]{:S(2)}) copy-start(f32[6]{0:T(128)} %get-tuple-element.69) | copy-start | bytes 76
  125.4 7.4 %copy-start.24 = (f32[6]{0:T(128)S(1)}, f32[6]{0:T(128)}, u32[]{:S(2)}) copy-start(f32[6]{0:T(128)} %get-tuple-element.70) | copy-start | bytes 76
  125.4 7.4 %copy-start.25 = (f32[6]{0:T(128)S(1)}, f32[6]{0:T(128)}, u32[]{:S(2)}) copy-start(f32[6]{0:T(128)} %get-tuple-element.72) | copy-start | bytes 76
  125.7 6.2 %collective-permute-start.12 = (f32[6,1,1024]{2,1,0:T(1,128)S(1)}, f32[6,1,1024]{2,1,0:T(1,128)S(1)}, u32[]{:S(2)}, u32[]{:S(2)}) collective-permute-start(f32[6,1,1024]{2,1,0:T(1,128)S(1)} %get-tuple-element.31), channel_id=1, source_target_pairs={{64,0},{128,64},{192,128},{256,192},{320,256},{384,320},{448,384},... | collective-permute-start | bytes 73736 | tf_op jit(solution)/shard_map/ppermute | solution.py:26
  127.6 5.1 %collective-permute-start.13 = (f32[6,1,1024]{2,1,0:T(1,128)S(1)}, f32[6,1,1024]{2,1,0:T(1,128)S(1)}, u32[]{:S(2)}, u32[]{:S(2)}) collective-permute-start(f32[6,1,1024]{2,1,0:T(1,128)S(1)} %get-tuple-element.32), channel_id=1, source_target_pairs={{0,64},{64,128},{128,192},{192,256},{256,320},{320,384},{384,448},... | collective-permute-start | bytes 73736 | tf_op jit(solution)/shard_map/ppermute | solution.py:25
  148.9 29.0 %copy-start.10 = (pred[64,128]{1,0:T(8,128)(4,1)S(1)}, pred[64,128]{1,0:T(8,128)(4,1)}, u32[]{:S(2)}) copy-start(pred[64,128]{1,0:T(8,128)(4,1)} %copy-done.9) | copy-start | bytes 24580
  148.9 29.0 %copy-start.15 = (pred[6,128]{1,0:T(8,128)(4,1)S(1)}, pred[6,128]{1,0:T(8,128)(4,1)}, u32[]{:S(2)}) copy-start(pred[6,128]{1,0:T(8,128)(4,1)} %copy-done.14) | copy-start | bytes 2308
  148.9 29.6 %copy-start.11 = (f32[128,128]{1,0:T(8,128)S(1)}, f32[128,128]{1,0:T(8,128)}, u32[]{:S(2)}) copy-start(f32[128,128]{1,0:T(8,128)} %param.18) | copy-start | bytes 196612
  148.9 48.5 %copy-start.17 = (f32[26]{0:T(128)S(1)}, f32[26]{0:T(128)}, u32[]{:S(2)}) copy-start(f32[26]{0:T(128)} %copy-done.16) | copy-start | bytes 316
  149.5 48.1 %copy-start.3 = (f32[24,16,128]{2,1,0:T(8,128)S(1)}, f32[24,16,128]{2,1,0:T(8,128)}, u32[]{:S(2)}) copy-start(f32[24,16,128]{2,1,0:T(8,128)} %param.12) | copy-start | bytes 589828
  149.5 48.1 %copy-start.5 = (f32[24,16,128]{2,1,0:T(8,128)S(1)}, f32[24,16,128]{2,1,0:T(8,128)}, u32[]{:S(2)}) copy-start(f32[24,16,128]{2,1,0:T(8,128)} %param.11) | copy-start | bytes 589828
  178.9 4.7 %collective-permute-start.14 = (f32[1,16,128]{2,1,0:T(8,128)S(1)}, f32[1,16,128]{2,1,0:T(8,128)S(1)}, u32[]{:S(2)}, u32[]{:S(2)}) collective-permute-start(f32[1,16,128]{2,1,0:T(8,128)S(1)} %get-tuple-element.63), channel_id=1, source_target_pairs={{0,64},{64,128},{128,192},{192,256},{256,320},{320,384},{384,448},... | collective-permute-start | bytes 24584 | tf_op jit(solution)/shard_map/ppermute | solution.py:25
  182.7 4.1 %collective-permute-start.15 = (f32[1,16,128]{2,1,0:T(8,128)S(1)}, f32[1,16,128]{2,1,0:T(8,128)S(1)}, u32[]{:S(2)}, u32[]{:S(2)}) collective-permute-start(f32[1,16,128]{2,1,0:T(8,128)S(1)} %get-tuple-element.64), channel_id=1, source_target_pairs={{64,0},{128,64},{192,128},{256,192},{320,256},{384,320},{448,384},... | collective-permute-start | bytes 24584 | tf_op jit(solution)/shard_map/ppermute | solution.py:26
  186.9 9.2 %collective-permute-start.16 = (f32[26,1,128]{2,1,0:T(1,128)S(1)}, f32[26,1,128]{2,1,0:T(1,128)S(1)}, u32[]{:S(2)}, u32[]{:S(2)}) collective-permute-start(f32[26,1,128]{2,1,0:T(1,128)S(1)} %get-tuple-element.61), channel_id=1, source_target_pairs={{0,1},{1,2},{2,3},{3,4},{4,5},{5,6},{6,7},{7,8},{8,9},{9,10},{10,1... | collective-permute-start | bytes 39944 | tf_op jit(solution)/shard_map/ppermute | solution.py:25
  190.3 7.1 %collective-permute-start.17 = (f32[26,1,128]{2,1,0:T(1,128)S(1)}, f32[26,1,128]{2,1,0:T(1,128)S(1)}, u32[]{:S(2)}, u32[]{:S(2)}) collective-permute-start(f32[26,1,128]{2,1,0:T(1,128)S(1)} %get-tuple-element.62), channel_id=1, source_target_pairs={{1,0},{2,1},{3,2},{4,3},{5,4},{6,5},{7,6},{8,7},{9,8},{10,9},{11,1... | collective-permute-start | bytes 39944 | tf_op jit(solution)/shard_map/ppermute | solution.py:26
  (7 other events, 30.6 us)
where the time goes:
time: 202 us; the launch traced here: 198 us
  starting transfers between devices  83.3 us (41%)
  waiting for transfers between devices  30.7 us (15%)
  blocking collectives  28.4 us (14%)
  other arithmetic  21.3 us (11%)
  local copies, waits for them, and re-layouts  20.9 us (10%)
  matrix products  12.4 us (6%)
    all_to_all x1, blocking collectives, local(): lax.all_to_all(to_patches(filtered, lon_count), 'lon', split_axis=0, conc...  28.4 us
    ppermute x9, starting transfers between devices, padded_2(): before = lax.ppermute(last, axis, up)  25.4 us
    all_to_all x1, starting transfers between devices, local(): lax.all_to_all(slot_params, 'lon', split_axis=0, concat_axis=0, tiled=True)  23.4 us
    ppermute x9, starting transfers between devices, padded_2(): after = lax.ppermute(leading, axis, down)  22.8 us
    all_to_all x1, waiting for transfers between devices, local(): lax.all_to_all(packed, 'lon', split_axis=0, concat_axis=0, tiled=True)  12.8 us
    ppermute x9, waiting for transfers between devices, padded_2(): before = lax.ppermute(last, axis, up)  11.8 us
    all_to_all x1, starting transfers between devices, local(): lax.all_to_all(packed, 'lon', split_axis=0, concat_axis=0, tiled=True)  11.7 us
    sin x1, other arithmetic, fourier_table(): return jnp.concatenate([jnp.cos(angles), jnp.sin(angles)], axis=1)  9.01 us
  transfers between devices with their start and end apart: 20, of which 11 were waited for; matrix products, arithmetic and copies ran while one was open for 11% of the time, Pallas kernels for 0%

commit v1 on v0

v1 whole, which is shorter than its diff:
```python
import math

import jax
import jax.numpy as jnp
import numpy as np
from jax import lax
from jax.experimental import pallas as pl
from jax.experimental.pallas import tpu as pltpu
from jax.sharding import PartitionSpec as P

MAXIT = 6
ROWS = 24
COLS = 16
CELLS = ROWS * COLS
LON = 1024
LAT = 384
MODES = 128
PATCHES = 64
SLOTS = 6
HOST = 2
EXT = 40
BLOCKS = LON // 128

f32 = jnp.float32
bf16 = jnp.bfloat16
VMEM = pl.BlockSpec(memory_space=pltpu.VMEM)
ANY = pl.BlockSpec(memory_space=pl.ANY)


def filter_tables():
    b = np.arange(128)[:, None].astype(np.float64)
    table = np.zeros((4, 256, 256))
    wave = np.zeros((4, 256))
    gain = np.zeros((4, 256))
    k2 = np.arange(65)[None, :]
    angle = 2 * np.pi * b * k2 / 128
    table[0, :128, :65] = np.cos(angle)
    table[0, :128, 65:128] = np.sin(angle[:, 1:64])
    wave[0, :65] = 8 * np.arange(65)
    wave[0, 65:128] = 8 * np.arange(1, 64)
    gain[0, :128] = 2.0
    gain[0, 0] = gain[0, 64] = 1.0
    k2 = np.arange(64)[None, :]
    angle = 2 * np.pi * b * (4 + 8 * k2) / 1024
    table[0, 128:, 128:192] = np.cos(angle)
    table[0, 128:, 192:] = np.sin(angle)
    wave[0, 128:192] = wave[0, 192:] = 4 + 8 * np.arange(64)
    gain[0, 128:] = 2.0
    for k1 in (1, 2, 3):
        k = k1 + 8 * np.arange(128)
        angle = 2 * np.pi * b * k[None, :] / 1024
        c, s = np.cos(angle), np.sin(angle)
        table[k1, :128, :128] = c
        table[k1, :128, 128:] = -s
        table[k1, 128:, :128] = s
        table[k1, 128:, 128:] = c
        wave[k1, :128] = wave[k1, 128:] = np.minimum(k, 1024 - k)
        gain[k1] = 2.0
    return table, wave, gain / LON


def split_value(x):
    high = x.astype(bf16)
    low = (x - high.astype(f32)).astype(bf16)
    return high, low


def dot3(a, b, dims):
    ah, al = a
    bh, bl = b

    def dot(x, y):
        return lax.dot_general(x, y, (dims, ((), ())), preferred_element_type=f32)

    return dot(ah, bh) + (dot(ah, bl) + dot(al, bh))


def block_swap(x):
    sub = lax.broadcasted_iota(jnp.int32, x.shape, 1)
    group = lax.broadcasted_iota(jnp.int32, x.shape, 2) // 16
    for d in (4, 2, 1):
        here = sub & d
        stay = here == (group & d)
        up = pltpu.roll(pltpu.roll(x, d, 1), 128 - 16 * d, 2)
        if d == 4:
            moved = up
        else:
            down = pltpu.roll(pltpu.roll(x, 8 - d, 1), 16 * d, 2)
            moved = jnp.where(here != 0, up, down)
        x = jnp.where(stay, x, moved)
    return x


def load_metric(metric, ext, sem, lat):
    start = pl.multiple_of(lat * ROWS, 8)
    low = pl.multiple_of(jnp.maximum(start - 8, 0), 8)
    high = pl.multiple_of(jnp.minimum(start + ROWS, LAT - 8), 8)
    return [
        pltpu.make_async_copy(metric.at[pl.ds(start, ROWS)], ext.at[pl.ds(8, ROWS)], sem.at[0]),
        pltpu.make_async_copy(metric.at[pl.ds(low, 8)], ext.at[pl.ds(0, 8)], sem.at[1]),
        pltpu.make_async_copy(metric.at[pl.ds(high, 8)], ext.at[pl.ds(8 + ROWS, 8)], sem.at[2]),
    ]


def mask_metric(ext, lat):
    ext[0:8, :] = ext[0:8, :] * jnp.where(lat > 0, 1.0, 0.0)
    ext[32:40, :] = ext[32:40, :] * jnp.where(lat < LAT // ROWS - 1, 1.0, 0.0)


def selection(holder):
    hb = jnp.broadcast_to(holder.astype(f32), (MODES, MODES))
    ha = hb.T
    ia = lax.broadcasted_iota(jnp.int32, (MODES, MODES), 0)
    ib = lax.broadcasted_iota(jnp.int32, (MODES, MODES), 1)
    same = jnp.where(ha == hb, 1.0, 0.0)
    before = jnp.where(ia < ib, 1.0, 0.0)
    after = jnp.where(ib < ia, 1.0, 0.0)
    rank_row = jnp.sum(same * before, axis=0, keepdims=True)
    rank_col = jnp.sum(same * after, axis=1, keepdims=True)
    over_row = jnp.where(rank_row >= HOST, 1.0, 0.0)
    over_col = jnp.where(rank_col >= HOST, 1.0, 0.0)
    over_index = jnp.sum(over_col * before, axis=0, keepdims=True)
    patch_a = (ia & (PATCHES - 1)).astype(f32)
    patch_b = (ib & (PATCHES - 1)).astype(f32)
    turn_a = (ia // PATCHES).astype(f32)
    turn_b = (ib // PATCHES).astype(f32)
    count_col = jnp.sum(jnp.where(hb == patch_a, 1.0, 0.0), axis=1, keepdims=True)
    count_row = jnp.sum(jnp.where(ha == patch_b, 1.0, 0.0), axis=0, keepdims=True)
    free_col = jnp.where(turn_a >= count_col, 1.0, 0.0)
    free_row = jnp.where(turn_b >= count_row, 1.0, 0.0)
    free_index = jnp.sum(free_row * after, axis=1, keepdims=True)
    home = jnp.where(ia.astype(f32) == rank_row * PATCHES + hb, 1.0, 0.0)
    guest = free_col * jnp.where(free_index == over_index, 1.0, 0.0)
    hosted = over_row * guest + (1.0 - over_row) * home
    rest = []
    for first in (2, 4):
        rest.append(
            jnp.where(ia.astype(f32) + first * PATCHES == rank_row * PATCHES + hb, 1.0, 0.0)
        )
    return jnp.concatenate([hosted] + rest, axis=0)


def cell_column(row):
    lane = lax.broadcasted_iota(jnp.int32, (COLS, 128), 1)
    sub = lax.broadcasted_iota(jnp.int32, (COLS, 128), 0)
    picked = jnp.where(lane == sub, jnp.broadcast_to(row, (COLS, 128)), 0.0)
    return jnp.broadcast_to(jnp.sum(picked, axis=1, keepdims=True), (COLS, 128))


def patch_kernel(
    u, v, t, q, metric, holder, project, depth, sweeps,
    packed, params, hosted, cell_metric,
    ext, own, field, chosen, sem,
):
    lat = lax.axis_index("lat")
    lon = lax.axis_index("lon")
    copies = load_metric(metric, ext, sem, lat)
    for c in copies:
        c.start()
    select = selection(holder[...])
    chosen[...] = select
    hosted[...] = select[: HOST * PATCHES].astype(bf16)
    params[...] = jnp.zeros_like(params)
    count = jnp.sum(jnp.where(holder[...] == lon, 1.0, 0.0), axis=1, keepdims=True)
    for s in range(SLOTS):
        row = chosen[pl.ds(s * PATCHES + lon, 1), :]
        value = jnp.sum(row * depth[...], axis=1, keepdims=True)
        params[0, s : s + 1, :] = jnp.broadcast_to(value, (1, 128))
        value = jnp.sum(row * sweeps[...].astype(f32), axis=1, keepdims=True)
        params[1, s : s + 1, :] = jnp.broadcast_to(value, (1, 128))
        params[2, s : s + 1, :] = jnp.broadcast_to(jnp.where(count > s, 1.0, 0.0), (1, 128))
    sel = select.astype(bf16)
    proj_high, proj_low = split_value(project[...])
    rows_high = jnp.dot(sel, proj_high, preferred_element_type=f32).astype(bf16)
    rows_low = jnp.dot(sel, proj_low, preferred_element_type=f32).astype(bf16)
    for c in copies:
        c.wait()
    mask_metric(ext, lat)

    block = lon // 8
    offset = (lon % 8) * COLS

    def lanes(b):
        return ext[:, pl.ds(pl.multiple_of(b * 128, 128), 128)]

    here = lanes(block)
    own[...] = pltpu.roll(here, (128 - offset) % 128, 1)
    west_block = jnp.where(offset == 0, (block + BLOCKS - 1) % BLOCKS, block)
    east_block = jnp.where(offset == 128 - COLS, (block + 1) % BLOCKS, block)
    west_metric = pltpu.roll(lanes(west_block), (129 - offset) % 128, 1)[8:32, 0:1]
    east_metric = pltpu.roll(lanes(east_block), (256 - COLS - offset) % 128, 1)[8:32, 0:1]

    uu = u[...].reshape(CELLS, MODES)
    vv = v[...].reshape(CELLS, MODES)
    virtual = t[...].reshape(CELLS, MODES) * (1.0 + 0.61 * q[...].reshape(CELLS, MODES))
    eighth = 0.125 * virtual
    to_west = eighth - 0.25 * uu
    to_east = eighth + 0.25 * uu
    to_south = eighth - 0.25 * vv
    to_north = eighth + 0.25 * vv
    col = lax.broadcasted_iota(jnp.int32, (CELLS, MODES), 0) & (COLS - 1)
    around = jnp.where(col == COLS - 1, 0.0, pltpu.roll(to_west, CELLS - 1, 0))
    around = around + jnp.where(col == 0, 0.0, pltpu.roll(to_east, 1, 0))
    zero = jnp.zeros((COLS, MODES), f32)
    around = around + jnp.concatenate([to_south[COLS:], zero], axis=0)
    around = around + jnp.concatenate([zero, to_north[: CELLS - COLS]], axis=0)
    scale = jnp.concatenate([cell_column(own[8 + r : 9 + r, :]) for r in range(ROWS)], axis=0)
    cell_metric[...] = 0.25 * scale
    field[0:CELLS, :] = virtual + scale * (around - 0.5 * virtual)

    field[CELLS:, :] = jnp.zeros((128, MODES), f32)
    first = t[:, 0, :] * (1.0 + 0.61 * q[:, 0, :])
    last = t[:, COLS - 1, :] * (1.0 + 0.61 * q[:, COLS - 1, :])
    edge_west = jnp.broadcast_to(west_metric, (ROWS, MODES)) * (0.125 * first - 0.25 * u[:, 0, :])
    edge_east = jnp.broadcast_to(east_metric, (ROWS, MODES)) * (
        0.125 * last + 0.25 * u[:, COLS - 1, :]
    )
    for rg in range(3):
        field[pl.ds(CELLS + rg, 8, stride=COLS), :] = edge_west[8 * rg : 8 * rg + 8]
        field[pl.ds(CELLS + 3 + rg, 8, stride=COLS), :] = edge_east[8 * rg : 8 * rg + 8]
    edge_south = cell_column(own[7:8, :]) * to_south[0:COLS]
    edge_north = cell_column(own[32:33, :]) * to_north[CELLS - COLS :]
    field[CELLS + 6 : CELLS + 16, :] = edge_north[0:10]
    field[CELLS + 22 : CELLS + 28, :] = edge_north[10:16]
    field[CELLS + 118 : CELLS + 128, :] = edge_south[0:10]
    field[CELLS + 102 : CELLS + 108, :] = edge_south[10:16]

    value = dot3((rows_high, rows_low), split_value(field[...]), ((1,), (1,)))
    for s in range(SLOTS):
        for part in range(4):
            packed[pl.ds(s * 4 + part, PATCHES, stride=4 * SLOTS), :] = value[
                s * PATCHES : (s + 1) * PATCHES, part * 128 : (part + 1) * 128
            ]


def patch_stage(u, v, t, q, metric, holder, project, depth, sweeps):
    return pl.pallas_call(
        patch_kernel,
        name="patch_stage",
        out_shape=(
            jax.ShapeDtypeStruct((PATCHES * SLOTS * 4, 128), f32),
            jax.ShapeDtypeStruct((3, 8, 128), f32),
            jax.ShapeDtypeStruct((HOST * PATCHES, MODES), bf16),
            jax.ShapeDtypeStruct((CELLS, MODES), f32),
        ),
        in_specs=[VMEM, VMEM, VMEM, VMEM, ANY, VMEM, VMEM, VMEM, VMEM],
        out_specs=(VMEM, VMEM, VMEM, VMEM),
        scratch_shapes=[
            pltpu.VMEM((EXT, LON), f32),
            pltpu.VMEM((EXT, 128), f32),
            pltpu.VMEM((CELLS + 128, MODES), f32),
            pltpu.VMEM((SLOTS * PATCHES, MODES), f32),
            pltpu.SemaphoreType.DMA((3,)),
        ],
    )(u, v, t, q, metric, holder, project, depth, sweeps)


def band_kernel(received, band, south, north):
    lane = lax.broadcasted_iota(jnp.int32, (PATCHES, 128), 1)
    place = lane & (COLS - 1)
    row = lax.broadcasted_iota(jnp.int32, (8, 128), 0)
    for s in range(SLOTS):
        edge = received[pl.ds(s * 4 + 3, PATCHES, stride=4 * SLOTS), :]
        from_east = pltpu.roll(edge, PATCHES - 1, 0)
        from_west = pltpu.roll(edge, 1, 0)
        bands = []
        for rg in range(3):
            x = received[pl.ds(s * 4 + rg, PATCHES, stride=4 * SLOTS), :]
            x = x + jnp.where(place == COLS - 1, pltpu.roll(from_east, 15 - rg, 1), 0.0)
            x = x + jnp.where(place == 0, pltpu.roll(from_west, 128 - 3 - rg, 1), 0.0)
            bands.append(block_swap(x.reshape(BLOCKS, 8, 128)))
        rim = jnp.where(
            lane < 10,
            pltpu.roll(edge, 128 - 6, 1),
            jnp.where(
                lane < 16,
                pltpu.roll(edge, 128 - 12, 1),
                jnp.where(lane < 122, pltpu.roll(edge, 128 - 6, 1), pltpu.roll(edge, 20, 1)),
            ),
        )
        rim = block_swap(rim.reshape(BLOCKS, 8, 128))
        for b in range(BLOCKS):
            at = slice(b * 128, (b + 1) * 128)
            for rg in range(3):
                band[s, 8 * rg : 8 * rg + 8, at] = bands[rg][b]
            south[s, :, at] = jnp.where(row == 7, rim[b], bands[0][b])
            north[s, :, at] = jnp.where(row == 0, rim[b], bands[2][b])


def band_stage(received):
    return pl.pallas_call(
        band_kernel,
        name="band_stage",
        out_shape=(
            jax.ShapeDtypeStruct((SLOTS, ROWS, LON), f32),
            jax.ShapeDtypeStruct((SLOTS, 8, LON), f32),
            jax.ShapeDtypeStruct((SLOTS, 8, LON), f32),
        ),
        in_specs=[VMEM],
        out_specs=(VMEM, VMEM, VMEM),
    )(received)


def solve_slots(
    first, count, band, south, north, from_south, from_north, params, cutoff, wave, gain,
    table_high, table_low, ext, spectral, solved, lat,
):
    row = lax.broadcasted_iota(jnp.int32, (8, LON), 0)
    for i in range(count):
        s = first + i
        depth = params[0, s : s + 1, 0:1]
        number = params[1, s : s + 1, 0:1]
        depth = jnp.where(depth > 0.0, depth, 1.0)
        centre = 1.0 + 8.0 * depth
        radius = 8.0 * depth
        relative = centre / radius
        ratio = 1.0 / relative

        def wide(x):
            return jnp.broadcast_to(x, (EXT, LON))

        below = from_south[s]
        above = from_north[s]
        source = jnp.concatenate(
            [
                below + jnp.where(row == 7, south[s], 0.0),
                band[s, 0:8] + jnp.where(row == 0, below, 0.0),
                band[s, 8:16],
                band[s, 16:24] + jnp.where(row == 7, above, 0.0),
                above + jnp.where(row == 0, north[s], 0.0),
            ],
            axis=0,
        )
        coupling = wide(depth) * ext[...]
        direction = source * wide(1.0 / centre)
        residual = source
        total = jnp.zeros_like(source)
        for sweep in range(MAXIT):
            total = total + wide(jnp.where(number > sweep, 1.0, 0.0)) * direction
            if sweep + 1 < MAXIT:
                around = (
                    pltpu.roll(direction, LON - 1, 1)
                    + pltpu.roll(direction, 1, 1)
                    + pltpu.roll(direction, EXT - 1, 0)
                    + pltpu.roll(direction, 1, 0)
                )
                residual = residual - direction + coupling * (around - 4.0 * direction)
                after = 1.0 / (2.0 * relative - ratio)
                direction = (
                    wide(after * ratio) * direction + wide(2.0 * after / radius) * residual
                )
                ratio = after
        x = [total[:, 128 * a : 128 * a + 128] for a in range(BLOCKS)]
        root = math.sqrt(0.5)
        s04, d04 = x[0] + x[4], x[0] - x[4]
        s26, d26 = x[2] + x[6], x[2] - x[6]
        s15, d15 = x[1] + x[5], x[1] - x[5]
        s37, d37 = x[3] + x[7], x[3] - x[7]
        even, odd = s04 + s26, s15 + s37
        lean, turn = root * (d15 - d37), root * (d15 + d37)
        at = slice(i * EXT, (i + 1) * EXT)
        spectral[0, at, 0:128] = even + odd
        spectral[0, at, 128:256] = even - odd
        spectral[1, at, 0:128] = d04 + lean
        spectral[1, at, 128:256] = -d26 - turn
        spectral[2, at, 0:128] = s04 - s26
        spectral[2, at, 128:256] = s37 - s15
        spectral[3, at, 0:128] = d04 - lean
        spectral[3, at, 128:256] = d26 - turn

    index = lax.broadcasted_iota(jnp.int32, (EXT, 128), 0) + (lat * ROWS - 8)
    lane = lax.broadcasted_iota(jnp.int32, (EXT, 128), 1)
    limit = jnp.zeros((EXT, 1), f32)
    for b in range(LAT // 128):
        picked = jnp.where(
            lane + 128 * b == index, jnp.broadcast_to(cutoff[b : b + 1, :], (EXT, 128)), 0.0
        )
        limit = limit + jnp.sum(picked, axis=1, keepdims=True)
    limit = jnp.where(limit > 0.0, limit, 1.0)
    inverse = 1.0 / (limit * (0.5 * LON))
    for k in range(4):
        table = (table_high[k], table_low[k])
        ratio = jnp.broadcast_to(wave[k : k + 1, :], (EXT, 256)) * jnp.broadcast_to(
            inverse, (EXT, 256)
        )
        ratio = ratio * ratio
        damping = jnp.broadcast_to(gain[k : k + 1, :], (EXT, 256)) / (1.0 + ratio * ratio)
        damping = jnp.concatenate([damping] * count, axis=0)
        spectrum = dot3(split_value(spectral[k, 0 : count * EXT, :]), table, ((1,), (0,)))
        spectral[k, 0 : count * EXT, :] = dot3(
            split_value(spectrum * damping), table, ((1,), (1,))
        )
    root = math.sqrt(0.5)
    y0 = spectral[0, 0 : count * EXT, 0:128]
    y4 = spectral[0, 0 : count * EXT, 128:256]
    p1, q1 = spectral[1, 0 : count * EXT, 0:128], spectral[1, 0 : count * EXT, 128:256]
    p2, q2 = spectral[2, 0 : count * EXT, 0:128], spectral[2, 0 : count * EXT, 128:256]
    p3, q3 = spectral[3, 0 : count * EXT, 0:128], spectral[3, 0 : count * EXT, 128:256]
    even, odd = y0 + y4, y0 - y4
    a1, b1 = root * p1, root * q1
    a3, b3 = root * p3, root * q3
    swing = q3 - q1
    parts = [None] * 8
    base, side = even + p2, p1 + p3
    parts[0], parts[4] = base + side, base - side
    base, side = even - p2, swing
    parts[2], parts[6] = base + side, base - side
    base, side = odd - q2, (a1 - b1) - (a3 + b3)
    parts[1], parts[5] = base + side, base - side
    base, side = odd + q2, (a3 - b3) - (a1 + b1)
    parts[3], parts[7] = base + side, base - side
    for i in range(count):
        for a in range(BLOCKS):
            solved[i, :, 128 * a : 128 * a + 128] = parts[a][i * EXT : (i + 1) * EXT]


def host_kernel(
    band, south, north, from_south, from_north, params, metric, cutoff, wave, gain,
    table_high, table_low,
    packed, own_modes,
    ext, spectral, solved, sem,
):
    lat = lax.axis_index("lat")
    copies = load_metric(metric, ext, sem, lat)
    for c in copies:
        c.start()
    for c in copies:
        c.wait()
    mask_metric(ext, lat)
    solve_slots(
        0, HOST, band, south, north, from_south, from_north, params, cutoff, wave, gain,
        table_high, table_low, ext, spectral, solved, lat,
    )
    lane = lax.broadcasted_iota(jnp.int32, (PATCHES, 128), 1)
    place = lane & (COLS - 1)
    for i in range(HOST):
        owned = jnp.broadcast_to(params[2, i : i + 1, 0:1], (ROWS, LON))
        own_modes[i] = solved[i, 8:32, :] * owned
        tiles = []
        for tile in range(5):
            x = jnp.stack(
                [solved[i, 8 * tile : 8 * tile + 8, 128 * b : 128 * b + 128] for b in range(BLOCKS)]
            )
            tiles.append(block_swap(x).reshape(PATCHES, 128))
        edge = jnp.zeros((PATCHES, 128), f32)
        for rg in range(3):
            x = tiles[rg + 1]
            packed[pl.ds(i * 4 + rg, PATCHES, stride=4 * HOST), :] = x
            west = pltpu.roll(pltpu.roll(x, 1, 0), 128 - 15 + rg, 1)
            east = pltpu.roll(pltpu.roll(x, PATCHES - 1, 0), 3 + rg, 1)
            edge = jnp.where(place == rg, west, edge)
            edge = jnp.where(place == 3 + rg, east, edge)
        far, near = tiles[4], tiles[0]
        edge = jnp.where((lane >= 6) & (lane < 16), pltpu.roll(far, 6, 1), edge)
        edge = jnp.where((lane >= 22) & (lane < 28), pltpu.roll(far, 12, 1), edge)
        edge = jnp.where(lane >= 118, pltpu.roll(near, 6, 1), edge)
        edge = jnp.where((lane >= 102) & (lane < 108), pltpu.roll(near, 108, 1), edge)
        packed[pl.ds(i * 4 + 3, PATCHES, stride=4 * HOST), :] = edge


def solver_scratch(count):
    return [
        pltpu.VMEM((EXT, LON), f32),
        pltpu.VMEM((4, count * EXT, 256), f32),
        pltpu.VMEM((count, EXT, LON), f32),
        pltpu.SemaphoreType.DMA((3,)),
    ]


def host_stage(*operands):
    return pl.pallas_call(
        host_kernel,
        name="host_stage",
        out_shape=(
            jax.ShapeDtypeStruct((PATCHES * HOST * 4, 128), f32),
            jax.ShapeDtypeStruct((HOST, ROWS, LON), f32),
        ),
        in_specs=[VMEM] * 6 + [ANY] + [VMEM] * 5,
        out_specs=(VMEM, VMEM),
        scratch_shapes=solver_scratch(HOST),
    )(*operands)


def rest_kernel(
    band, south, north, from_south, from_north, params, metric, cutoff, wave, gain,
    table_high, table_low, own_modes, hosted, expand,
    modes, expand_high, expand_low,
    ext, spectral, solved, sem,
):
    lat = lax.axis_index("lat")
    copies = load_metric(metric, ext, sem, lat)
    for c in copies:
        c.start()
    for c in copies:
        c.wait()
    mask_metric(ext, lat)
    high, low = split_value(expand[...])
    dims = (((1,), (1,)), ((), ()))
    expand_high[...] = lax.dot_general(
        hosted[...], high, dims, preferred_element_type=f32
    ).astype(bf16)
    expand_low[...] = lax.dot_general(
        hosted[...], low, dims, preferred_element_type=f32
    ).astype(bf16)
    modes[0:HOST] = own_modes[...]
    solve_slots(
        HOST, SLOTS - HOST, band, south, north, from_south, from_north, params, cutoff, wave, gain,
        table_high, table_low, ext, spectral, solved, lat,
    )
    for i in range(SLOTS - HOST):
        modes[HOST + i] = solved[i, 8:32, :]


def rest_stage(*operands):
    return pl.pallas_call(
        rest_kernel,
        name="rest_stage",
        out_shape=(
            jax.ShapeDtypeStruct((SLOTS, ROWS, LON), f32),
            jax.ShapeDtypeStruct((MODES, MODES), bf16),
            jax.ShapeDtypeStruct((MODES, MODES), bf16),
        ),
        in_specs=[VMEM] * 6 + [ANY] + [VMEM] * 8,
        out_specs=(VMEM, VMEM, VMEM),
        scratch_shapes=solver_scratch(SLOTS - HOST),
    )(*operands)


def wind_kernel(received, expand_high, expand_low, cell_metric, u, v, u_new, v_new, tall, edge):
    table = (expand_high[...], expand_low[...])
    for part in range(4):
        x = jnp.concatenate(
            [received[pl.ds(i * 4 + part, PATCHES, stride=4 * HOST), :] for i in range(HOST)],
            axis=0,
        )
        value = dot3(split_value(x.T), table, ((1,), (0,)))
        if part < 3:
            tall[COLS + part * 128 : COLS + part * 128 + 128, :] = value
        else:
            edge[...] = value
    tall[0:10, :] = edge[118:128, :]
    tall[10:16, :] = edge[102:108, :]
    tall[CELLS + COLS : CELLS + COLS + 10, :] = edge[6:16, :]
    tall[CELLS + COLS + 10 : CELLS + 2 * COLS, :] = edge[22:28, :]
    pressure = tall[COLS : CELLS + COLS, :]

    def spread(base):
        return jnp.concatenate(
            [
                jnp.broadcast_to(
                    edge[(r % 8) * COLS + base + r // 8 : (r % 8) * COLS + base + r // 8 + 1, :],
                    (COLS, MODES),
                )
                for r in range(ROWS)
            ],
            axis=0,
        )

    col = lax.broadcasted_iota(jnp.int32, (CELLS, MODES), 0) & (COLS - 1)
    east = jnp.where(col == COLS - 1, spread(3), pltpu.roll(pressure, CELLS - 1, 0))
    west = jnp.where(col == 0, spread(0), pltpu.roll(pressure, 1, 0))
    scale = cell_metric[...]
    u_new[...] = u[...] - (scale * (east - west)).reshape(ROWS, COLS, MODES)
    slope = tall[2 * COLS : CELLS + 2 * COLS, :] - tall[0:CELLS, :]
    v_new[...] = v[...] - (scale * slope).reshape(ROWS, COLS, MODES)


def wind_stage(*operands):
    shape = jax.ShapeDtypeStruct((ROWS, COLS, MODES), f32)
    return pl.pallas_call(
        wind_kernel,
        name="wind_stage",
        out_shape=(shape, shape),
        in_specs=[VMEM] * 6,
        out_specs=(VMEM, VMEM),
        scratch_shapes=[
            pltpu.VMEM((CELLS + 2 * COLS, MODES), f32),
            pltpu.VMEM((128, MODES), f32),
        ],
    )(*operands)


def exchange(x, rows):
    x = x.reshape(PATCHES, rows, 128)
    x = lax.all_to_all(x, "lon", split_axis=0, concat_axis=0, tiled=True)
    return x.reshape(PATCHES * rows, 128)


def local(
    eastward_velocity,
    northward_velocity,
    thermal_anomaly,
    water_content,
    gridbox_factor,
    filter_threshold,
    layers_to_eigen,
    eigen_to_layers,
    eigen_screening_factor,
    chebyshev_sweeps,
    eigen_region_holder,
):
    table, wave, gain = filter_tables()
    table_high = np.asarray(table, np.float32).astype(bf16)
    table_low = (table - table_high.astype(np.float64)).astype(np.float32).astype(bf16)
    table_high, table_low = jnp.asarray(table_high), jnp.asarray(table_low)
    wave, gain = jnp.asarray(wave, f32), jnp.asarray(gain, f32)
    packed, params, hosted, cell_metric = patch_stage(
        eastward_velocity,
        northward_velocity,
        thermal_anomaly,
        water_content,
        gridbox_factor,
        eigen_region_holder.reshape(1, MODES),
        layers_to_eigen,
        eigen_screening_factor.reshape(1, MODES),
        chebyshev_sweeps.reshape(1, MODES),
    )
    band, south, north = band_stage(exchange(packed, 4 * SLOTS))
    size = lax.axis_size("lat")
    up = [(i, i + 1) for i in range(size - 1)]
    down = [(j, i) for i, j in up]
    from_south = lax.ppermute(north, "lat", up)
    from_north = lax.ppermute(south, "lat", down)
    solver = (
        band, south, north, from_south, from_north, params, gridbox_factor,
        filter_threshold.reshape(LAT // 128, 128), wave, gain, table_high, table_low,
    )
    returned, own_modes = host_stage(*solver)
    returned = exchange(returned, 4 * HOST)
    mode_solution, expand_high, expand_low = rest_stage(
        *solver, own_modes, hosted, eigen_to_layers
    )
    u_new, v_new = wind_stage(
        returned, expand_high, expand_low, cell_metric, eastward_velocity, northward_velocity
    )
    return u_new, v_new, mode_solution


def solution(mesh):
    return jax.shard_map(
        local,
        mesh=mesh,
        in_specs=(P("lat", "lon", None),) * 4 + (P(),) * 7,
        out_specs=(P("lat", "lon", None), P("lat", "lon", None), P("lon", "lat", None)),
        check_vma=False,
    )
```

time: 202 us -> 101 us (0.50); the launches traced: 198 us -> 101 us
  starting transfers between devices: 83.3 us -> 10.9 us
  Pallas kernels: 0 us -> 27.6 us
  other arithmetic: 21.3 us -> 0 us
  local copies, waits for them, and re-layouts: 20.9 us -> 1.39 us
  blocking collectives: 28.4 us -> 47.4 us
  waiting for transfers between devices: 30.7 us -> 12.7 us
  matrix products: 12.4 us -> 0 us
    ppermute x18 -> x2, starting transfers between devices: 48.2 us -> 4.31 us  [the longest x1 2.41 us: local(): from_south = lax.ppermute(north, 'lat', up)]
    all_to_all x2 -> x1, starting transfers between devices: 35.1 us -> 6.59 us  [exchange(): x = lax.all_to_all(x, 'lon', split_axis=0, concat_axis=0, tiled=True)]
    pallas_call x0 -> x5, Pallas kernels: none -> 27.6 us  [the longest x1 7.55 us: rest_stage(): pl.pallas_call(rest_kernel, name='rest_stage', out_shape=(jax.ShapeDtypeS...]
    all_to_all x1, blocking collectives: 28.4 us -> 47.4 us  [exchange(): x = lax.all_to_all(x, 'lon', split_axis=0, concat_axis=0, tiled=True)]
    ppermute x18 -> x2, waiting for transfers between devices: 17.8 us -> 4.78 us  [the longest x1 3.71 us: local(): from_south = lax.ppermute(north, 'lat', up)]
    dot_general x9 -> x0, matrix products: 12.4 us -> none  [the longest x1 4.55 us: polar_filter(): jnp.einsum('irk,nk->irn', spectrum * weights[None], fourier, precision=hi...]
    sin x1 -> x0, other arithmetic: 9.01 us -> none  [fourier_table(): return jnp.concatenate([jnp.cos(angles), jnp.sin(angles)], axis=1)]
    reshape x3 -> x0, local copies, waits for them, and re-layouts: 8.55 us -> none  [the longest x1 4.98 us: local(): band_rhs = mode_data.reshape(lon_count, item_count, lat_rows, lon_cols).t...]
  transfers between devices with their start and end apart: 20 -> 3, of which waited for: 11 -> 3; matrix products, arithmetic and copies ran while one was open for 11% -> 0% of each run, Pallas kernels for 0% -> 7%
where the time goes in v1:
time: 101 us
  blocking collectives  47.4 us (47%)
  Pallas kernels  27.6 us (27%)
  waiting for transfers between devices  12.7 us (13%)
  starting transfers between devices  10.9 us (11%)
  local copies, waits for them, and re-layouts  1.39 us (1%)
    all_to_all x1, blocking collectives, exchange(): x = lax.all_to_all(x, 'lon', split_axis=0, concat_axis=0, tiled=True)  47.4 us
    all_to_all x1, waiting for transfers between devices, exchange(): x = lax.all_to_all(x, 'lon', split_axis=0, concat_axis=0, tiled=True)  7.96 us
    pallas_call x1, Pallas kernels, rest_stage(): pl.pallas_call(rest_kernel, name='rest_stage', out_shape=(jax.ShapeDtypeS...  7.55 us
    pallas_call x1, Pallas kernels, band_stage(): pl.pallas_call(band_kernel, name='band_stage', out_shape=(jax.ShapeDtypeS...  7.22 us
    all_to_all x1, starting transfers between devices, exchange(): x = lax.all_to_all(x, 'lon', split_axis=0, concat_axis=0, tiled=True)  6.59 us
    pallas_call x1, Pallas kernels, host_stage(): pl.pallas_call(host_kernel, name='host_stage', out_shape=(jax.ShapeDtypeS...  6.51 us
    pallas_call x1, Pallas kernels, patch_stage(): pl.pallas_call(patch_kernel, name='patch_stage', out_shape=(jax.ShapeDtyp...  4.02 us
    ppermute x1, waiting for transfers between devices, local(): from_south = lax.ppermute(north, 'lat', up)  3.71 us
  transfers between devices with their start and end apart: 3, of which 3 were waited for; matrix products, arithmetic and copies ran while one was open for 0% of the time, Pallas kernels for 7%

profile of v1, /device:TPU:6, one launch (start us, length us, event | category | flops | bytes accessed | tf_op | source)
XLA Modules:
  0.0 100.8 jit_solution(473693424996866182)
XLA Ops:
  0.6 4.0 %patch_stage.1 = (f32[1536,128]{1,0:T(8,128)}, f32[3,8,128]{2,1,0:T(8,128)}, bf16[128,128]{1,0:T(8,128)(2,1)}, f32[384,128]{1,0:T(8,128)}) custom-call(f32[24,16,128]{2,1,0:T(8,128)} %u.3, f32[24,16,128]{2,1,0:T(8,128)} %v.3, f32[24,16,128]{2,1,0:T(8,128)} %t.1, f32[24,16,128]{2,1,0:T(8,128)} %q.1, f32[384,1024]{1,0:T(8,128)} %metric.5, s32[1,128]{1,0:T(1,128)} %bitcast.14, ...), custom_call_target="tpu_custom_call" | custom-call | tf_op jit(solution)/shard_map/patch_stage/pallas_call | solution.py:237
  4.7 47.4 %all_to_all.10 = f32[64,24,128]{2,1,0:T(8,128)} all-to-all(f32[64,24,128]{2,1,0:T(8,128)} %bitcast.10), channel_id=1, replica_groups=mesh['lat'=16,'lon'=64] {'lon'}, dimensions={0} | all-to-all | bytes 1572864 | tf_op jit(solution)/shard_map/all_to_all | solution.py:585
  52.1 7.2 %band_stage.1 = (f32[6,24,1024]{2,1,0:T(8,128)}, f32[6,8,1024]{2,1,0:T(8,128)}, f32[6,8,1024]{2,1,0:T(8,128)}) custom-call(f32[1536,128]{1,0:T(8,128)} %bitcast.8), custom_call_target="tpu_custom_call" | custom-call | tf_op jit(solution)/shard_map/band_stage/pallas_call | solution.py:291
  59.3 1.9 %collective-permute-start.1 = (f32[6,8,1024]{2,1,0:T(8,128)}, f32[6,8,1024]{2,1,0:T(8,128)S(1)}, u32[]{:S(2)}, u32[]{:S(2)}) collective-permute-start(f32[6,8,1024]{2,1,0:T(8,128)} %get-tuple-element.19.south), channel_id=1, source_target_pairs={{64,0},{128,64},{192,128},{256,192},{320,256},{384,320},{448,384},... | collective-permute-start | bytes 589832 | tf_op jit(solution)/shard_map/ppermute | solution.py:623
  61.2 2.4 %collective-permute-start = (f32[6,8,1024]{2,1,0:T(8,128)}, f32[6,8,1024]{2,1,0:T(8,128)S(1)}, u32[]{:S(2)}, u32[]{:S(2)}) collective-permute-start(f32[6,8,1024]{2,1,0:T(8,128)} %get-tuple-element.20.north), channel_id=1, source_target_pairs={{0,64},{64,128},{128,192},{192,256},{256,320},{320,384},{384,448},... | collective-permute-start | bytes 589832 | tf_op jit(solution)/shard_map/ppermute | solution.py:622
  63.7 1.1 %collective-permute-done.1.from_north = f32[6,8,1024]{2,1,0:T(8,128)S(1)} collective-permute-done((f32[6,8,1024]{2,1,0:T(8,128)}, f32[6,8,1024]{2,1,0:T(8,128)S(1)}, u32[]{:S(2)}, u32[]{:S(2)}) %collective-permute-start.1) | collective-permute-done | bytes 196640 | tf_op jit(solution)/shard_map/ppermute | solution.py:623
  64.7 0.0 copy-start.1
  64.7 3.7 %collective-permute-done.from_south = f32[6,8,1024]{2,1,0:T(8,128)S(1)} collective-permute-done((f32[6,8,1024]{2,1,0:T(8,128)}, f32[6,8,1024]{2,1,0:T(8,128)S(1)}, u32[]{:S(2)}, u32[]{:S(2)}) %collective-permute-start) | collective-permute-done | bytes 196640 | tf_op jit(solution)/shard_map/ppermute | solution.py:622
  68.4 0.0 copy-start.2
  68.4 0.0 copy-done.1
  68.4 0.7 copy-done.2
  69.1 6.5 %host_stage.1 = (f32[512,128]{1,0:T(8,128)}, f32[2,24,1024]{2,1,0:T(8,128)}) custom-call(f32[6,24,1024]{2,1,0:T(8,128)} %get-tuple-element.18.band, f32[6,8,1024]{2,1,0:T(8,128)} %get-tuple-element.19.south, f32[6,8,1024]{2,1,0:T(8,128)} %get-tuple-element.20.north, f32[6,8,1024]{2,1,0:T(8,128)} %copy-done.2, f32[6,8,1024]{2,1,0:T(8,128)} %copy-done.1, ...), custom_call_target="tpu_custom_call" | custom-call | tf_op jit(solution)/shard_map/host_stage/pallas_call | solution.py:471
  75.6 6.6 %all-to-all-start.1 = ((f32[64,8,128]{2,1,0:T(8,128)}), f32[64,8,128]{2,1,0:T(8,128)S(1)}, u32[]{:S(2)}, u32[]{:S(2)}) async-start(f32[64,8,128]{2,1,0:T(8,128)} %bitcast.11), calls=%async_computation.1 | async-start | bytes 524288 | tf_op jit(solution)/shard_map/all_to_all | solution.py:585
  82.2 7.6 %rest_stage.1 = (f32[6,24,1024]{2,1,0:T(8,128)}, bf16[128,128]{1,0:T(8,128)(2,1)}, bf16[128,128]{1,0:T(8,128)(2,1)}) custom-call(f32[6,24,1024]{2,1,0:T(8,128)} %get-tuple-element.18.band, f32[6,8,1024]{2,1,0:T(8,128)} %get-tuple-element.19.south, f32[6,8,1024]{2,1,0:T(8,128)} %get-tuple-element.20.north, f32[6,8,1024]{2,1,0:T(8,128)} %copy-done.2, ...), custom_call_target="tpu_custom_call" | custom-call | tf_op jit(solution)/shard_map/rest_stage/pallas_call | solution.py:515
  89.8 8.0 %all-to-all-done.1 = f32[64,8,128]{2,1,0:T(8,128)S(1)} async-done(((f32[64,8,128]{2,1,0:T(8,128)}), f32[64,8,128]{2,1,0:T(8,128)S(1)}, u32[]{:S(2)}, u32[]{:S(2)}) %all-to-all-start.1) | async-done | bytes 262176 | tf_op jit(solution)/shard_map/all_to_all | solution.py:585
  97.8 0.0 copy-start
  97.8 0.7 copy-done
  98.5 2.3 %wind_stage.1 = (f32[24,16,128]{2,1,0:T(8,128)}, f32[24,16,128]{2,1,0:T(8,128)}) custom-call(f32[512,128]{1,0:T(8,128)} %bitcast.9, bf16[128,128]{1,0:T(8,128)(2,1)} %get-tuple-element.25.expand_high, bf16[128,128]{1,0:T(8,128)(2,1)} %get-tuple-element.26.expand_low, f32[384,128]{1,0:T(8,128)} %get-tuple-element.27.cell_metric, f32[24,16,128]{2,1,0:T(8,128)} %u.3, ...), custom_call_target="tpu_custom_call" | custom-call | tf_op jit(solution)/shard_map/wind_stage/pallas_call | solution.py:570
Async XLA Ops:
  59.3 5.4 %collective-permute-start.1 = (f32[6,8,1024]{2,1,0:T(8,128)}, f32[6,8,1024]{2,1,0:T(8,128)S(1)}, u32[]{:S(2)}, u32[]{:S(2)}) collective-permute-start(f32[6,8,1024]{2,1,0:T(8,128)} %get-tuple-element.19.south), channel_id=1, source_target_pairs={{64,0},{128,64},{192,128},{256,192},{320,256},{384,320},{448,384},... | collective-permute-start | bytes 589832 | tf_op jit(solution)/shard_map/ppermute | solution.py:623
  61.2 7.2 %collective-permute-start = (f32[6,8,1024]{2,1,0:T(8,128)}, f32[6,8,1024]{2,1,0:T(8,128)S(1)}, u32[]{:S(2)}, u32[]{:S(2)}) collective-permute-start(f32[6,8,1024]{2,1,0:T(8,128)} %get-tuple-element.20.north), channel_id=1, source_target_pairs={{0,64},{64,128},{128,192},{192,256},{256,320},{320,384},{384,448},... | collective-permute-start | bytes 589832 | tf_op jit(solution)/shard_map/ppermute | solution.py:622
  64.7 3.7 %copy-start.1 = (f32[6,8,1024]{2,1,0:T(8,128)}, f32[6,8,1024]{2,1,0:T(8,128)S(1)}, u32[]{:S(2)}) copy-start(f32[6,8,1024]{2,1,0:T(8,128)S(1)} %collective-permute-done.1.from_north) | copy-start | bytes 589828
  68.4 0.7 copy-start.2
  75.6 22.1 %all-to-all-start.1 = ((f32[64,8,128]{2,1,0:T(8,128)}), f32[64,8,128]{2,1,0:T(8,128)S(1)}, u32[]{:S(2)}, u32[]{:S(2)}) async-start(f32[64,8,128]{2,1,0:T(8,128)} %bitcast.11), calls=%async_computation.1 | async-start | bytes 524288 | tf_op jit(solution)/shard_map/all_to_all | solution.py:585
  97.8 0.7 copy-start

commit v2 on v1

--- a/solution.py
+++ b/solution.py
@@ -9,6 +9,7 @@
 from jax.sharding import PartitionSpec as P
 
 MAXIT = 6
+MINIT = 3
 ROWS = 24
 COLS = 16
 CELLS = ROWS * COLS
@@ -23,8 +24,9 @@
 
 f32 = jnp.float32
 bf16 = jnp.bfloat16
+GRANT = pltpu.CompilerParams(vmem_limit_bytes=24 << 20)
 VMEM = pl.BlockSpec(memory_space=pltpu.VMEM)
-ANY = pl.BlockSpec(memory_space=pl.ANY)
+FAR = pl.BlockSpec(memory_space=pltpu.HBM)
 
 
 def filter_tables():
@@ -75,20 +77,26 @@
     return dot(ah, bh) + (dot(ah, bl) + dot(al, bh))
 
 
-def block_swap(x):
-    sub = lax.broadcasted_iota(jnp.int32, x.shape, 1)
+def turn_groups(x, sign):
     group = lax.broadcasted_iota(jnp.int32, x.shape, 2) // 16
     for d in (4, 2, 1):
-        here = sub & d
-        stay = here == (group & d)
-        up = pltpu.roll(pltpu.roll(x, d, 1), 128 - 16 * d, 2)
-        if d == 4:
-            moved = up
-        else:
-            down = pltpu.roll(pltpu.roll(x, 8 - d, 1), 16 * d, 2)
-            moved = jnp.where(here != 0, up, down)
-        x = jnp.where(stay, x, moved)
+        x = jnp.where((group & d) != 0, pltpu.roll(x, d if sign > 0 else 8 - d, 1), x)
     return x
+
+
+def gather_rows(x):
+    return pltpu.roll(turn_groups(x, -1), 0, 2, stride=COLS, stride_axis=1)
+
+
+def scatter_rows(x):
+    row = lax.broadcasted_iota(jnp.int32, x.shape, 1)
+    for d in (4, 2, 1):
+        x = jnp.where((row & d) != 0, pltpu.roll(x, 128 - COLS * d, 2), x)
+    return turn_groups(x, 1)
+
+
+def aligned(x):
+    return pl.multiple_of(x, COLS)
 
 
 def load_metric(metric, ext, sem, lat):
@@ -148,13 +156,17 @@
 
 
 def patch_kernel(
-    u, v, t, q, metric, holder, project, depth, sweeps,
-    packed, params, hosted, cell_metric,
-    ext, own, field, chosen, sem,
+    u_far, v_far, t_far, q_far, metric, holder, project, depth, sweeps,
+    packed, params, hosted, cell_metric, ext,
+    u, v, t, q, own, field, edges, chosen, sem, field_sem,
 ):
     lat = lax.axis_index("lat")
     lon = lax.axis_index("lon")
-    copies = load_metric(metric, ext, sem, lat)
+    metric_copies = load_metric(metric, ext, sem, lat)
+    fields = ((u_far, u), (v_far, v), (t_far, t), (q_far, q))
+    copies = metric_copies + [
+        pltpu.make_async_copy(far, here, field_sem.at[i]) for i, (far, here) in enumerate(fields)
+    ]
     for c in copies:
         c.start()
     select = selection(holder[...])
@@ -173,12 +185,13 @@
     proj_high, proj_low = split_value(project[...])
     rows_high = jnp.dot(sel, proj_high, preferred_element_type=f32).astype(bf16)
     rows_low = jnp.dot(sel, proj_low, preferred_element_type=f32).astype(bf16)
-    for c in copies:
+    for c in metric_copies:
         c.wait()
     mask_metric(ext, lat)
 
     block = lon // 8
-    offset = (lon % 8) * COLS
+    turn = lon % 8
+    offset = turn * COLS
 
     def lanes(b):
         return ext[:, pl.ds(pl.multiple_of(b * 128, 128), 128)]
@@ -189,6 +202,10 @@
     east_block = jnp.where(offset == 128 - COLS, (block + 1) % BLOCKS, block)
     west_metric = pltpu.roll(lanes(west_block), (129 - offset) % 128, 1)[8:32, 0:1]
     east_metric = pltpu.roll(lanes(east_block), (256 - COLS - offset) % 128, 1)[8:32, 0:1]
+    scale = jnp.concatenate([cell_column(own[8 + r : 9 + r, :]) for r in range(ROWS)], axis=0)
+    cell_metric[...] = 0.25 * scale
+    for c in copies[len(metric_copies) :]:
+        c.wait()
 
     uu = u[...].reshape(CELLS, MODES)
     vv = v[...].reshape(CELLS, MODES)
@@ -204,11 +221,12 @@
     zero = jnp.zeros((COLS, MODES), f32)
     around = around + jnp.concatenate([to_south[COLS:], zero], axis=0)
     around = around + jnp.concatenate([zero, to_north[: CELLS - COLS]], axis=0)
-    scale = jnp.concatenate([cell_column(own[8 + r : 9 + r, :]) for r in range(ROWS)], axis=0)
-    cell_metric[...] = 0.25 * scale
-    field[0:CELLS, :] = virtual + scale * (around - 0.5 * virtual)
-
-    field[CELLS:, :] = jnp.zeros((128, MODES), f32)
+    forcing = virtual + scale * (around - 0.5 * virtual)
+    for r in range(ROWS):
+        at = aligned(r // 8 * 128 + COLS * ((turn - r) & 7))
+        field[pl.ds(at, COLS), :] = forcing[r * COLS : (r + 1) * COLS]
+
+    edges[...] = jnp.zeros((128, MODES), f32)
     first = t[:, 0, :] * (1.0 + 0.61 * q[:, 0, :])
     last = t[:, COLS - 1, :] * (1.0 + 0.61 * q[:, COLS - 1, :])
     edge_west = jnp.broadcast_to(west_metric, (ROWS, MODES)) * (0.125 * first - 0.25 * u[:, 0, :])
@@ -216,14 +234,15 @@
         0.125 * last + 0.25 * u[:, COLS - 1, :]
     )
     for rg in range(3):
-        field[pl.ds(CELLS + rg, 8, stride=COLS), :] = edge_west[8 * rg : 8 * rg + 8]
-        field[pl.ds(CELLS + 3 + rg, 8, stride=COLS), :] = edge_east[8 * rg : 8 * rg + 8]
+        edges[pl.ds(rg, 8, stride=COLS), :] = edge_west[8 * rg : 8 * rg + 8]
+        edges[pl.ds(3 + rg, 8, stride=COLS), :] = edge_east[8 * rg : 8 * rg + 8]
     edge_south = cell_column(own[7:8, :]) * to_south[0:COLS]
     edge_north = cell_column(own[32:33, :]) * to_north[CELLS - COLS :]
-    field[CELLS + 6 : CELLS + 16, :] = edge_north[0:10]
-    field[CELLS + 22 : CELLS + 28, :] = edge_north[10:16]
-    field[CELLS + 118 : CELLS + 128, :] = edge_south[0:10]
-    field[CELLS + 102 : CELLS + 108, :] = edge_south[10:16]
+    edges[8:16, :] = edge_north[0:8]
+    edges[24:32, :] = edge_north[8:16]
+    edges[104:112, :] = edge_south[0:8]
+    edges[120:128, :] = edge_south[8:16]
+    order_edges(edges, turn, field, CELLS)
 
     value = dot3((rows_high, rows_low), split_value(field[...]), ((1,), (1,)))
     for s in range(SLOTS):
@@ -233,31 +252,46 @@
             ]
 
 
+def order_edges(source, turn, target, base):
+    sub = lax.broadcasted_iota(jnp.int32, (COLS, MODES), 0)
+    for g in range(8):
+        west = source[pl.ds(aligned(COLS * ((turn - 1 - g) & 7)), COLS), :]
+        east = source[pl.ds(aligned(COLS * ((turn + 1 - g) & 7)), COLS), :]
+        rim = source[pl.ds(aligned(COLS * ((turn - g) & 7)), COLS), :]
+        target[base + COLS * g : base + COLS * g + COLS, :] = jnp.where(
+            sub < 3, west, jnp.where(sub < 6, east, rim)
+        )
+
+
 def patch_stage(u, v, t, q, metric, holder, project, depth, sweeps):
     return pl.pallas_call(
         patch_kernel,
         name="patch_stage",
+
         out_shape=(
-            jax.ShapeDtypeStruct((PATCHES * SLOTS * 4, 128), f32),
-            jax.ShapeDtypeStruct((3, 8, 128), f32),
-            jax.ShapeDtypeStruct((HOST * PATCHES, MODES), bf16),
-            jax.ShapeDtypeStruct((CELLS, MODES), f32),
+            pltpu.VMEM((PATCHES * SLOTS * 4, 128), f32),
+            pltpu.VMEM((3, 8, 128), f32),
+            pltpu.VMEM((HOST * PATCHES, MODES), bf16),
+            pltpu.VMEM((CELLS, MODES), f32),
+            pltpu.VMEM((EXT, LON), f32),
         ),
-        in_specs=[VMEM, VMEM, VMEM, VMEM, ANY, VMEM, VMEM, VMEM, VMEM],
-        out_specs=(VMEM, VMEM, VMEM, VMEM),
-        scratch_shapes=[
-            pltpu.VMEM((EXT, LON), f32),
+        in_specs=[FAR] * 5 + [VMEM] * 4,
+        out_specs=(VMEM,) * 5,
+        scratch_shapes=[pltpu.VMEM((ROWS, COLS, MODES), f32)] * 4
+        + [
             pltpu.VMEM((EXT, 128), f32),
             pltpu.VMEM((CELLS + 128, MODES), f32),
+            pltpu.VMEM((128, MODES), f32),
             pltpu.VMEM((SLOTS * PATCHES, MODES), f32),
             pltpu.SemaphoreType.DMA((3,)),
+            pltpu.SemaphoreType.DMA((4,)),
         ],
     )(u, v, t, q, metric, holder, project, depth, sweeps)
 
 
 def band_kernel(received, band, south, north):
-    lane = lax.broadcasted_iota(jnp.int32, (PATCHES, 128), 1)
-    place = lane & (COLS - 1)
+    place = lax.broadcasted_iota(jnp.int32, (PATCHES, 128), 1) & (COLS - 1)
+    near_half = (lax.broadcasted_iota(jnp.int32, (BLOCKS, 8, 128), 2) & (COLS - 1)) < 8
     row = lax.broadcasted_iota(jnp.int32, (8, 128), 0)
     for s in range(SLOTS):
         edge = received[pl.ds(s * 4 + 3, PATCHES, stride=4 * SLOTS), :]
@@ -268,33 +302,28 @@
             x = received[pl.ds(s * 4 + rg, PATCHES, stride=4 * SLOTS), :]
             x = x + jnp.where(place == COLS - 1, pltpu.roll(from_east, 15 - rg, 1), 0.0)
             x = x + jnp.where(place == 0, pltpu.roll(from_west, 128 - 3 - rg, 1), 0.0)
-            bands.append(block_swap(x.reshape(BLOCKS, 8, 128)))
-        rim = jnp.where(
-            lane < 10,
-            pltpu.roll(edge, 128 - 6, 1),
-            jnp.where(
-                lane < 16,
-                pltpu.roll(edge, 128 - 12, 1),
-                jnp.where(lane < 122, pltpu.roll(edge, 128 - 6, 1), pltpu.roll(edge, 20, 1)),
-            ),
-        )
-        rim = block_swap(rim.reshape(BLOCKS, 8, 128))
+            bands.append(gather_rows(x.reshape(BLOCKS, 8, 128)))
+        rim = gather_rows(edge.reshape(BLOCKS, 8, 128))
+        low = pltpu.roll(rim, 128 - 8, 2)
+        to_north = jnp.where(near_half, low, pltpu.roll(rim, 7, 1))
+        to_south = jnp.where(near_half, pltpu.roll(low, 1, 1), rim)
         for b in range(BLOCKS):
             at = slice(b * 128, (b + 1) * 128)
             for rg in range(3):
                 band[s, 8 * rg : 8 * rg + 8, at] = bands[rg][b]
-            south[s, :, at] = jnp.where(row == 7, rim[b], bands[0][b])
-            north[s, :, at] = jnp.where(row == 0, rim[b], bands[2][b])
+            south[s, :, at] = jnp.where(row == 7, to_south[b], bands[0][b])
+            north[s, :, at] = jnp.where(row == 0, to_north[b], bands[2][b])
 
 
 def band_stage(received):
     return pl.pallas_call(
         band_kernel,
         name="band_stage",
+
         out_shape=(
-            jax.ShapeDtypeStruct((SLOTS, ROWS, LON), f32),
-            jax.ShapeDtypeStruct((SLOTS, 8, LON), f32),
-            jax.ShapeDtypeStruct((SLOTS, 8, LON), f32),
+            pltpu.VMEM((SLOTS, ROWS, LON), f32),
+            pltpu.VMEM((SLOTS, 8, LON), f32),
+            pltpu.VMEM((SLOTS, 8, LON), f32),
         ),
         in_specs=[VMEM],
         out_specs=(VMEM, VMEM, VMEM),
@@ -302,9 +331,11 @@
 
 
 def solve_slots(
-    first, count, band, south, north, from_south, from_north, params, cutoff, wave, gain,
-    table_high, table_low, ext, spectral, solved, lat,
+    first, count, band, south, north, from_south, from_north, params, ext, fetches, constants,
+    spectral, solved,
 ):
+    cutoff, wave, gain, table_high, table_low, back_high, back_low = constants
+    lat = lax.axis_index("lat")
     row = lax.broadcasted_iota(jnp.int32, (8, LON), 0)
     for i in range(count):
         s = first + i
@@ -336,7 +367,10 @@
         residual = source
         total = jnp.zeros_like(source)
         for sweep in range(MAXIT):
-            total = total + wide(jnp.where(number > sweep, 1.0, 0.0)) * direction
+            if sweep < MINIT:
+                total = total + direction
+            else:
+                total = total + wide(jnp.where(number > sweep, 1.0, 0.0)) * direction
             if sweep + 1 < MAXIT:
                 around = (
                     pltpu.roll(direction, LON - 1, 1)
@@ -368,6 +402,8 @@
         spectral[3, at, 0:128] = d04 - lean
         spectral[3, at, 128:256] = d26 - turn
 
+    for c in fetches:
+        c.wait()
     index = lax.broadcasted_iota(jnp.int32, (EXT, 128), 0) + (lat * ROWS - 8)
     lane = lax.broadcasted_iota(jnp.int32, (EXT, 128), 1)
     limit = jnp.zeros((EXT, 1), f32)
@@ -387,9 +423,8 @@
         damping = jnp.broadcast_to(gain[k : k + 1, :], (EXT, 256)) / (1.0 + ratio * ratio)
         damping = jnp.concatenate([damping] * count, axis=0)
         spectrum = dot3(split_value(spectral[k, 0 : count * EXT, :]), table, ((1,), (0,)))
-        spectral[k, 0 : count * EXT, :] = dot3(
-            split_value(spectrum * damping), table, ((1,), (1,))
-        )
+        back = (back_high[k], back_low[k])
+        spectral[k, 0 : count * EXT, :] = dot3(split_value(spectrum * damping), back, ((1,), (0,)))
     root = math.sqrt(0.5)
     y0 = spectral[0, 0 : count * EXT, 0:128]
     y4 = spectral[0, 0 : count * EXT, 128:256]
@@ -414,56 +449,72 @@
             solved[i, :, 128 * a : 128 * a + 128] = parts[a][i * EXT : (i + 1) * EXT]
 
 
+def fetch_all(far, here, sem):
+    fetches = [
+        pltpu.make_async_copy(source, target, sem.at[i])
+        for i, (source, target) in enumerate(zip(far, here))
+    ]
+    for c in fetches:
+        c.start()
+    return fetches
+
+
 def host_kernel(
-    band, south, north, from_south, from_north, params, metric, cutoff, wave, gain,
-    table_high, table_low,
-    packed, own_modes,
-    ext, spectral, solved, sem,
+    band, south, north, from_south, from_north, params, ext,
+    *rest,
 ):
-    lat = lax.axis_index("lat")
-    copies = load_metric(metric, ext, sem, lat)
-    for c in copies:
-        c.start()
-    for c in copies:
-        c.wait()
-    mask_metric(ext, lat)
+    far_constants, (packed, own_modes, spectral, solved), (*constants, sem) = (
+        rest[:7], rest[7:11], rest[11:],
+    )
+    fetches = fetch_all(far_constants, constants, sem)
     solve_slots(
-        0, HOST, band, south, north, from_south, from_north, params, cutoff, wave, gain,
-        table_high, table_low, ext, spectral, solved, lat,
-    )
-    lane = lax.broadcasted_iota(jnp.int32, (PATCHES, 128), 1)
-    place = lane & (COLS - 1)
+        0, HOST, band, south, north, from_south, from_north, params, ext, fetches, constants,
+        spectral, solved,
+    )
+    place = lax.broadcasted_iota(jnp.int32, (PATCHES, 128), 1) & (COLS - 1)
+    row = lax.broadcasted_iota(jnp.int32, (BLOCKS, 8, 128), 1)
     for i in range(HOST):
         owned = jnp.broadcast_to(params[2, i : i + 1, 0:1], (ROWS, LON))
         own_modes[i] = solved[i, 8:32, :] * owned
-        tiles = []
-        for tile in range(5):
-            x = jnp.stack(
-                [solved[i, 8 * tile : 8 * tile + 8, 128 * b : 128 * b + 128] for b in range(BLOCKS)]
+
+        def tile(k):
+            return jnp.stack(
+                [solved[i, 8 * k : 8 * k + 8, 128 * b : 128 * b + 128] for b in range(BLOCKS)]
             )
-            tiles.append(block_swap(x).reshape(PATCHES, 128))
-        edge = jnp.zeros((PATCHES, 128), f32)
+
+        far, close = tile(4), tile(0)
+        rim = jnp.where(
+            row == 0,
+            pltpu.roll(far, 8, 2),
+            jnp.where(
+                row == 1,
+                pltpu.roll(far, 1, 1),
+                jnp.where(row == 6, pltpu.roll(pltpu.roll(close, 7, 1), 8, 2), close),
+            ),
+        )
+        edge = scatter_rows(rim).reshape(PATCHES, 128)
         for rg in range(3):
-            x = tiles[rg + 1]
+            x = scatter_rows(tile(rg + 1)).reshape(PATCHES, 128)
             packed[pl.ds(i * 4 + rg, PATCHES, stride=4 * HOST), :] = x
             west = pltpu.roll(pltpu.roll(x, 1, 0), 128 - 15 + rg, 1)
             east = pltpu.roll(pltpu.roll(x, PATCHES - 1, 0), 3 + rg, 1)
             edge = jnp.where(place == rg, west, edge)
             edge = jnp.where(place == 3 + rg, east, edge)
-        far, near = tiles[4], tiles[0]
-        edge = jnp.where((lane >= 6) & (lane < 16), pltpu.roll(far, 6, 1), edge)
-        edge = jnp.where((lane >= 22) & (lane < 28), pltpu.roll(far, 12, 1), edge)
-        edge = jnp.where(lane >= 118, pltpu.roll(near, 6, 1), edge)
-        edge = jnp.where((lane >= 102) & (lane < 108), pltpu.roll(near, 108, 1), edge)
         packed[pl.ds(i * 4 + 3, PATCHES, stride=4 * HOST), :] = edge
 
 
 def solver_scratch(count):
     return [
-        pltpu.VMEM((EXT, LON), f32),
         pltpu.VMEM((4, count * EXT, 256), f32),
         pltpu.VMEM((count, EXT, LON), f32),
-        pltpu.SemaphoreType.DMA((3,)),
+        pltpu.VMEM((LAT // 128, 128), f32),
+        pltpu.VMEM((4, 256), f32),
+        pltpu.VMEM((4, 256), f32),
+        pltpu.VMEM((4, 256, 256), bf16),
+        pltpu.VMEM((4, 256, 256), bf16),
+        pltpu.VMEM((4, 256, 256), bf16),
+        pltpu.VMEM((4, 256, 256), bf16),
+        pltpu.SemaphoreType.DMA((7,)),
     ]
 
 
@@ -471,29 +522,25 @@
     return pl.pallas_call(
         host_kernel,
         name="host_stage",
+
         out_shape=(
-            jax.ShapeDtypeStruct((PATCHES * HOST * 4, 128), f32),
-            jax.ShapeDtypeStruct((HOST, ROWS, LON), f32),
+            pltpu.VMEM((PATCHES * HOST * 4, 128), f32),
+            pltpu.VMEM((HOST, ROWS, LON), f32),
         ),
-        in_specs=[VMEM] * 6 + [ANY] + [VMEM] * 5,
+        in_specs=[VMEM] * 7 + [FAR] * 7,
         out_specs=(VMEM, VMEM),
         scratch_shapes=solver_scratch(HOST),
     )(*operands)
 
 
 def rest_kernel(
-    band, south, north, from_south, from_north, params, metric, cutoff, wave, gain,
-    table_high, table_low, own_modes, hosted, expand,
-    modes, expand_high, expand_low,
-    ext, spectral, solved, sem,
+    band, south, north, from_south, from_north, params, ext,
+    *rest,
 ):
-    lat = lax.axis_index("lat")
-    copies = load_metric(metric, ext, sem, lat)
-    for c in copies:
-        c.start()
-    for c in copies:
-        c.wait()
-    mask_metric(ext, lat)
+    far_constants, rest = rest[:7], rest[7:]
+    own_modes, hosted, expand, modes, expand_high, expand_low, spectral, solved = rest[:8]
+    *constants, sem = rest[8:]
+    fetches = fetch_all(far_constants, constants, sem)
     high, low = split_value(expand[...])
     dims = (((1,), (1,)), ((), ()))
     expand_high[...] = lax.dot_general(
@@ -504,8 +551,8 @@
     ).astype(bf16)
     modes[0:HOST] = own_modes[...]
     solve_slots(
-        HOST, SLOTS - HOST, band, south, north, from_south, from_north, params, cutoff, wave, gain,
-        table_high, table_low, ext, spectral, solved, lat,
+        HOST, SLOTS - HOST, band, south, north, from_south, from_north, params, ext, fetches,
+        constants, spectral, solved,
     )
     for i in range(SLOTS - HOST):
         modes[HOST + i] = solved[i, 8:32, :]
@@ -515,18 +562,24 @@
     return pl.pallas_call(
         rest_kernel,
         name="rest_stage",
+
         out_shape=(
             jax.ShapeDtypeStruct((SLOTS, ROWS, LON), f32),
-            jax.ShapeDtypeStruct((MODES, MODES), bf16),
-            jax.ShapeDtypeStruct((MODES, MODES), bf16),
+            pltpu.VMEM((MODES, MODES), bf16),
+            pltpu.VMEM((MODES, MODES), bf16),
         ),
-        in_specs=[VMEM] * 6 + [ANY] + [VMEM] * 8,
+        in_specs=[VMEM] * 7 + [FAR] * 7 + [VMEM] * 3,
         out_specs=(VMEM, VMEM, VMEM),
         scratch_shapes=solver_scratch(SLOTS - HOST),
     )(*operands)
 
 
-def wind_kernel(received, expand_high, expand_low, cell_metric, u, v, u_new, v_new, tall, edge):
+def wind_kernel(
+    received, expand_high, expand_low, cell_metric, u_far, v_far, u_new, v_new,
+    tall, edges, edge, u, v, sem,
+):
+    fetches = fetch_all((u_far, v_far), (u, v), sem)
+    turn = lax.axis_index("lon") % 8
     table = (expand_high[...], expand_low[...])
     for part in range(4):
         x = jnp.concatenate(
@@ -535,13 +588,16 @@
         )
         value = dot3(split_value(x.T), table, ((1,), (0,)))
         if part < 3:
-            tall[COLS + part * 128 : COLS + part * 128 + 128, :] = value
+            for g in range(8):
+                at = aligned(COLS + part * 128 + COLS * ((turn - g) & 7))
+                tall[pl.ds(at, COLS), :] = value[COLS * g : COLS * g + COLS]
         else:
-            edge[...] = value
-    tall[0:10, :] = edge[118:128, :]
-    tall[10:16, :] = edge[102:108, :]
-    tall[CELLS + COLS : CELLS + COLS + 10, :] = edge[6:16, :]
-    tall[CELLS + COLS + 10 : CELLS + 2 * COLS, :] = edge[22:28, :]
+            edges[...] = value
+    order_edges(edges, turn, edge, 0)
+    tall[0:8, :] = edge[104:112, :]
+    tall[8:16, :] = edge[120:128, :]
+    tall[CELLS + COLS : CELLS + COLS + 8, :] = edge[8:16, :]
+    tall[CELLS + COLS + 8 : CELLS + 2 * COLS, :] = edge[24:32, :]
     pressure = tall[COLS : CELLS + COLS, :]
 
     def spread(base):
@@ -560,6 +616,8 @@
     east = jnp.where(col == COLS - 1, spread(3), pltpu.roll(pressure, CELLS - 1, 0))
     west = jnp.where(col == 0, spread(0), pltpu.roll(pressure, 1, 0))
     scale = cell_metric[...]
+    for c in fetches:
+        c.wait()
     u_new[...] = u[...] - (scale * (east - west)).reshape(ROWS, COLS, MODES)
     slope = tall[2 * COLS : CELLS + 2 * COLS, :] - tall[0:CELLS, :]
     v_new[...] = v[...] - (scale * slope).reshape(ROWS, COLS, MODES)
@@ -570,14 +628,23 @@
     return pl.pallas_call(
         wind_kernel,
         name="wind_stage",
+
         out_shape=(shape, shape),
-        in_specs=[VMEM] * 6,
+        in_specs=[VMEM] * 4 + [FAR] * 2,
         out_specs=(VMEM, VMEM),
         scratch_shapes=[
             pltpu.VMEM((CELLS + 2 * COLS, MODES), f32),
             pltpu.VMEM((128, MODES), f32),
+            pltpu.VMEM((128, MODES), f32),
+            pltpu.VMEM((ROWS, COLS, MODES), f32),
+            pltpu.VMEM((ROWS, COLS, MODES), f32),
+            pltpu.SemaphoreType.DMA((2,)),
         ],
     )(*operands)
+
+
+def near(*arrays):
+    return tuple(pltpu.with_memory_space_constraint(x, pltpu.VMEM) for x in arrays)
 
 
 def exchange(x, rows):
@@ -600,11 +667,12 @@
     eigen_region_holder,
 ):
     table, wave, gain = filter_tables()
-    table_high = np.asarray(table, np.float32).astype(bf16)
-    table_low = (table - table_high.astype(np.float64)).astype(np.float32).astype(bf16)
-    table_high, table_low = jnp.asarray(table_high), jnp.asarray(table_low)
-    wave, gain = jnp.asarray(wave, f32), jnp.asarray(gain, f32)
-    packed, params, hosted, cell_metric = patch_stage(
+    tables = []
+    for x in (table, table.transpose(0, 2, 1)):
+        high = np.asarray(x, np.float32).astype(bf16)
+        tables += [high, (x - high.astype(np.float64)).astype(np.float32).astype(bf16)]
+    constants = [jnp.asarray(x) for x in [wave.astype(np.float32), gain.astype(np.float32)] + tables]
+    packed, params, hosted, cell_metric, ext = patch_stage(
         eastward_velocity,
         northward_velocity,
         thermal_anomaly,
@@ -615,23 +683,22 @@
         eigen_screening_factor.reshape(1, MODES),
         chebyshev_sweeps.reshape(1, MODES),
     )
-    band, south, north = band_stage(exchange(packed, 4 * SLOTS))
+    band, south, north = band_stage(*near(exchange(packed, 4 * SLOTS)))
     size = lax.axis_size("lat")
     up = [(i, i + 1) for i in range(size - 1)]
     down = [(j, i) for i, j in up]
     from_south = lax.ppermute(north, "lat", up)
     from_north = lax.ppermute(south, "lat", down)
-    solver = (
-        band, south, north, from_south, from_north, params, gridbox_factor,
-        filter_threshold.reshape(LAT // 128, 128), wave, gain, table_high, table_low,
+    solver = near(band, south, north, from_south, from_north, params, ext) + (
+        filter_threshold.reshape(LAT // 128, 128), *constants,
     )
     returned, own_modes = host_stage(*solver)
     returned = exchange(returned, 4 * HOST)
     mode_solution, expand_high, expand_low = rest_stage(
-        *solver, own_modes, hosted, eigen_to_layers
+        *solver, *near(own_modes, hosted), eigen_to_layers
     )
     u_new, v_new = wind_stage(
-        returned, expand_high, expand_low, cell_metric, eastward_velocity, northward_velocity
+        *near(returned, expand_high, expand_low, cell_metric), eastward_velocity, northward_velocity
     )
     return u_new, v_new, mode_solution
 

time: 101 us -> 91.3 us (0.904)
  Pallas kernels: 27.6 us -> 19.5 us
  local copies, waits for them, and re-layouts: 1.39 us -> 0 us
    pallas_call x3, Pallas kernels: 17.8 us -> 10.1 us  [the longest x1 5.17 us: host_stage(): pl.pallas_call(host_kernel, name='host_stage', out_shape=(pltpu.VMEM((PAT...]
    unnamed x6 -> x0, local copies, waits for them, and re-layouts: 1.39 us -> none
  transfers between devices with their start and end apart: 3 -> 3, of which waited for: 3 -> 3; matrix products, arithmetic and copies ran while one was open for 0% -> 0% of each run, Pallas kernels for 7% -> 8%
where the time goes in v2:
time: 91.3 us; the launch traced here: 90.8 us
  blocking collectives  47.1 us (52%)
  Pallas kernels  19.5 us (21%)
  waiting for transfers between devices  12.6 us (14%)
  starting transfers between devices  10.9 us (12%)
    all_to_all x1, blocking collectives, exchange(): x = lax.all_to_all(x, 'lon', split_axis=0, concat_axis=0, tiled=True)  47.1 us
    all_to_all x1, waiting for transfers between devices, exchange(): x = lax.all_to_all(x, 'lon', split_axis=0, concat_axis=0, tiled=True)  8.05 us
    pallas_call x1, Pallas kernels, rest_stage(): pl.pallas_call(rest_kernel, name='rest_stage', out_shape=(jax.ShapeDtypeS...  7.36 us
    all_to_all x1, starting transfers between devices, exchange(): x = lax.all_to_all(x, 'lon', split_axis=0, concat_axis=0, tiled=True)  6.59 us
    pallas_call x1, Pallas kernels, host_stage(): pl.pallas_call(host_kernel, name='host_stage', out_shape=(pltpu.VMEM((PAT...  5.17 us
    ppermute x1, waiting for transfers between devices, local(): from_south = lax.ppermute(north, 'lat', up)  3.82 us
    pallas_call x1, Pallas kernels, patch_stage(): pl.pallas_call(patch_kernel, name='patch_stage', out_shape=(pltpu.VMEM((P...  3.14 us
    ppermute x1, starting transfers between devices, local(): from_south = lax.ppermute(north, 'lat', up)  2.41 us
  transfers between devices with their start and end apart: 3, of which 3 were waited for; matrix products, arithmetic and copies ran while one was open for 0% of the time, Pallas kernels for 8%

profile of v2, /device:TPU:6, one launch (start us, length us, event | category | flops | bytes accessed | tf_op | source)
XLA Modules:
  0.0 90.8 jit_solution(14266662393816676136)
XLA Ops:
  0.6 3.1 %patch_stage.1 = (f32[1536,128]{1,0:T(8,128)S(1)}, f32[3,8,128]{2,1,0:T(8,128)S(1)}, bf16[128,128]{1,0:T(8,128)(2,1)S(1)}, f32[384,128]{1,0:T(8,128)S(1)}, f32[40,1024]{1,0:T(8,128)S(1)}) custom-call(f32[24,16,128]{2,1,0:T(8,128)} %u_far.3, f32[24,16,128]{2,1,0:T(8,128)} %v_far.3, f32[24,16,128]{2,1,0:T(8,128)} %t_far.1, f32[24,16,128]{2,1,0:T(8,128)} %q_far.1, ...), custom_call_target="tpu_custom_call" | custom-call | tf_op jit(solution)/shard_map/patch_stage/pallas_call | solution.py:267
  3.8 47.1 %all_to_all.10 = f32[64,24,128]{2,1,0:T(8,128)S(1)} all-to-all(f32[64,24,128]{2,1,0:T(8,128)S(1)} %bitcast.10), channel_id=1, replica_groups=mesh['lat'=16,'lon'=64] {'lon'}, dimensions={0} | all-to-all | bytes 1572864 | tf_op jit(solution)/shard_map/all_to_all | solution.py:652
  50.9 1.8 %band_stage.1 = (f32[6,24,1024]{2,1,0:T(8,128)S(1)}, f32[6,8,1024]{2,1,0:T(8,128)S(1)}, f32[6,8,1024]{2,1,0:T(8,128)S(1)}) custom-call(f32[1536,128]{1,0:T(8,128)S(1)} %bitcast.8), custom_call_target="tpu_custom_call" | custom-call | tf_op jit(solution)/shard_map/band_stage/pallas_call | solution.py:319
  52.7 1.9 %collective-permute-start.1 = (f32[6,8,1024]{2,1,0:T(8,128)S(1)}, f32[6,8,1024]{2,1,0:T(8,128)S(1)}, u32[]{:S(2)}, u32[]{:S(2)}) collective-permute-start(f32[6,8,1024]{2,1,0:T(8,128)S(1)} %get-tuple-element.20.south), channel_id=1, source_target_pairs={{64,0},{128,64},{192,128},{256,192},{320,256},{384,320},{448,384},... | collective-permute-start | bytes 589832 | tf_op jit(solution)/shard_map/ppermute | solution.py:691
  54.6 2.4 %collective-permute-start = (f32[6,8,1024]{2,1,0:T(8,128)S(1)}, f32[6,8,1024]{2,1,0:T(8,128)S(1)}, u32[]{:S(2)}, u32[]{:S(2)}) collective-permute-start(f32[6,8,1024]{2,1,0:T(8,128)S(1)} %get-tuple-element.21.north), channel_id=1, source_target_pairs={{0,64},{64,128},{128,192},{192,256},{256,320},{320,384},{384,448},... | collective-permute-start | bytes 589832 | tf_op jit(solution)/shard_map/ppermute | solution.py:690
  57.1 0.8 collective-permute-done.1.from_north
  57.8 3.8 %collective-permute-done.from_south = f32[6,8,1024]{2,1,0:T(8,128)S(1)} collective-permute-done((f32[6,8,1024]{2,1,0:T(8,128)S(1)}, f32[6,8,1024]{2,1,0:T(8,128)S(1)}, u32[]{:S(2)}, u32[]{:S(2)}) %collective-permute-start) | collective-permute-done | bytes 196640 | tf_op jit(solution)/shard_map/ppermute | solution.py:690
  61.6 5.2 %host_stage.1 = (f32[512,128]{1,0:T(8,128)}, f32[2,24,1024]{2,1,0:T(8,128)S(1)}) custom-call(f32[6,24,1024]{2,1,0:T(8,128)S(1)} %get-tuple-element.19.band, f32[6,8,1024]{2,1,0:T(8,128)S(1)} %get-tuple-element.20.south, f32[6,8,1024]{2,1,0:T(8,128)S(1)} %get-tuple-element.21.north, f32[6,8,1024]{2,1,0:T(8,128)S(1)} %collective-permute-done.from_south, ...), custom_call_target="tpu_custom_call" | custom-call | tf_op jit(solution)/shard_map/host_stage/pallas_call | solution.py:522
  66.8 6.6 %all-to-all-start.1 = ((f32[64,8,128]{2,1,0:T(8,128)}), f32[64,8,128]{2,1,0:T(8,128)S(1)}, u32[]{:S(2)}, u32[]{:S(2)}) async-start(f32[64,8,128]{2,1,0:T(8,128)} %bitcast.6), calls=%async_computation.1 | async-start | bytes 524288 | tf_op jit(solution)/shard_map/all_to_all | solution.py:652
  73.4 7.4 %rest_stage.1 = (f32[6,24,1024]{2,1,0:T(8,128)}, bf16[128,128]{1,0:T(8,128)(2,1)S(1)}, bf16[128,128]{1,0:T(8,128)(2,1)S(1)}) custom-call(f32[6,24,1024]{2,1,0:T(8,128)S(1)} %get-tuple-element.19.band, f32[6,8,1024]{2,1,0:T(8,128)S(1)} %get-tuple-element.20.south, f32[6,8,1024]{2,1,0:T(8,128)S(1)} %get-tuple-element.21.north, ...), custom_call_target="tpu_custom_call" | custom-call | tf_op jit(solution)/shard_map/rest_stage/pallas_call | solution.py:562
  80.8 8.1 %all-to-all-done.1 = f32[64,8,128]{2,1,0:T(8,128)S(1)} async-done(((f32[64,8,128]{2,1,0:T(8,128)}), f32[64,8,128]{2,1,0:T(8,128)S(1)}, u32[]{:S(2)}, u32[]{:S(2)}) %all-to-all-start.1) | async-done | bytes 262176 | tf_op jit(solution)/shard_map/all_to_all | solution.py:652
  88.8 2.0 %wind_stage.1 = (f32[24,16,128]{2,1,0:T(8,128)}, f32[24,16,128]{2,1,0:T(8,128)}) custom-call(f32[512,128]{1,0:T(8,128)S(1)} %bitcast.9, bf16[128,128]{1,0:T(8,128)(2,1)S(1)} %get-tuple-element.27.expand_high, bf16[128,128]{1,0:T(8,128)(2,1)S(1)} %get-tuple-element.28.expand_low, f32[384,128]{1,0:T(8,128)S(1)} %get-tuple-element.29.cell_metric, ...), custom_call_target="tpu_custom_call" | custom-call | tf_op jit(solution)/shard_map/wind_stage/pallas_call | solution.py:628
Async XLA Ops:
  52.7 5.1 %collective-permute-start.1 = (f32[6,8,1024]{2,1,0:T(8,128)S(1)}, f32[6,8,1024]{2,1,0:T(8,128)S(1)}, u32[]{:S(2)}, u32[]{:S(2)}) collective-permute-start(f32[6,8,1024]{2,1,0:T(8,128)S(1)} %get-tuple-element.20.south), channel_id=1, source_target_pairs={{64,0},{128,64},{192,128},{256,192},{320,256},{384,320},{448,384},... | collective-permute-start | bytes 589832 | tf_op jit(solution)/shard_map/ppermute | solution.py:691
  54.6 7.0 %collective-permute-start = (f32[6,8,1024]{2,1,0:T(8,128)S(1)}, f32[6,8,1024]{2,1,0:T(8,128)S(1)}, u32[]{:S(2)}, u32[]{:S(2)}) collective-permute-start(f32[6,8,1024]{2,1,0:T(8,128)S(1)} %get-tuple-element.21.north), channel_id=1, source_target_pairs={{0,64},{64,128},{128,192},{192,256},{256,320},{320,384},{384,448},... | collective-permute-start | bytes 589832 | tf_op jit(solution)/shard_map/ppermute | solution.py:690
  66.8 22.0 %all-to-all-start.1 = ((f32[64,8,128]{2,1,0:T(8,128)}), f32[64,8,128]{2,1,0:T(8,128)S(1)}, u32[]{:S(2)}, u32[]{:S(2)}) async-start(f32[64,8,128]{2,1,0:T(8,128)} %bitcast.6), calls=%async_computation.1 | async-start | bytes 524288 | tf_op jit(solution)/shard_map/all_to_all | solution.py:652

commit v3 on v2

--- a/solution.py
+++ b/solution.py
@@ -19,7 +19,9 @@
 PATCHES = 64
 SLOTS = 6
 HOST = 2
+REST = 4
 EXT = 40
+TALL = 32
 BLOCKS = LON // 128
 
 f32 = jnp.float32
@@ -289,6 +291,10 @@
     )(u, v, t, q, metric, holder, project, depth, sweeps)
 
 
+def spread_rows(row, block, count=8):
+    return pl.ds(row * BLOCKS + block, count, stride=BLOCKS)
+
+
 def band_kernel(received, band, south, north):
     place = lax.broadcasted_iota(jnp.int32, (PATCHES, 128), 1) & (COLS - 1)
     near_half = (lax.broadcasted_iota(jnp.int32, (BLOCKS, 8, 128), 2) & (COLS - 1)) < 8
@@ -308,11 +314,10 @@
         to_north = jnp.where(near_half, low, pltpu.roll(rim, 7, 1))
         to_south = jnp.where(near_half, pltpu.roll(low, 1, 1), rim)
         for b in range(BLOCKS):
-            at = slice(b * 128, (b + 1) * 128)
             for rg in range(3):
-                band[s, 8 * rg : 8 * rg + 8, at] = bands[rg][b]
-            south[s, :, at] = jnp.where(row == 7, to_south[b], bands[0][b])
-            north[s, :, at] = jnp.where(row == 0, to_north[b], bands[2][b])
+                band[spread_rows(s * ROWS + 8 * rg, b), :] = bands[rg][b]
+            south[spread_rows(s * 8, b), :] = jnp.where(row == 7, to_south[b], bands[0][b])
+            north[spread_rows(s * 8, b), :] = jnp.where(row == 0, to_north[b], bands[2][b])
 
 
 def band_stage(received):
@@ -321,9 +326,9 @@
         name="band_stage",
 
         out_shape=(
-            pltpu.VMEM((SLOTS, ROWS, LON), f32),
-            pltpu.VMEM((SLOTS, 8, LON), f32),
-            pltpu.VMEM((SLOTS, 8, LON), f32),
+            pltpu.VMEM((SLOTS * ROWS * BLOCKS, 128), f32),
+            pltpu.VMEM((SLOTS * 8 * BLOCKS, 128), f32),
+            pltpu.VMEM((SLOTS * 8 * BLOCKS, 128), f32),
         ),
         in_specs=[VMEM],
         out_specs=(VMEM, VMEM, VMEM),
@@ -331,12 +336,22 @@
 
 
 def solve_slots(
-    first, count, band, south, north, from_south, from_north, params, ext, fetches, constants,
-    spectral, solved,
+    first, count, edge, band, south, north, from_south, from_north, params, metric, damping,
+    fetches, constants, totals, spectral, solved,
 ):
-    cutoff, wave, gain, table_high, table_low, back_high, back_low = constants
-    lat = lax.axis_index("lat")
-    row = lax.broadcasted_iota(jnp.int32, (8, LON), 0)
+    table_high, table_low, back_high, back_low = constants
+    height = solved.shape[1]
+    reach = MAXIT - 1 + edge
+    out = ROWS + 2 * edge
+
+    def neighbours(x):
+        lane = lax.broadcasted_iota(jnp.int32, x.shape, 2)
+        east = pltpu.roll(x, 127, 2)
+        east = jnp.where(lane == 127, pltpu.roll(east, BLOCKS - 1, 1), east)
+        west = pltpu.roll(x, 1, 2)
+        west = jnp.where(lane == 0, pltpu.roll(west, 1, 1), west)
+        return east + west
+
     for i in range(count):
         s = first + i
         depth = params[0, s : s + 1, 0:1]
@@ -348,43 +363,54 @@
         ratio = 1.0 / relative
 
         def wide(x):
-            return jnp.broadcast_to(x, (EXT, LON))
-
-        below = from_south[s]
-        above = from_north[s]
-        source = jnp.concatenate(
+            return jnp.broadcast_to(x, (BLOCKS, 128))[None]
+
+
+        def rows_of(source, rows):
+            x = source[s * rows * BLOCKS : (s + 1) * rows * BLOCKS, :]
+            return x.reshape(rows, BLOCKS, 128)
+
+        below, above, mine = rows_of(from_south, 8), rows_of(from_north, 8), rows_of(band, ROWS)
+        residual = jnp.concatenate(
             [
-                below + jnp.where(row == 7, south[s], 0.0),
-                band[s, 0:8] + jnp.where(row == 0, below, 0.0),
-                band[s, 8:16],
-                band[s, 16:24] + jnp.where(row == 7, above, 0.0),
-                above + jnp.where(row == 0, north[s], 0.0),
+                below[8 - reach : 7],
+                below[7:8] + rows_of(south, 8)[7:8],
+                mine[0:1] + below[0:1],
+                mine[1:23],
+                mine[23:24] + above[7:8],
+                above[0:1] + rows_of(north, 8)[0:1],
+                above[1:reach],
             ],
             axis=0,
         )
-        coupling = wide(depth) * ext[...]
-        direction = source * wide(1.0 / centre)
-        residual = source
-        total = jnp.zeros_like(source)
-        for sweep in range(MAXIT):
+        height_now = ROWS + 2 * reach - 2
+        at = (8 - reach + 1) * BLOCKS
+        coupling = wide(depth) * metric[at : at + height_now * BLOCKS, :].reshape(
+            height_now, BLOCKS, 128
+        )
+        direction = residual * wide(1.0 / centre)
+        total = direction[MAXIT - 1 : MAXIT - 1 + out]
+        for sweep in range(1, MAXIT):
+            middle = direction[1:-1]
+            around = neighbours(middle) + (direction[2:] + direction[:-2])
+            residual = residual[1:-1] - middle + coupling * (around - 4.0 * middle)
+            coupling = coupling[1:-1]
+            after = 1.0 / (2.0 * relative - ratio)
+            direction = wide(after * ratio) * middle + wide(2.0 * after / radius) * residual
+            ratio = after
+            low = MAXIT - 1 - sweep
             if sweep < MINIT:
-                total = total + direction
+                total = total + direction[low : low + out]
             else:
-                total = total + wide(jnp.where(number > sweep, 1.0, 0.0)) * direction
-            if sweep + 1 < MAXIT:
-                around = (
-                    pltpu.roll(direction, LON - 1, 1)
-                    + pltpu.roll(direction, 1, 1)
-                    + pltpu.roll(direction, EXT - 1, 0)
-                    + pltpu.roll(direction, 1, 0)
-                )
-                residual = residual - direction + coupling * (around - 4.0 * direction)
-                after = 1.0 / (2.0 * relative - ratio)
-                direction = (
-                    wide(after * ratio) * direction + wide(2.0 * after / radius) * residual
-                )
-                ratio = after
-        x = [total[:, 128 * a : 128 * a + 128] for a in range(BLOCKS)]
+                active = wide(jnp.where(number > sweep, 1.0, 0.0))
+                total = total + active * direction[low : low + out]
+        at = i * height * BLOCKS
+        if edge:
+            parts = [total[1 : ROWS + 2], total[0:1]]
+            parts.append(jnp.zeros((height - ROWS - 2, BLOCKS, 128), f32))
+            total = jnp.concatenate(parts, axis=0)
+        totals[at : at + height * BLOCKS, :] = total.reshape(height * BLOCKS, 128)
+        x = [totals[spread_rows(i * height, a, height), :] for a in range(BLOCKS)]
         root = math.sqrt(0.5)
         s04, d04 = x[0] + x[4], x[0] - x[4]
         s26, d26 = x[2] + x[6], x[2] - x[6]
@@ -392,7 +418,7 @@
         s37, d37 = x[3] + x[7], x[3] - x[7]
         even, odd = s04 + s26, s15 + s37
         lean, turn = root * (d15 - d37), root * (d15 + d37)
-        at = slice(i * EXT, (i + 1) * EXT)
+        at = slice(i * height, (i + 1) * height)
         spectral[0, at, 0:128] = even + odd
         spectral[0, at, 128:256] = even - odd
         spectral[1, at, 0:128] = d04 + lean
@@ -404,33 +430,18 @@
 
     for c in fetches:
         c.wait()
-    index = lax.broadcasted_iota(jnp.int32, (EXT, 128), 0) + (lat * ROWS - 8)
-    lane = lax.broadcasted_iota(jnp.int32, (EXT, 128), 1)
-    limit = jnp.zeros((EXT, 1), f32)
-    for b in range(LAT // 128):
-        picked = jnp.where(
-            lane + 128 * b == index, jnp.broadcast_to(cutoff[b : b + 1, :], (EXT, 128)), 0.0
-        )
-        limit = limit + jnp.sum(picked, axis=1, keepdims=True)
-    limit = jnp.where(limit > 0.0, limit, 1.0)
-    inverse = 1.0 / (limit * (0.5 * LON))
     for k in range(4):
         table = (table_high[k], table_low[k])
-        ratio = jnp.broadcast_to(wave[k : k + 1, :], (EXT, 256)) * jnp.broadcast_to(
-            inverse, (EXT, 256)
-        )
-        ratio = ratio * ratio
-        damping = jnp.broadcast_to(gain[k : k + 1, :], (EXT, 256)) / (1.0 + ratio * ratio)
-        damping = jnp.concatenate([damping] * count, axis=0)
-        spectrum = dot3(split_value(spectral[k, 0 : count * EXT, :]), table, ((1,), (0,)))
+        weight = jnp.concatenate([damping[k, 0:height, :]] * count, axis=0)
+        spectrum = dot3(split_value(spectral[k, 0 : count * height, :]), table, ((1,), (0,)))
         back = (back_high[k], back_low[k])
-        spectral[k, 0 : count * EXT, :] = dot3(split_value(spectrum * damping), back, ((1,), (0,)))
+        spectral[k, 0 : count * height, :] = dot3(split_value(spectrum * weight), back, ((1,), (0,)))
     root = math.sqrt(0.5)
-    y0 = spectral[0, 0 : count * EXT, 0:128]
-    y4 = spectral[0, 0 : count * EXT, 128:256]
-    p1, q1 = spectral[1, 0 : count * EXT, 0:128], spectral[1, 0 : count * EXT, 128:256]
-    p2, q2 = spectral[2, 0 : count * EXT, 0:128], spectral[2, 0 : count * EXT, 128:256]
-    p3, q3 = spectral[3, 0 : count * EXT, 0:128], spectral[3, 0 : count * EXT, 128:256]
+    y0 = spectral[0, 0 : count * height, 0:128]
+    y4 = spectral[0, 0 : count * height, 128:256]
+    p1, q1 = spectral[1, 0 : count * height, 0:128], spectral[1, 0 : count * height, 128:256]
+    p2, q2 = spectral[2, 0 : count * height, 0:128], spectral[2, 0 : count * height, 128:256]
+    p3, q3 = spectral[3, 0 : count * height, 0:128], spectral[3, 0 : count * height, 128:256]
     even, odd = y0 + y4, y0 - y4
     a1, b1 = root * p1, root * q1
     a3, b3 = root * p3, root * q3
@@ -446,7 +457,44 @@
     parts[3], parts[7] = base + side, base - side
     for i in range(count):
         for a in range(BLOCKS):
-            solved[i, :, 128 * a : 128 * a + 128] = parts[a][i * EXT : (i + 1) * EXT]
+            solved[i, :, 128 * a : 128 * a + 128] = parts[a][i * height : (i + 1) * height]
+
+
+def damping_kernel(ext, cutoff, wave, gain, damping, metric):
+    for tile in range(EXT // 8):
+        for b in range(BLOCKS):
+            metric[spread_rows(8 * tile, b), :] = ext[
+                8 * tile : 8 * tile + 8, 128 * b : 128 * b + 128
+            ]
+    start = lax.axis_index("lat") * ROWS
+    sub = lax.broadcasted_iota(jnp.int32, (TALL, 128), 0)
+    index = jnp.where(sub == ROWS + 1, start - 1, start + sub)
+    lane = lax.broadcasted_iota(jnp.int32, (TALL, 128), 1)
+    limit = jnp.zeros((TALL, 1), f32)
+    for b in range(LAT // 128):
+        picked = jnp.where(
+            lane + 128 * b == index, jnp.broadcast_to(cutoff[b : b + 1, :], (TALL, 128)), 0.0
+        )
+        limit = limit + jnp.sum(picked, axis=1, keepdims=True)
+    limit = jnp.where(limit > 0.0, limit, 1.0)
+    inverse = jnp.broadcast_to(1.0 / (limit * (0.5 * LON)), (TALL, 256))
+    for k in range(4):
+        ratio = jnp.broadcast_to(wave[k : k + 1, :], (TALL, 256)) * inverse
+        ratio = ratio * ratio
+        damping[k] = jnp.broadcast_to(gain[k : k + 1, :], (TALL, 256)) / (1.0 + ratio * ratio)
+
+
+def damping_stage(*operands):
+    return pl.pallas_call(
+        damping_kernel,
+        name="damping_stage",
+        out_shape=(
+            pltpu.VMEM((4, TALL, 256), f32),
+            pltpu.VMEM((EXT * BLOCKS, 128), f32),
+        ),
+        in_specs=[VMEM] * 4,
+        out_specs=(VMEM, VMEM),
+    )(*operands)
 
 
 def fetch_all(far, here, sem):
@@ -460,41 +508,42 @@
 
 
 def host_kernel(
-    band, south, north, from_south, from_north, params, ext,
+    band, south, north, from_south, from_north, params, metric, damping,
     *rest,
 ):
-    far_constants, (packed, own_modes, spectral, solved), (*constants, sem) = (
-        rest[:7], rest[7:11], rest[11:],
+    far_constants, (packed, own_modes, totals, spectral, solved), (*constants, sem) = (
+        rest[:4], rest[4:9], rest[9:],
     )
     fetches = fetch_all(far_constants, constants, sem)
     solve_slots(
-        0, HOST, band, south, north, from_south, from_north, params, ext, fetches, constants,
-        spectral, solved,
+        0, HOST, 1, band, south, north, from_south, from_north, params, metric, damping, fetches,
+        constants, totals, spectral, solved,
     )
     place = lax.broadcasted_iota(jnp.int32, (PATCHES, 128), 1) & (COLS - 1)
     row = lax.broadcasted_iota(jnp.int32, (BLOCKS, 8, 128), 1)
     for i in range(HOST):
         owned = jnp.broadcast_to(params[2, i : i + 1, 0:1], (ROWS, LON))
-        own_modes[i] = solved[i, 8:32, :] * owned
+        own_modes[i] = solved[i, 0:ROWS, :] * owned
 
         def tile(k):
             return jnp.stack(
                 [solved[i, 8 * k : 8 * k + 8, 128 * b : 128 * b + 128] for b in range(BLOCKS)]
             )
 
-        far, close = tile(4), tile(0)
+        last = tile(3)
+        shifted = pltpu.roll(last, 8, 2)
         rim = jnp.where(
             row == 0,
-            pltpu.roll(far, 8, 2),
+            shifted,
             jnp.where(
                 row == 1,
-                pltpu.roll(far, 1, 1),
-                jnp.where(row == 6, pltpu.roll(pltpu.roll(close, 7, 1), 8, 2), close),
+                pltpu.roll(last, 1, 1),
+                jnp.where(row == 6, pltpu.roll(shifted, 5, 1), pltpu.roll(last, 6, 1)),
             ),
         )
         edge = scatter_rows(rim).reshape(PATCHES, 128)
         for rg in range(3):
-            x = scatter_rows(tile(rg + 1)).reshape(PATCHES, 128)
+            x = scatter_rows(tile(rg)).reshape(PATCHES, 128)
             packed[pl.ds(i * 4 + rg, PATCHES, stride=4 * HOST), :] = x
             west = pltpu.roll(pltpu.roll(x, 1, 0), 128 - 15 + rg, 1)
             east = pltpu.roll(pltpu.roll(x, PATCHES - 1, 0), 3 + rg, 1)
@@ -503,18 +552,16 @@
         packed[pl.ds(i * 4 + 3, PATCHES, stride=4 * HOST), :] = edge
 
 
-def solver_scratch(count):
+def solver_scratch(count, height):
     return [
-        pltpu.VMEM((4, count * EXT, 256), f32),
-        pltpu.VMEM((count, EXT, LON), f32),
-        pltpu.VMEM((LAT // 128, 128), f32),
-        pltpu.VMEM((4, 256), f32),
-        pltpu.VMEM((4, 256), f32),
+        pltpu.VMEM((count * height * BLOCKS, 128), f32),
+        pltpu.VMEM((4, count * height, 256), f32),
+        pltpu.VMEM((count, height, LON), f32),
         pltpu.VMEM((4, 256, 256), bf16),
         pltpu.VMEM((4, 256, 256), bf16),
         pltpu.VMEM((4, 256, 256), bf16),
         pltpu.VMEM((4, 256, 256), bf16),
-        pltpu.SemaphoreType.DMA((7,)),
+        pltpu.SemaphoreType.DMA((4,)),
     ]
 
 
@@ -527,19 +574,19 @@
             pltpu.VMEM((PATCHES * HOST * 4, 128), f32),
             pltpu.VMEM((HOST, ROWS, LON), f32),
         ),
-        in_specs=[VMEM] * 7 + [FAR] * 7,
+        in_specs=[VMEM] * 8 + [FAR] * 4,
         out_specs=(VMEM, VMEM),
-        scratch_shapes=solver_scratch(HOST),
+        scratch_shapes=solver_scratch(HOST, TALL),
     )(*operands)
 
 
 def rest_kernel(
-    band, south, north, from_south, from_north, params, ext,
+    band, south, north, from_south, from_north, params, metric, damping,
     *rest,
 ):
-    far_constants, rest = rest[:7], rest[7:]
-    own_modes, hosted, expand, modes, expand_high, expand_low, spectral, solved = rest[:8]
-    *constants, sem = rest[8:]
+    far_constants, rest = rest[:4], rest[4:]
+    own_modes, hosted, expand, modes, expand_high, expand_low = rest[:6]
+    totals, spectral, solved, *constants, sem = rest[6:]
     fetches = fetch_all(far_constants, constants, sem)
     high, low = split_value(expand[...])
     dims = (((1,), (1,)), ((), ()))
@@ -551,11 +598,11 @@
     ).astype(bf16)
     modes[0:HOST] = own_modes[...]
     solve_slots(
-        HOST, SLOTS - HOST, band, south, north, from_south, from_north, params, ext, fetches,
-        constants, spectral, solved,
-    )
-    for i in range(SLOTS - HOST):
-        modes[HOST + i] = solved[i, 8:32, :]
+        HOST, REST, 0, band, south, north, from_south, from_north, params, metric, damping, fetches,
+        constants, totals, spectral, solved,
+    )
+    for i in range(REST):
+        modes[HOST + i] = solved[i]
 
 
 def rest_stage(*operands):
@@ -568,9 +615,9 @@
             pltpu.VMEM((MODES, MODES), bf16),
             pltpu.VMEM((MODES, MODES), bf16),
         ),
-        in_specs=[VMEM] * 7 + [FAR] * 7 + [VMEM] * 3,
+        in_specs=[VMEM] * 8 + [FAR] * 4 + [VMEM] * 3,
         out_specs=(VMEM, VMEM, VMEM),
-        scratch_shapes=solver_scratch(SLOTS - HOST),
+        scratch_shapes=solver_scratch(REST, ROWS),
     )(*operands)
 
 
@@ -683,14 +730,19 @@
         eigen_screening_factor.reshape(1, MODES),
         chebyshev_sweeps.reshape(1, MODES),
     )
+    wave, gain, *constants = constants
+
     band, south, north = band_stage(*near(exchange(packed, 4 * SLOTS)))
     size = lax.axis_size("lat")
     up = [(i, i + 1) for i in range(size - 1)]
     down = [(j, i) for i, j in up]
     from_south = lax.ppermute(north, "lat", up)
     from_north = lax.ppermute(south, "lat", down)
-    solver = near(band, south, north, from_south, from_north, params, ext) + (
-        filter_threshold.reshape(LAT // 128, 128), *constants,
+    damping, metric = damping_stage(
+        *near(ext), filter_threshold.reshape(LAT // 128, 128), wave, gain
+    )
+    solver = near(band, south, north, from_south, from_north, params, metric, damping) + tuple(
+        constants
     )
     returned, own_modes = host_stage(*solver)
     returned = exchange(returned, 4 * HOST)

time: 91.3 us -> 90.3 us (0.989)
  Pallas kernels: 19.5 us -> 18 us
    pallas_call x1, Pallas kernels: 7.36 us -> 6.07 us  [rest_stage(): pl.pallas_call(rest_kernel, name='rest_stage', out_shape=(jax.ShapeDtypeS...]
    all_to_all x1, waiting for transfers between devices: 8.05 us -> 9.33 us  [exchange(): x = lax.all_to_all(x, 'lon', split_axis=0, concat_axis=0, tiled=True)]
    pallas_call x1, Pallas kernels: 5.17 us -> 4.11 us  [host_stage(): pl.pallas_call(host_kernel, name='host_stage', out_shape=(pltpu.VMEM((PAT...]
  transfers between devices with their start and end apart: 3 -> 3, of which waited for: 3 -> 2; matrix products, arithmetic and copies ran while one was open for 0% -> 0% of each run, Pallas kernels for 8% -> 8%
where the time goes in v3:
time: 90.3 us; the launch traced here: 89.8 us
  blocking collectives  47.1 us (52%)
  Pallas kernels  18 us (20%)
  waiting for transfers between devices  13 us (14%)
  starting transfers between devices  10.9 us (12%)
    all_to_all x1, blocking collectives, exchange(): x = lax.all_to_all(x, 'lon', split_axis=0, concat_axis=0, tiled=True)  47.1 us
    all_to_all x1, waiting for transfers between devices, exchange(): x = lax.all_to_all(x, 'lon', split_axis=0, concat_axis=0, tiled=True)  9.33 us
    all_to_all x1, starting transfers between devices, exchange(): x = lax.all_to_all(x, 'lon', split_axis=0, concat_axis=0, tiled=True)  6.59 us
    pallas_call x1, Pallas kernels, rest_stage(): pl.pallas_call(rest_kernel, name='rest_stage', out_shape=(jax.ShapeDtypeS...  6.07 us
    pallas_call x1, Pallas kernels, host_stage(): pl.pallas_call(host_kernel, name='host_stage', out_shape=(pltpu.VMEM((PAT...  4.11 us
    ppermute x1, waiting for transfers between devices, local(): from_south = lax.ppermute(north, 'lat', up)  3.68 us
    pallas_call x1, Pallas kernels, patch_stage(): pl.pallas_call(patch_kernel, name='patch_stage', out_shape=(pltpu.VMEM((P...  3.14 us
    ppermute x1, starting transfers between devices, local(): from_south = lax.ppermute(north, 'lat', up)  2.41 us
  transfers between devices with their start and end apart: 3, of which 2 were waited for; matrix products, arithmetic and copies ran while one was open for 0% of the time, Pallas kernels for 8%

profile of v3, /device:TPU:6, one launch (start us, length us, event | category | flops | bytes accessed | tf_op | source)
XLA Modules:
  0.0 89.8 jit_solution(9775657203181323314)
XLA Ops:
  0.6 3.1 %patch_stage.1 = (f32[1536,128]{1,0:T(8,128)S(1)}, f32[3,8,128]{2,1,0:T(8,128)S(1)}, bf16[128,128]{1,0:T(8,128)(2,1)S(1)}, f32[384,128]{1,0:T(8,128)S(1)}, f32[40,1024]{1,0:T(8,128)S(1)}) custom-call(f32[24,16,128]{2,1,0:T(8,128)} %u_far.3, f32[24,16,128]{2,1,0:T(8,128)} %v_far.3, f32[24,16,128]{2,1,0:T(8,128)} %t_far.1, f32[24,16,128]{2,1,0:T(8,128)} %q_far.1, ...), custom_call_target="tpu_custom_call" | custom-call | tf_op jit(solution)/shard_map/patch_stage/pallas_call | solution.py:269
  3.8 0.0 copy-start
  3.8 47.1 %all_to_all.10 = f32[64,24,128]{2,1,0:T(8,128)S(1)} all-to-all(f32[64,24,128]{2,1,0:T(8,128)S(1)} %bitcast.10), channel_id=1, replica_groups=mesh['lat'=16,'lon'=64] {'lon'}, dimensions={0} | all-to-all | bytes 1572864 | tf_op jit(solution)/shard_map/all_to_all | solution.py:699
  50.9 1.8 %band_stage.1 = (f32[1152,128]{1,0:T(8,128)S(1)}, f32[384,128]{1,0:T(8,128)S(1)}, f32[384,128]{1,0:T(8,128)S(1)}) custom-call(f32[1536,128]{1,0:T(8,128)S(1)} %bitcast.8), custom_call_target="tpu_custom_call" | custom-call | tf_op jit(solution)/shard_map/band_stage/pallas_call | solution.py:324
  52.7 1.9 %collective-permute-start.1 = (f32[384,128]{1,0:T(8,128)S(1)}, f32[384,128]{1,0:T(8,128)S(1)}, u32[]{:S(2)}, u32[]{:S(2)}) collective-permute-start(f32[384,128]{1,0:T(8,128)S(1)} %get-tuple-element.22.south), channel_id=1, source_target_pairs={{64,0},{128,64},{192,128},{256,192},{320,256},{384,320},{448,384},... | collective-permute-start | bytes 589832 | tf_op jit(solution)/shard_map/ppermute | solution.py:740
  54.7 0.0 copy-done
  54.7 2.4 %collective-permute-start = (f32[384,128]{1,0:T(8,128)S(1)}, f32[384,128]{1,0:T(8,128)S(1)}, u32[]{:S(2)}, u32[]{:S(2)}) collective-permute-start(f32[384,128]{1,0:T(8,128)S(1)} %get-tuple-element.23.north), channel_id=1, source_target_pairs={{0,64},{64,128},{128,192},{192,256},{256,320},{320,384},{384,448},... | collective-permute-start | bytes 589832 | tf_op jit(solution)/shard_map/ppermute | solution.py:739
  57.1 0.9 damping_stage.1
  58.0 0.0 collective-permute-done.1.from_north
  58.0 3.7 %collective-permute-done.from_south = f32[384,128]{1,0:T(8,128)S(1)} collective-permute-done((f32[384,128]{1,0:T(8,128)S(1)}, f32[384,128]{1,0:T(8,128)S(1)}, u32[]{:S(2)}, u32[]{:S(2)}) %collective-permute-start) | collective-permute-done | bytes 196640 | tf_op jit(solution)/shard_map/ppermute | solution.py:739
  61.7 4.1 %host_stage.1 = (f32[512,128]{1,0:T(8,128)}, f32[2,24,1024]{2,1,0:T(8,128)S(1)}) custom-call(f32[1152,128]{1,0:T(8,128)S(1)} %get-tuple-element.21.band, f32[384,128]{1,0:T(8,128)S(1)} %get-tuple-element.22.south, f32[384,128]{1,0:T(8,128)S(1)} %get-tuple-element.23.north, f32[384,128]{1,0:T(8,128)S(1)} %collective-permute-done.from_south, ...), custom_call_target="tpu_custom_call" | custom-call | tf_op jit(solution)/shard_map/host_stage/pallas_call | solution.py:569
  65.8 6.6 %all-to-all-start.1 = ((f32[64,8,128]{2,1,0:T(8,128)}), f32[64,8,128]{2,1,0:T(8,128)S(1)}, u32[]{:S(2)}, u32[]{:S(2)}) async-start(f32[64,8,128]{2,1,0:T(8,128)} %bitcast.6), calls=%async_computation.1 | async-start | bytes 524288 | tf_op jit(solution)/shard_map/all_to_all | solution.py:699
  72.4 0.0 copy-start.1
  72.4 6.1 %rest_stage.1 = (f32[6,24,1024]{2,1,0:T(8,128)}, bf16[128,128]{1,0:T(8,128)(2,1)S(1)}, bf16[128,128]{1,0:T(8,128)(2,1)S(1)}) custom-call(f32[1152,128]{1,0:T(8,128)S(1)} %get-tuple-element.21.band, f32[384,128]{1,0:T(8,128)S(1)} %get-tuple-element.22.south, f32[384,128]{1,0:T(8,128)S(1)} %get-tuple-element.23.north, ...), custom_call_target="tpu_custom_call" | custom-call | tf_op jit(solution)/shard_map/rest_stage/pallas_call | solution.py:609
  78.5 9.3 %all-to-all-done.1 = f32[64,8,128]{2,1,0:T(8,128)S(1)} async-done(((f32[64,8,128]{2,1,0:T(8,128)}), f32[64,8,128]{2,1,0:T(8,128)S(1)}, u32[]{:S(2)}, u32[]{:S(2)}) %all-to-all-start.1) | async-done | bytes 262176 | tf_op jit(solution)/shard_map/all_to_all | solution.py:699
  87.8 0.0 copy-done.1
  87.8 2.0 %wind_stage.1 = (f32[24,16,128]{2,1,0:T(8,128)}, f32[24,16,128]{2,1,0:T(8,128)}) custom-call(f32[512,128]{1,0:T(8,128)S(1)} %bitcast.9, bf16[128,128]{1,0:T(8,128)(2,1)S(1)} %get-tuple-element.31.expand_high, bf16[128,128]{1,0:T(8,128)(2,1)S(1)} %get-tuple-element.32.expand_low, f32[384,128]{1,0:T(8,128)S(1)} %copy-done.1, f32[24,16,128]{2,1,0:T(8,128)} %u_far.3, ...), custom_call_target="tpu_custom_call" | custom-call | tf_op jit(solution)/shard_map/wind_stage/pallas_call | solution.py:675
Async XLA Ops:
  3.8 50.9 %copy-start = (f32[384,128]{1,0:T(8,128)}, f32[384,128]{1,0:T(8,128)S(1)}, u32[]{:S(2)}) copy-start(f32[384,128]{1,0:T(8,128)S(1)} %get-tuple-element.33.cell_metric) | copy-start | bytes 589828
  52.7 5.2 %collective-permute-start.1 = (f32[384,128]{1,0:T(8,128)S(1)}, f32[384,128]{1,0:T(8,128)S(1)}, u32[]{:S(2)}, u32[]{:S(2)}) collective-permute-start(f32[384,128]{1,0:T(8,128)S(1)} %get-tuple-element.22.south), channel_id=1, source_target_pairs={{64,0},{128,64},{192,128},{256,192},{320,256},{384,320},{448,384},... | collective-permute-start | bytes 589832 | tf_op jit(solution)/shard_map/ppermute | solution.py:740
  54.7 7.0 %collective-permute-start = (f32[384,128]{1,0:T(8,128)S(1)}, f32[384,128]{1,0:T(8,128)S(1)}, u32[]{:S(2)}, u32[]{:S(2)}) collective-permute-start(f32[384,128]{1,0:T(8,128)S(1)} %get-tuple-element.23.north), channel_id=1, source_target_pairs={{0,64},{64,128},{128,192},{192,256},{256,320},{320,384},{384,448},... | collective-permute-start | bytes 589832 | tf_op jit(solution)/shard_map/ppermute | solution.py:739
  65.8 22.0 %all-to-all-start.1 = ((f32[64,8,128]{2,1,0:T(8,128)}), f32[64,8,128]{2,1,0:T(8,128)S(1)}, u32[]{:S(2)}, u32[]{:S(2)}) async-start(f32[64,8,128]{2,1,0:T(8,128)} %bitcast.6), calls=%async_computation.1 | async-start | bytes 524288 | tf_op jit(solution)/shard_map/all_to_all | solution.py:699
  72.4 15.4 %copy-start.1 = (f32[384,128]{1,0:T(8,128)S(1)}, f32[384,128]{1,0:T(8,128)}, u32[]{:S(2)}) copy-start(f32[384,128]{1,0:T(8,128)} %copy-done) | copy-start | bytes 589828

commit v4 on v3

--- a/solution.py
+++ b/solution.py
@@ -159,7 +159,7 @@
 
 def patch_kernel(
     u_far, v_far, t_far, q_far, metric, holder, project, depth, sweeps,
-    packed, params, hosted, cell_metric, ext,
+    packed, params, hosted, ext,
     u, v, t, q, own, field, edges, chosen, sem, field_sem,
 ):
     lat = lax.axis_index("lat")
@@ -205,7 +205,6 @@
     west_metric = pltpu.roll(lanes(west_block), (129 - offset) % 128, 1)[8:32, 0:1]
     east_metric = pltpu.roll(lanes(east_block), (256 - COLS - offset) % 128, 1)[8:32, 0:1]
     scale = jnp.concatenate([cell_column(own[8 + r : 9 + r, :]) for r in range(ROWS)], axis=0)
-    cell_metric[...] = 0.25 * scale
     for c in copies[len(metric_copies) :]:
         c.wait()
 
@@ -274,11 +273,10 @@
             pltpu.VMEM((PATCHES * SLOTS * 4, 128), f32),
             pltpu.VMEM((3, 8, 128), f32),
             pltpu.VMEM((HOST * PATCHES, MODES), bf16),
-            pltpu.VMEM((CELLS, MODES), f32),
             pltpu.VMEM((EXT, LON), f32),
         ),
         in_specs=[FAR] * 5 + [VMEM] * 4,
-        out_specs=(VMEM,) * 5,
+        out_specs=(VMEM,) * 4,
         scratch_shapes=[pltpu.VMEM((ROWS, COLS, MODES), f32)] * 4
         + [
             pltpu.VMEM((EXT, 128), f32),
@@ -335,6 +333,44 @@
     )(received)
 
 
+def split_eight(x, spectral, row):
+    root = math.sqrt(0.5)
+    s04, d04 = x[0] + x[4], x[0] - x[4]
+    s26, d26 = x[2] + x[6], x[2] - x[6]
+    s15, d15 = x[1] + x[5], x[1] - x[5]
+    s37, d37 = x[3] + x[7], x[3] - x[7]
+    even, odd = s04 + s26, s15 + s37
+    lean, turn = root * (d15 - d37), root * (d15 + d37)
+    at = slice(row, row + 8)
+    spectral[0, at, 0:128] = even + odd
+    spectral[0, at, 128:256] = even - odd
+    spectral[1, at, 0:128] = d04 + lean
+    spectral[1, at, 128:256] = -d26 - turn
+    spectral[2, at, 0:128] = s04 - s26
+    spectral[2, at, 128:256] = s37 - s15
+    spectral[3, at, 0:128] = d04 - lean
+    spectral[3, at, 128:256] = d26 - turn
+
+
+def join_eight(spectral, row):
+    root = math.sqrt(0.5)
+    at = slice(row, row + 8)
+    y0, y4 = spectral[0, at, 0:128], spectral[0, at, 128:256]
+    p1, q1 = spectral[1, at, 0:128], spectral[1, at, 128:256]
+    p2, q2 = spectral[2, at, 0:128], spectral[2, at, 128:256]
+    p3, q3 = spectral[3, at, 0:128], spectral[3, at, 128:256]
+    even, odd = y0 + y4, y0 - y4
+    lean = root * ((p1 - p3) - (q1 + q3))
+    turn = root * ((p3 - p1) - (q1 + q3))
+    side, swing = p1 + p3, q3 - q1
+    up, down = even + p2, even - p2
+    left, right = odd - q2, odd + q2
+    return (
+        up + side, left + lean, down + swing, right + turn,
+        up - side, left - lean, down - swing, right - turn,
+    )
+
+
 def solve_slots(
     first, count, edge, band, south, north, from_south, from_north, params, metric, damping,
     fetches, constants, totals, spectral, solved,
@@ -343,6 +379,9 @@
     height = solved.shape[1]
     reach = MAXIT - 1 + edge
     out = ROWS + 2 * edge
+
+    def rows_list(x):
+        return [x[r : r + 1] for r in range(x.shape[0])]
 
     def neighbours(x):
         lane = lax.broadcasted_iota(jnp.int32, x.shape, 2)
@@ -389,45 +428,34 @@
             height_now, BLOCKS, 128
         )
         direction = residual * wide(1.0 / centre)
-        total = direction[MAXIT - 1 : MAXIT - 1 + out]
+        total = rows_list(direction[MAXIT - 1 : MAXIT - 1 + out])
+        direction, residual, coupling = map(rows_list, (direction, residual, coupling))
         for sweep in range(1, MAXIT):
-            middle = direction[1:-1]
-            around = neighbours(middle) + (direction[2:] + direction[:-2])
-            residual = residual[1:-1] - middle + coupling * (around - 4.0 * middle)
-            coupling = coupling[1:-1]
             after = 1.0 / (2.0 * relative - ratio)
-            direction = wide(after * ratio) * middle + wide(2.0 * after / radius) * residual
+            keep, push = wide(after * ratio), wide(2.0 * after / radius)
+            active = wide(jnp.where(number > sweep, 1.0, 0.0))
             ratio = after
             low = MAXIT - 1 - sweep
-            if sweep < MINIT:
-                total = total + direction[low : low + out]
-            else:
-                active = wide(jnp.where(number > sweep, 1.0, 0.0))
-                total = total + active * direction[low : low + out]
+            fresh, left = [], []
+            for r in range(len(direction) - 2):
+                middle = direction[r + 1]
+                around = neighbours(middle) + (direction[r] + direction[r + 2])
+                rest = residual[r + 1] - middle + coupling[r + sweep - 1] * (around - 4.0 * middle)
+                left.append(rest)
+                fresh.append(keep * middle + push * rest)
+                if low <= r < low + out:
+                    gain = fresh[r] if sweep < MINIT else active * fresh[r]
+                    total[r - low] = total[r - low] + gain
+            direction, residual = fresh, left
+        total = jnp.concatenate(total, axis=0)
         at = i * height * BLOCKS
         if edge:
             parts = [total[1 : ROWS + 2], total[0:1]]
             parts.append(jnp.zeros((height - ROWS - 2, BLOCKS, 128), f32))
             total = jnp.concatenate(parts, axis=0)
         totals[at : at + height * BLOCKS, :] = total.reshape(height * BLOCKS, 128)
-        x = [totals[spread_rows(i * height, a, height), :] for a in range(BLOCKS)]
-        root = math.sqrt(0.5)
-        s04, d04 = x[0] + x[4], x[0] - x[4]
-        s26, d26 = x[2] + x[6], x[2] - x[6]
-        s15, d15 = x[1] + x[5], x[1] - x[5]
-        s37, d37 = x[3] + x[7], x[3] - x[7]
-        even, odd = s04 + s26, s15 + s37
-        lean, turn = root * (d15 - d37), root * (d15 + d37)
-        at = slice(i * height, (i + 1) * height)
-        spectral[0, at, 0:128] = even + odd
-        spectral[0, at, 128:256] = even - odd
-        spectral[1, at, 0:128] = d04 + lean
-        spectral[1, at, 128:256] = -d26 - turn
-        spectral[2, at, 0:128] = s04 - s26
-        spectral[2, at, 128:256] = s37 - s15
-        spectral[3, at, 0:128] = d04 - lean
-        spectral[3, at, 128:256] = d26 - turn
-
+        for row in range(i * height, (i + 1) * height, 8):
+            split_eight([totals[spread_rows(row, a), :] for a in range(BLOCKS)], spectral, row)
     for c in fetches:
         c.wait()
     for k in range(4):
@@ -436,28 +464,10 @@
         spectrum = dot3(split_value(spectral[k, 0 : count * height, :]), table, ((1,), (0,)))
         back = (back_high[k], back_low[k])
         spectral[k, 0 : count * height, :] = dot3(split_value(spectrum * weight), back, ((1,), (0,)))
-    root = math.sqrt(0.5)
-    y0 = spectral[0, 0 : count * height, 0:128]
-    y4 = spectral[0, 0 : count * height, 128:256]
-    p1, q1 = spectral[1, 0 : count * height, 0:128], spectral[1, 0 : count * height, 128:256]
-    p2, q2 = spectral[2, 0 : count * height, 0:128], spectral[2, 0 : count * height, 128:256]
-    p3, q3 = spectral[3, 0 : count * height, 0:128], spectral[3, 0 : count * height, 128:256]
-    even, odd = y0 + y4, y0 - y4
-    a1, b1 = root * p1, root * q1
-    a3, b3 = root * p3, root * q3
-    swing = q3 - q1
-    parts = [None] * 8
-    base, side = even + p2, p1 + p3
-    parts[0], parts[4] = base + side, base - side
-    base, side = even - p2, swing
-    parts[2], parts[6] = base + side, base - side
-    base, side = odd - q2, (a1 - b1) - (a3 + b3)
-    parts[1], parts[5] = base + side, base - side
-    base, side = odd + q2, (a3 - b3) - (a1 + b1)
-    parts[3], parts[7] = base + side, base - side
-    for i in range(count):
-        for a in range(BLOCKS):
-            solved[i, :, 128 * a : 128 * a + 128] = parts[a][i * height : (i + 1) * height]
+    for row in range(0, count * height, 8):
+        i, start = row // height, row % height
+        for a, part in enumerate(join_eight(spectral, row)):
+            solved[i, start : start + 8, 128 * a : 128 * a + 128] = part
 
 
 def damping_kernel(ext, cutoff, wave, gain, damping, metric):
@@ -585,8 +595,9 @@
     *rest,
 ):
     far_constants, rest = rest[:4], rest[4:]
-    own_modes, hosted, expand, modes, expand_high, expand_low = rest[:6]
-    totals, spectral, solved, *constants, sem = rest[6:]
+    own_modes, hosted, expand, u_far, v_far, modes, expand_high, expand_low, u, v = rest[:10]
+    cell_metric, totals, spectral, solved, *constants, sem, wind_sem, own = rest[10:]
+    winds = fetch_all((u_far, v_far), (u, v), wind_sem)
     fetches = fetch_all(far_constants, constants, sem)
     high, low = split_value(expand[...])
     dims = (((1,), (1,)), ((), ()))
@@ -603,6 +614,14 @@
     )
     for i in range(REST):
         modes[HOST + i] = solved[i]
+    lon = lax.axis_index("lon")
+    own[...] = pltpu.roll(
+        metric[spread_rows(8, lon // 8, ROWS), :], (128 - lon % 8 * COLS) % 128, 1
+    )
+    for r in range(ROWS):
+        cell_metric[r * COLS : (r + 1) * COLS, :] = 0.25 * cell_column(own[r : r + 1, :])
+    for c in winds:
+        c.wait()
 
 
 def rest_stage(*operands):
@@ -614,18 +633,20 @@
             jax.ShapeDtypeStruct((SLOTS, ROWS, LON), f32),
             pltpu.VMEM((MODES, MODES), bf16),
             pltpu.VMEM((MODES, MODES), bf16),
+            pltpu.VMEM((ROWS, COLS, MODES), f32),
+            pltpu.VMEM((ROWS, COLS, MODES), f32),
+            pltpu.VMEM((CELLS, MODES), f32),
         ),
-        in_specs=[VMEM] * 8 + [FAR] * 4 + [VMEM] * 3,
-        out_specs=(VMEM, VMEM, VMEM),
-        scratch_shapes=solver_scratch(REST, ROWS),
+        in_specs=[VMEM] * 8 + [FAR] * 4 + [VMEM] * 3 + [FAR] * 2,
+        out_specs=(VMEM,) * 6,
+        scratch_shapes=solver_scratch(REST, ROWS)
+        + [pltpu.SemaphoreType.DMA((2,)), pltpu.VMEM((ROWS, 128), f32)],
     )(*operands)
 
 
 def wind_kernel(
-    received, expand_high, expand_low, cell_metric, u_far, v_far, u_new, v_new,
-    tall, edges, edge, u, v, sem,
+    received, expand_high, expand_low, cell_metric, u, v, u_new, v_new, tall, edges, edge
 ):
-    fetches = fetch_all((u_far, v_far), (u, v), sem)
     turn = lax.axis_index("lon") % 8
     table = (expand_high[...], expand_low[...])
     for part in range(4):
@@ -663,8 +684,6 @@
     east = jnp.where(col == COLS - 1, spread(3), pltpu.roll(pressure, CELLS - 1, 0))
     west = jnp.where(col == 0, spread(0), pltpu.roll(pressure, 1, 0))
     scale = cell_metric[...]
-    for c in fetches:
-        c.wait()
     u_new[...] = u[...] - (scale * (east - west)).reshape(ROWS, COLS, MODES)
     slope = tall[2 * COLS : CELLS + 2 * COLS, :] - tall[0:CELLS, :]
     v_new[...] = v[...] - (scale * slope).reshape(ROWS, COLS, MODES)
@@ -677,15 +696,12 @@
         name="wind_stage",
 
         out_shape=(shape, shape),
-        in_specs=[VMEM] * 4 + [FAR] * 2,
+        in_specs=[VMEM] * 6,
         out_specs=(VMEM, VMEM),
         scratch_shapes=[
             pltpu.VMEM((CELLS + 2 * COLS, MODES), f32),
             pltpu.VMEM((128, MODES), f32),
             pltpu.VMEM((128, MODES), f32),
-            pltpu.VMEM((ROWS, COLS, MODES), f32),
-            pltpu.VMEM((ROWS, COLS, MODES), f32),
-            pltpu.SemaphoreType.DMA((2,)),
         ],
     )(*operands)
 
@@ -719,7 +735,7 @@
         high = np.asarray(x, np.float32).astype(bf16)
         tables += [high, (x - high.astype(np.float64)).astype(np.float32).astype(bf16)]
     constants = [jnp.asarray(x) for x in [wave.astype(np.float32), gain.astype(np.float32)] + tables]
-    packed, params, hosted, cell_metric, ext = patch_stage(
+    packed, params, hosted, ext = patch_stage(
         eastward_velocity,
         northward_velocity,
         thermal_anomaly,
@@ -746,11 +762,11 @@
     )
     returned, own_modes = host_stage(*solver)
     returned = exchange(returned, 4 * HOST)
-    mode_solution, expand_high, expand_low = rest_stage(
-        *solver, *near(own_modes, hosted), eigen_to_layers
+    mode_solution, expand_high, expand_low, u, v, cell_metric = rest_stage(
+        *solver, *near(own_modes, hosted), eigen_to_layers, eastward_velocity, northward_velocity
     )
     u_new, v_new = wind_stage(
-        *near(returned, expand_high, expand_low, cell_metric), eastward_velocity, northward_velocity
+        *near(returned, expand_high, expand_low, cell_metric, u, v)
     )
     return u_new, v_new, mode_solution
 

time: 90.3 us -> 90.6 us (level)
  the two profiles are of different devices: /device:TPU:6 before, /device:TPU:7 now
where the time goes in v4:
time: 90.6 us; the launch traced here: 90.1 us
  blocking collectives  44.9 us (50%)
  Pallas kernels  16.7 us (18%)
  starting transfers between devices  15.4 us (17%)
  waiting for transfers between devices  10.6 us (12%)
  local copies, waits for them, and re-layouts  1.86 us (2%)
    all_to_all x1, blocking collectives, exchange(): x = lax.all_to_all(x, 'lon', split_axis=0, concat_axis=0, tiled=True)  44.9 us
    ppermute x1, starting transfers between devices, local(): from_south = lax.ppermute(north, 'lat', up)  7.16 us
    all_to_all x1, starting transfers between devices, exchange(): x = lax.all_to_all(x, 'lon', split_axis=0, concat_axis=0, tiled=True)  6.3 us
    pallas_call x1, Pallas kernels, rest_stage(): pl.pallas_call(rest_kernel, name='rest_stage', out_shape=(jax.ShapeDtypeS...  5.48 us
    ppermute x1, waiting for transfers between devices, local(): from_north = lax.ppermute(south, 'lat', down)  5.38 us
    all_to_all x1, waiting for transfers between devices, exchange(): x = lax.all_to_all(x, 'lon', split_axis=0, concat_axis=0, tiled=True)  5.18 us
    pallas_call x1, Pallas kernels, host_stage(): pl.pallas_call(host_kernel, name='host_stage', out_shape=(pltpu.VMEM((PAT...  4.29 us
    pallas_call x1, Pallas kernels, patch_stage(): pl.pallas_call(patch_kernel, name='patch_stage', out_shape=(pltpu.VMEM((P...  3.03 us
  transfers between devices with their start and end apart: 3, of which 2 were waited for; matrix products, arithmetic and copies ran while one was open for 0% of the time, Pallas kernels for 7%

profile of v4, /device:TPU:7, one launch (start us, length us, event | category | flops | bytes accessed | tf_op | source)
XLA Modules:
  0.0 90.1 jit_solution(4227109498426574319)
XLA Ops:
  0.6 3.0 %patch_stage.1 = (f32[1536,128]{1,0:T(8,128)S(1)}, f32[3,8,128]{2,1,0:T(8,128)S(1)}, bf16[128,128]{1,0:T(8,128)(2,1)S(1)}, f32[40,1024]{1,0:T(8,128)S(1)}) custom-call(f32[24,16,128]{2,1,0:T(8,128)} %rest_7_.1, f32[24,16,128]{2,1,0:T(8,128)} %rest_8_.1, f32[24,16,128]{2,1,0:T(8,128)} %t_far.1, f32[24,16,128]{2,1,0:T(8,128)} %q_far.1, f32[384,1024]{1,0:T(8,128)} %metric.1, ...), custom_call_target="tpu_custom_call" | custom-call | tf_op jit(solution)/shard_map/patch_stage/pallas_call | solution.py:268
  3.7 44.9 %all_to_all.10 = f32[64,24,128]{2,1,0:T(8,128)S(1)} all-to-all(f32[64,24,128]{2,1,0:T(8,128)S(1)} %bitcast.10), channel_id=1, replica_groups=mesh['lat'=16,'lon'=64] {'lon'}, dimensions={0} | all-to-all | bytes 1572864 | tf_op jit(solution)/shard_map/all_to_all | solution.py:715
  48.5 1.8 %band_stage.1 = (f32[1152,128]{1,0:T(8,128)S(1)}, f32[384,128]{1,0:T(8,128)S(1)}, f32[384,128]{1,0:T(8,128)S(1)}) custom-call(f32[1536,128]{1,0:T(8,128)S(1)} %bitcast.8), custom_call_target="tpu_custom_call" | custom-call | tf_op jit(solution)/shard_map/band_stage/pallas_call | solution.py:322
  50.4 0.0 copy-start
  50.4 0.0 copy-start.2
  50.4 7.2 %collective-permute-start = (f32[384,128]{1,0:T(8,128)S(1)}, f32[384,128]{1,0:T(8,128)S(1)}, u32[]{:S(2)}, u32[]{:S(2)}) collective-permute-start(f32[384,128]{1,0:T(8,128)S(1)} %get-tuple-element.25.north), channel_id=1, source_target_pairs={{0,64},{64,128},{128,192},{192,256},{256,320},{320,384},{384,448},... | collective-permute-start | bytes 589832 | tf_op jit(solution)/shard_map/ppermute | solution.py:755
  57.5 1.9 %collective-permute-start.1 = (f32[384,128]{1,0:T(8,128)S(1)}, f32[384,128]{1,0:T(8,128)S(1)}, u32[]{:S(2)}, u32[]{:S(2)}) collective-permute-start(f32[384,128]{1,0:T(8,128)S(1)} %get-tuple-element.24.south), channel_id=1, source_target_pairs={{64,0},{128,64},{192,128},{256,192},{320,256},{384,320},{448,384},... | collective-permute-start | bytes 589832 | tf_op jit(solution)/shard_map/ppermute | solution.py:756
  59.5 0.9 damping_stage.1
  60.4 0.0 collective-permute-done.from_south
  60.4 5.4 %collective-permute-done.1.from_north = f32[384,128]{1,0:T(8,128)S(1)} collective-permute-done((f32[384,128]{1,0:T(8,128)S(1)}, f32[384,128]{1,0:T(8,128)S(1)}, u32[]{:S(2)}, u32[]{:S(2)}) %collective-permute-start.1) | collective-permute-done | bytes 196640 | tf_op jit(solution)/shard_map/ppermute | solution.py:756
  65.7 4.3 %host_stage.1 = (f32[512,128]{1,0:T(8,128)}, f32[2,24,1024]{2,1,0:T(8,128)S(1)}) custom-call(f32[1152,128]{1,0:T(8,128)S(1)} %get-tuple-element.23.band, f32[384,128]{1,0:T(8,128)S(1)} %get-tuple-element.24.south, f32[384,128]{1,0:T(8,128)S(1)} %get-tuple-element.25.north, f32[384,128]{1,0:T(8,128)S(1)} %collective-permute-done.from_south, ...), custom_call_target="tpu_custom_call" | custom-call | tf_op jit(solution)/shard_map/host_stage/pallas_call | solution.py:579
  70.1 0.0 copy-done
  70.1 0.0 copy-done.2
  70.1 6.3 %all-to-all-start.1 = ((f32[64,8,128]{2,1,0:T(8,128)}), f32[64,8,128]{2,1,0:T(8,128)S(1)}, u32[]{:S(2)}, u32[]{:S(2)}) async-start(f32[64,8,128]{2,1,0:T(8,128)} %bitcast.6), calls=%async_computation.1 | async-start | bytes 524288 | tf_op jit(solution)/shard_map/all_to_all | solution.py:715
  76.4 0.0 copy-start.1
  76.4 0.9 %copy-done.1 = f32[384,128]{1,0:T(8,128)S(1)} copy-done((f32[384,128]{1,0:T(8,128)S(1)}, f32[384,128]{1,0:T(8,128)}, u32[]{:S(2)}) %copy-start.1) | copy-done | bytes 196632
  77.3 0.0 copy-start.3
  77.3 0.9 %copy-done.3 = f32[384,128]{1,0:T(8,128)S(1)} copy-done((f32[384,128]{1,0:T(8,128)S(1)}, f32[384,128]{1,0:T(8,128)}, u32[]{:S(2)}) %copy-start.3) | copy-done | bytes 196632
  78.2 5.5 %rest_stage.1 = (f32[6,24,1024]{2,1,0:T(8,128)}, bf16[128,128]{1,0:T(8,128)(2,1)S(1)}, bf16[128,128]{1,0:T(8,128)(2,1)S(1)}, f32[24,16,128]{2,1,0:T(8,128)S(1)},...) custom-call(f32[1152,128]{1,0:T(8,128)S(1)} %get-tuple-element.23.band, f32[384,128]{1,0:T(8,128)S(1)} %copy-done.1, ...), custom_call_target="tpu_custom_call" | custom-call | tf_op jit(solution)/shard_map/rest_stage/pallas_call | solution.py:628
  83.7 5.2 %all-to-all-done.1 = f32[64,8,128]{2,1,0:T(8,128)S(1)} async-done(((f32[64,8,128]{2,1,0:T(8,128)}), f32[64,8,128]{2,1,0:T(8,128)S(1)}, u32[]{:S(2)}, u32[]{:S(2)}) %all-to-all-start.1) | async-done | bytes 262176 | tf_op jit(solution)/shard_map/all_to_all | solution.py:715
  88.9 1.2 %wind_stage.1 = (f32[24,16,128]{2,1,0:T(8,128)}, f32[24,16,128]{2,1,0:T(8,128)}) custom-call(f32[512,128]{1,0:T(8,128)S(1)} %bitcast.9, bf16[128,128]{1,0:T(8,128)(2,1)S(1)} %get-tuple-element.33.expand_high, bf16[128,128]{1,0:T(8,128)(2,1)S(1)} %get-tuple-element.34.expand_low, f32[384,128]{1,0:T(8,128)S(1)} %get-tuple-element.35.cell_metric, ...), custom_call_target="tpu_custom_call" | custom-call | tf_op jit(solution)/shard_map/wind_stage/pallas_call | solution.py:694
Async XLA Ops:
  50.4 19.7 %copy-start = (f32[384,128]{1,0:T(8,128)}, f32[384,128]{1,0:T(8,128)S(1)}, u32[]{:S(2)}) copy-start(f32[384,128]{1,0:T(8,128)S(1)} %get-tuple-element.24.south) | copy-start | bytes 589828
  50.4 19.7 %copy-start.2 = (f32[384,128]{1,0:T(8,128)}, f32[384,128]{1,0:T(8,128)S(1)}, u32[]{:S(2)}) copy-start(f32[384,128]{1,0:T(8,128)S(1)} %get-tuple-element.25.north) | copy-start | bytes 589828
  50.4 10.0 %collective-permute-start = (f32[384,128]{1,0:T(8,128)S(1)}, f32[384,128]{1,0:T(8,128)S(1)}, u32[]{:S(2)}, u32[]{:S(2)}) collective-permute-start(f32[384,128]{1,0:T(8,128)S(1)} %get-tuple-element.25.north), channel_id=1, source_target_pairs={{0,64},{64,128},{128,192},{192,256},{256,320},{320,384},{384,448},... | collective-permute-start | bytes 589832 | tf_op jit(solution)/shard_map/ppermute | solution.py:755
  57.5 8.2 %collective-permute-start.1 = (f32[384,128]{1,0:T(8,128)S(1)}, f32[384,128]{1,0:T(8,128)S(1)}, u32[]{:S(2)}, u32[]{:S(2)}) collective-permute-start(f32[384,128]{1,0:T(8,128)S(1)} %get-tuple-element.24.south), channel_id=1, source_target_pairs={{64,0},{128,64},{192,128},{256,192},{320,256},{384,320},{448,384},... | collective-permute-start | bytes 589832 | tf_op jit(solution)/shard_map/ppermute | solution.py:756
  70.1 18.8 %all-to-all-start.1 = ((f32[64,8,128]{2,1,0:T(8,128)}), f32[64,8,128]{2,1,0:T(8,128)S(1)}, u32[]{:S(2)}, u32[]{:S(2)}) async-start(f32[64,8,128]{2,1,0:T(8,128)} %bitcast.6), calls=%async_computation.1 | async-start | bytes 524288 | tf_op jit(solution)/shard_map/all_to_all | solution.py:715
  76.4 0.9 %copy-start.1 = (f32[384,128]{1,0:T(8,128)S(1)}, f32[384,128]{1,0:T(8,128)}, u32[]{:S(2)}) copy-start(f32[384,128]{1,0:T(8,128)} %copy-done) | copy-start | bytes 589828
  77.3 0.9 %copy-start.3 = (f32[384,128]{1,0:T(8,128)S(1)}, f32[384,128]{1,0:T(8,128)}, u32[]{:S(2)}) copy-start(f32[384,128]{1,0:T(8,128)} %copy-done.2) | copy-start | bytes 589828

commit v5 on v4

--- a/solution.py
+++ b/solution.py
@@ -372,7 +372,7 @@
 
 
 def solve_slots(
-    first, count, edge, band, south, north, from_south, from_north, params, metric, damping,
+    first, count, edge, band, rims, from_south, from_north, params, metric, damping,
     fetches, constants, totals, spectral, solved,
 ):
     table_high, table_low, back_high, back_low = constants
@@ -413,11 +413,11 @@
         residual = jnp.concatenate(
             [
                 below[8 - reach : 7],
-                below[7:8] + rows_of(south, 8)[7:8],
+                below[7:8] + rows_of(rims, 2)[0:1],
                 mine[0:1] + below[0:1],
                 mine[1:23],
                 mine[23:24] + above[7:8],
-                above[0:1] + rows_of(north, 8)[0:1],
+                above[0:1] + rows_of(rims, 2)[1:2],
                 above[1:reach],
             ],
             axis=0,
@@ -456,12 +456,15 @@
         totals[at : at + height * BLOCKS, :] = total.reshape(height * BLOCKS, 128)
         for row in range(i * height, (i + 1) * height, 8):
             split_eight([totals[spread_rows(row, a), :] for a in range(BLOCKS)], spectral, row)
-    for c in fetches:
+    for c in fetches[:2]:
         c.wait()
     for k in range(4):
         table = (table_high[k], table_low[k])
         weight = jnp.concatenate([damping[k, 0:height, :]] * count, axis=0)
         spectrum = dot3(split_value(spectral[k, 0 : count * height, :]), table, ((1,), (0,)))
+        if k == 0:
+            for c in fetches[2:]:
+                c.wait()
         back = (back_high[k], back_low[k])
         spectral[k, 0 : count * height, :] = dot3(split_value(spectrum * weight), back, ((1,), (0,)))
     for row in range(0, count * height, 8):
@@ -470,7 +473,11 @@
             solved[i, start : start + 8, 128 * a : 128 * a + 128] = part
 
 
-def damping_kernel(ext, cutoff, wave, gain, damping, metric):
+def damping_kernel(ext, south, north, cutoff, wave, gain, damping, metric, rims):
+    for s in range(SLOTS):
+        top, bottom = s * 8 * BLOCKS, 2 * s * BLOCKS
+        rims[bottom : bottom + BLOCKS, :] = south[top + 7 * BLOCKS : top + 8 * BLOCKS, :]
+        rims[bottom + BLOCKS : bottom + 2 * BLOCKS, :] = north[top : top + BLOCKS, :]
     for tile in range(EXT // 8):
         for b in range(BLOCKS):
             metric[spread_rows(8 * tile, b), :] = ext[
@@ -501,9 +508,10 @@
         out_shape=(
             pltpu.VMEM((4, TALL, 256), f32),
             pltpu.VMEM((EXT * BLOCKS, 128), f32),
+            pltpu.VMEM((SLOTS * 2 * BLOCKS, 128), f32),
         ),
-        in_specs=[VMEM] * 4,
-        out_specs=(VMEM, VMEM),
+        in_specs=[VMEM] * 6,
+        out_specs=(VMEM,) * 3,
     )(*operands)
 
 
@@ -518,7 +526,7 @@
 
 
 def host_kernel(
-    band, south, north, from_south, from_north, params, metric, damping,
+    band, rims, from_south, from_north, params, metric, damping,
     *rest,
 ):
     far_constants, (packed, own_modes, totals, spectral, solved), (*constants, sem) = (
@@ -526,7 +534,7 @@
     )
     fetches = fetch_all(far_constants, constants, sem)
     solve_slots(
-        0, HOST, 1, band, south, north, from_south, from_north, params, metric, damping, fetches,
+        0, HOST, 1, band, rims, from_south, from_north, params, metric, damping, fetches,
         constants, totals, spectral, solved,
     )
     place = lax.broadcasted_iota(jnp.int32, (PATCHES, 128), 1) & (COLS - 1)
@@ -584,14 +592,14 @@
             pltpu.VMEM((PATCHES * HOST * 4, 128), f32),
             pltpu.VMEM((HOST, ROWS, LON), f32),
         ),
-        in_specs=[VMEM] * 8 + [FAR] * 4,
+        in_specs=[VMEM] * 7 + [FAR] * 4,
         out_specs=(VMEM, VMEM),
         scratch_shapes=solver_scratch(HOST, TALL),
     )(*operands)
 
 
 def rest_kernel(
-    band, south, north, from_south, from_north, params, metric, damping,
+    band, rims, from_south, from_north, params, metric, damping,
     *rest,
 ):
     far_constants, rest = rest[:4], rest[4:]
@@ -609,7 +617,7 @@
     ).astype(bf16)
     modes[0:HOST] = own_modes[...]
     solve_slots(
-        HOST, REST, 0, band, south, north, from_south, from_north, params, metric, damping, fetches,
+        HOST, REST, 0, band, rims, from_south, from_north, params, metric, damping, fetches,
         constants, totals, spectral, solved,
     )
     for i in range(REST):
@@ -637,7 +645,7 @@
             pltpu.VMEM((ROWS, COLS, MODES), f32),
             pltpu.VMEM((CELLS, MODES), f32),
         ),
-        in_specs=[VMEM] * 8 + [FAR] * 4 + [VMEM] * 3 + [FAR] * 2,
+        in_specs=[VMEM] * 7 + [FAR] * 4 + [VMEM] * 3 + [FAR] * 2,
         out_specs=(VMEM,) * 6,
         scratch_shapes=solver_scratch(REST, ROWS)
         + [pltpu.SemaphoreType.DMA((2,)), pltpu.VMEM((ROWS, 128), f32)],
@@ -754,10 +762,10 @@
     down = [(j, i) for i, j in up]
     from_south = lax.ppermute(north, "lat", up)
     from_north = lax.ppermute(south, "lat", down)
-    damping, metric = damping_stage(
-        *near(ext), filter_threshold.reshape(LAT // 128, 128), wave, gain
-    )
-    solver = near(band, south, north, from_south, from_north, params, metric, damping) + tuple(
+    damping, metric, rims = damping_stage(
+        *near(ext, south, north), filter_threshold.reshape(LAT // 128, 128), wave, gain
+    )
+    solver = near(band, rims, from_south, from_north, params, metric, damping) + tuple(
         constants
     )
     returned, own_modes = host_stage(*solver)

time: 90.6 us -> 90.4 us (level)
  waiting for transfers between devices: 10.6 us -> 12.5 us
  local copies, waits for them, and re-layouts: 1.86 us -> 0 us
    all_to_all x1, waiting for transfers between devices: 5.18 us -> 7.12 us  [exchange(): x = lax.all_to_all(x, 'lon', split_axis=0, concat_axis=0, tiled=True)]
    unnamed x8 -> x0, local copies, waits for them, and re-layouts: 1.86 us -> none
where the time goes in v5:
time: 90.4 us; the launch traced here: 89.9 us
  blocking collectives  44.9 us (50%)
  Pallas kernels  16.5 us (18%)
  starting transfers between devices  15.4 us (17%)
  waiting for transfers between devices  12.5 us (14%)
    all_to_all x1, blocking collectives, exchange(): x = lax.all_to_all(x, 'lon', split_axis=0, concat_axis=0, tiled=True)  44.9 us
    ppermute x1, starting transfers between devices, local(): from_south = lax.ppermute(north, 'lat', up)  7.16 us
    all_to_all x1, waiting for transfers between devices, exchange(): x = lax.all_to_all(x, 'lon', split_axis=0, concat_axis=0, tiled=True)  7.12 us
    all_to_all x1, starting transfers between devices, exchange(): x = lax.all_to_all(x, 'lon', split_axis=0, concat_axis=0, tiled=True)  6.3 us
    pallas_call x1, Pallas kernels, rest_stage(): pl.pallas_call(rest_kernel, name='rest_stage', out_shape=(jax.ShapeDtypeS...  5.39 us
    ppermute x1, waiting for transfers between devices, local(): from_north = lax.ppermute(south, 'lat', down)  5.38 us
    pallas_call x1, Pallas kernels, host_stage(): pl.pallas_call(host_kernel, name='host_stage', out_shape=(pltpu.VMEM((PAT...  4.22 us
    pallas_call x1, Pallas kernels, patch_stage(): pl.pallas_call(patch_kernel, name='patch_stage', out_shape=(pltpu.VMEM((P...  3.03 us
  transfers between devices with their start and end apart: 3, of which 2 were waited for; matrix products, arithmetic and copies ran while one was open for 0% of the time, Pallas kernels for 7%

profile of v5, /device:TPU:7, one launch (start us, length us, event | category | flops | bytes accessed | tf_op | source)
XLA Modules:
  0.0 89.9 jit_solution(11155055291793231192)
XLA Ops:
  0.6 3.0 %patch_stage.1 = (f32[1536,128]{1,0:T(8,128)S(1)}, f32[3,8,128]{2,1,0:T(8,128)S(1)}, bf16[128,128]{1,0:T(8,128)(2,1)S(1)}, f32[40,1024]{1,0:T(8,128)S(1)}) custom-call(f32[24,16,128]{2,1,0:T(8,128)} %rest_7_.1, f32[24,16,128]{2,1,0:T(8,128)} %rest_8_.1, f32[24,16,128]{2,1,0:T(8,128)} %t_far.1, f32[24,16,128]{2,1,0:T(8,128)} %q_far.1, f32[384,1024]{1,0:T(8,128)} %metric.1, ...), custom_call_target="tpu_custom_call" | custom-call | tf_op jit(solution)/shard_map/patch_stage/pallas_call | solution.py:268
  3.7 44.9 %all_to_all.10 = f32[64,24,128]{2,1,0:T(8,128)S(1)} all-to-all(f32[64,24,128]{2,1,0:T(8,128)S(1)} %bitcast.10), channel_id=1, replica_groups=mesh['lat'=16,'lon'=64] {'lon'}, dimensions={0} | all-to-all | bytes 1572864 | tf_op jit(solution)/shard_map/all_to_all | solution.py:723
  48.5 1.8 %band_stage.1 = (f32[1152,128]{1,0:T(8,128)S(1)}, f32[384,128]{1,0:T(8,128)S(1)}, f32[384,128]{1,0:T(8,128)S(1)}) custom-call(f32[1536,128]{1,0:T(8,128)S(1)} %bitcast.8), custom_call_target="tpu_custom_call" | custom-call | tf_op jit(solution)/shard_map/band_stage/pallas_call | solution.py:322
  50.4 7.2 %collective-permute-start = (f32[384,128]{1,0:T(8,128)S(1)}, f32[384,128]{1,0:T(8,128)S(1)}, u32[]{:S(2)}, u32[]{:S(2)}) collective-permute-start(f32[384,128]{1,0:T(8,128)S(1)} %get-tuple-element.27.north), channel_id=1, source_target_pairs={{0,64},{64,128},{128,192},{192,256},{256,320},{320,384},{384,448},... | collective-permute-start | bytes 589832 | tf_op jit(solution)/shard_map/ppermute | solution.py:763
  57.5 1.9 %collective-permute-start.1 = (f32[384,128]{1,0:T(8,128)S(1)}, f32[384,128]{1,0:T(8,128)S(1)}, u32[]{:S(2)}, u32[]{:S(2)}) collective-permute-start(f32[384,128]{1,0:T(8,128)S(1)} %get-tuple-element.26.south), channel_id=1, source_target_pairs={{64,0},{128,64},{192,128},{256,192},{320,256},{384,320},{448,384},... | collective-permute-start | bytes 589832 | tf_op jit(solution)/shard_map/ppermute | solution.py:764
  59.5 0.9 damping_stage.1
  60.3 0.0 collective-permute-done.from_south
  60.3 5.4 %collective-permute-done.1.from_north = f32[384,128]{1,0:T(8,128)S(1)} collective-permute-done((f32[384,128]{1,0:T(8,128)S(1)}, f32[384,128]{1,0:T(8,128)S(1)}, u32[]{:S(2)}, u32[]{:S(2)}) %collective-permute-start.1) | collective-permute-done | bytes 196640 | tf_op jit(solution)/shard_map/ppermute | solution.py:764
  65.7 4.2 %host_stage.1 = (f32[512,128]{1,0:T(8,128)}, f32[2,24,1024]{2,1,0:T(8,128)S(1)}) custom-call(f32[1152,128]{1,0:T(8,128)S(1)} %get-tuple-element.24.band, f32[96,128]{1,0:T(8,128)S(1)} %get-tuple-element.28.rims, f32[384,128]{1,0:T(8,128)S(1)} %collective-permute-done.from_south, f32[384,128]{1,0:T(8,128)S(1)} %collective-permute-done.1.from_north, ...), custom_call_target="tpu_custom_call" | custom-call | tf_op jit(solution)/shard_map/host_stage/pallas_call | solution.py:587
  70.0 6.3 %all-to-all-start.1 = ((f32[64,8,128]{2,1,0:T(8,128)}), f32[64,8,128]{2,1,0:T(8,128)S(1)}, u32[]{:S(2)}, u32[]{:S(2)}) async-start(f32[64,8,128]{2,1,0:T(8,128)} %bitcast.6), calls=%async_computation.1 | async-start | bytes 524288 | tf_op jit(solution)/shard_map/all_to_all | solution.py:723
  76.3 5.4 %rest_stage.1 = (f32[6,24,1024]{2,1,0:T(8,128)}, bf16[128,128]{1,0:T(8,128)(2,1)S(1)}, bf16[128,128]{1,0:T(8,128)(2,1)S(1)}, f32[24,16,128]{2,1,0:T(8,128)S(1)},...) custom-call(f32[1152,128]{1,0:T(8,128)S(1)} %get-tuple-element.24.band, f32[96,128]{1,0:T(8,128)S(1)} %get-tuple-element.28.rims, ...), custom_call_target="tpu_custom_call" | custom-call | tf_op jit(solution)/shard_map/rest_stage/pallas_call | solution.py:636
  81.7 7.1 %all-to-all-done.1 = f32[64,8,128]{2,1,0:T(8,128)S(1)} async-done(((f32[64,8,128]{2,1,0:T(8,128)}), f32[64,8,128]{2,1,0:T(8,128)S(1)}, u32[]{:S(2)}, u32[]{:S(2)}) %all-to-all-start.1) | async-done | bytes 262176 | tf_op jit(solution)/shard_map/all_to_all | solution.py:723
  88.8 1.2 %wind_stage.1 = (f32[24,16,128]{2,1,0:T(8,128)}, f32[24,16,128]{2,1,0:T(8,128)}) custom-call(f32[512,128]{1,0:T(8,128)S(1)} %bitcast.9, bf16[128,128]{1,0:T(8,128)(2,1)S(1)} %get-tuple-element.35.expand_high, bf16[128,128]{1,0:T(8,128)(2,1)S(1)} %get-tuple-element.36.expand_low, f32[384,128]{1,0:T(8,128)S(1)} %get-tuple-element.37.cell_metric, ...), custom_call_target="tpu_custom_call" | custom-call | tf_op jit(solution)/shard_map/wind_stage/pallas_call | solution.py:702
Async XLA Ops:
  50.4 10.0 %collective-permute-start = (f32[384,128]{1,0:T(8,128)S(1)}, f32[384,128]{1,0:T(8,128)S(1)}, u32[]{:S(2)}, u32[]{:S(2)}) collective-permute-start(f32[384,128]{1,0:T(8,128)S(1)} %get-tuple-element.27.north), channel_id=1, source_target_pairs={{0,64},{64,128},{128,192},{192,256},{256,320},{320,384},{384,448},... | collective-permute-start | bytes 589832 | tf_op jit(solution)/shard_map/ppermute | solution.py:763
  57.5 8.2 %collective-permute-start.1 = (f32[384,128]{1,0:T(8,128)S(1)}, f32[384,128]{1,0:T(8,128)S(1)}, u32[]{:S(2)}, u32[]{:S(2)}) collective-permute-start(f32[384,128]{1,0:T(8,128)S(1)} %get-tuple-element.26.south), channel_id=1, source_target_pairs={{64,0},{128,64},{192,128},{256,192},{320,256},{384,320},{448,384},... | collective-permute-start | bytes 589832 | tf_op jit(solution)/shard_map/ppermute | solution.py:764
  70.0 18.8 %all-to-all-start.1 = ((f32[64,8,128]{2,1,0:T(8,128)}), f32[64,8,128]{2,1,0:T(8,128)S(1)}, u32[]{:S(2)}, u32[]{:S(2)}) async-start(f32[64,8,128]{2,1,0:T(8,128)} %bitcast.6), calls=%async_computation.1 | async-start | bytes 524288 | tf_op jit(solution)/shard_map/all_to_all | solution.py:723
